TPU v7x, 32 devices: a whole 2x2x4 slice. The times are simulated.
32 devices in a mesh: lon: 8 (over y, x, core), lat: 4 (over z).
Axes of the slice: x: 2, y: 2, z: 4, core: 2. Of those that a mesh axis runs over, the one named last changes fastest.
Arguments:
- tracers: float32 [2, 8, 192, 1024], P(None, None, 'lat', 'lon'), may hold values from -6 to 6
- east_courant: float32 [8, 192, 1024], P(None, 'lat', 'lon'), may hold values from -0.25 to 0.25
- north_courant: float32 [8, 192, 1024], P(None, 'lat', 'lon'), may hold values from -0.25 to 0.25
- diffusivity: float32 [8, 192, 1024], P(None, 'lat', 'lon'), may hold values from 0.01 to 0.12
- wet_levels: int32 [192, 1024], P('lat', 'lon'), may hold values from 0 to 8
Outputs:
- advected: float32 [2, 8, 192, 1024], P(None, None, 'lat', 'lon')
All inputs are finite; a program needn't handle non-finite values.
Results may differ from a plain program's by a relative error of at most 0.0003.
Values sent between devices are 32-bit elements; how exact they have to be, the bound alone decides.
No kernel may reach another device: no remote copies, remote signals or barrier semaphores. Data moves between devices by JAX's collectives and lax.ppermute only.
A program may use at most 64 MiB of HBM per device.

v0:
```python
import jax
import jax.numpy as jnp
from jax import lax
from jax.sharding import PartitionSpec as P

STEPS = 3


def from_partner(shard, axis, stride):
    return lax.ppermute(shard, axis, [(i, i ^ 1 << stride) for i in range(lax.axis_size(axis))])


def padded(shard, sides, width, wrap):
    for axis, dim in sides:
        size, length = (lax.axis_size(axis), shard.shape[dim])
        up = [(i, (i + 1) % size) for i in range(size if wrap else size - 1)]
        down = [(j, i) for i, j in up]
        last = lax.slice_in_dim(shard, length - width, length, axis=dim)
        leading = lax.slice_in_dim(shard, 0, width, axis=dim)
        before = lax.ppermute(last, axis, up)
        after = lax.ppermute(leading, axis, down)
        shard = jnp.concatenate([before, shard, after], axis=dim)
    return shard


def minmod(first, second):
    return 0.5 * (jnp.sign(first) + jnp.sign(second)) * jnp.minimum(jnp.abs(first), jnp.abs(second))


def face_flux(behind, left_cell, right_cell, beyond, courant, face_kappa, face_mask):
    difference = right_cell - left_cell
    forward = courant > 0
    upwind = jnp.where(forward, left_cell, right_cell)
    upslope = jnp.where(forward, left_cell - behind, beyond - right_cell)
    magnitude = jnp.abs(courant)
    limited = minmod(difference, upslope)
    return (
        courant * upwind + 0.5 * magnitude * (1.0 - magnitude) * limited - face_kappa * difference
    ) * face_mask


def per_device(tracers, east_courant, north_courant, diffusivity, wet_levels):
    level_count = east_courant.shape[0]
    row_count = tracers.shape[2]
    col_count = tracers.shape[3]
    at_top = lax.axis_index("lat") == lax.axis_size("lat") - 1

    def mirror(edge_rows):
        moving = edge_rows
        for bit_number in range(lax.axis_size("lon").bit_length() - 1):
            moving = from_partner(moving, "lon", bit_number)
        result = moving[:, :, ::-1]
        return result

    def rims(field, skipped):
        zonal = padded(field, (("lon", 2),), 2, True)
        meridional = padded(field, (("lat", 1),), 2, False)
        folded = mirror(field[skipped:, ::-1][:, :2])
        if skipped > 0:
            folded = jnp.concatenate([jnp.zeros((skipped, 2, col_count), jnp.float32), folded], 0)
        northern = jnp.where(at_top, folded, meridional[:, row_count + 2 :])
        return (zonal, jnp.concatenate([meridional[:, : row_count + 2], northern], 1))

    statics = jnp.concatenate(
        [east_courant, north_courant, diffusivity, wet_levels.astype(jnp.float32)[None]], 0
    )
    static_zonal, static_merid = rims(statics, level_count)
    layers = jnp.arange(level_count, dtype=jnp.float32)[:, None, None]
    wet_zonal = (layers < static_zonal[3 * level_count][None]).astype(jnp.float32)
    east_speed = static_zonal[0:level_count, :, 1 : col_count + 2]
    kappa_zonal = static_zonal[2 * level_count : 3 * level_count]
    east_kappa = 0.5 * (kappa_zonal[:, :, 1 : col_count + 2] + kappa_zonal[:, :, 2 : col_count + 3])
    east_mask = wet_zonal[:, :, 1 : col_count + 2] * wet_zonal[:, :, 2 : col_count + 3]
    speed_rows = static_merid[level_count : 2 * level_count]
    fold_speed = 0.5 * (speed_rows[:, row_count + 1] - speed_rows[:, row_count + 2])
    last_speed = jnp.where(at_top, fold_speed, speed_rows[:, row_count + 1])
    north_speed = jnp.concatenate([speed_rows[:, 1 : row_count + 1], last_speed[:, None]], 1)
    kappa_merid = static_merid[2 * level_count : 3 * level_count]
    north_kappa = 0.5 * (kappa_merid[:, 1 : row_count + 2] + kappa_merid[:, 2 : row_count + 3])
    wet_merid = (layers < static_merid[3 * level_count][None]).astype(jnp.float32)
    north_mask = wet_merid[:, 1 : row_count + 2] * wet_merid[:, 2 : row_count + 3]
    current = tracers
    for repeat in range(STEPS):
        zonal, meridional = rims(current.reshape(2 * level_count, row_count, col_count), 0)
        zonal = zonal.reshape(2, level_count, row_count, col_count + 4)
        meridional = meridional.reshape(2, level_count, row_count + 4, col_count)
        east_flux = face_flux(
            zonal[:, :, :, 0 : col_count + 1],
            zonal[:, :, :, 1 : col_count + 2],
            zonal[:, :, :, 2 : col_count + 3],
            zonal[:, :, :, 3 : col_count + 4],
            east_speed,
            east_kappa,
            east_mask,
        )
        north_flux = face_flux(
            meridional[:, :, 0 : row_count + 1],
            meridional[:, :, 1 : row_count + 2],
            meridional[:, :, 2 : row_count + 3],
            meridional[:, :, 3 : row_count + 4],
            north_speed,
            north_kappa,
            north_mask,
        )
        current = (
            current
            - (east_flux[:, :, :, 1:] - east_flux[:, :, :, :-1])
            - (north_flux[:, :, 1:] - north_flux[:, :, :-1])
        )
    return current


def solution(mesh):
    placed = (
        P(None, None, "lat", "lon"),
        P(None, "lat", "lon"),
        P(None, "lat", "lon"),
        P(None, "lat", "lon"),
        P("lat", "lon"),
    )
    return jax.shard_map(
        per_device,
        mesh=mesh,
        in_specs=placed,
        out_specs=P(None, None, "lat", "lon"),
        check_vma=False,
    )
```

profile of v0, /device:TPU:1, one launch (start us, length us, event | category | flops | bytes accessed | tf_op | source)
XLA Modules:
  0.0 81.4 jit_solution(3180785442569148166)
XLA Ops:
  0.0 0.8 convert_bitcast_fusion
  0.8 0.8 %pad_maximum_fusion.43 = f32[17,2,128]{2,1,0:T(2,128)S(1)} fusion(f32[1,48,128]{2,1,0:T(8,128)S(1)} %convert_bitcast_fusion, f32[8,48,128]{2,1,0:T(8,128)} %param.8, f32[8,48,128]{2,1,0:T(8,128)} %param.7), kind=kLoop, calls=%fused_computation.114 | loop fusion | flops 8704 | bytes 435200 | tf_op jit(solution)/shard_map/concatenate | solution.py:64
  1.7 0.1 collective-permute-start.5
  1.8 1.5 %fusion.41 = (f32[16,2,128]{2,1,0:T(2,128)}, f32[16,2,128]{2,1,0:T(2,128)S(1)}) fusion(f32[16,48,128]{2,1,0:T(8,128)} %bitcast.34), kind=kLoop, calls=%fused_computation.128 | loop fusion | bytes 65536 | tf_op jit(solution)/shard_map/slice | solution.py:19
  3.2 5.3 %collective-permute-start.9 = (f32[16,2,128]{2,1,0:T(2,128)S(1)}, f32[16,2,128]{2,1,0:T(2,128)}, u32[]{:S(2)}, u32[]{:S(2)}) collective-permute-start(f32[16,2,128]{2,1,0:T(2,128)S(1)} %get-tuple-element.24), channel_id=1, source_target_pairs={{0,1},{1,2},{2,3},{4,5},{5,6},{6,7},{8,9},{9,10},{10,11},{12,13},{... | collective-permute-start | bytes 49160 | tf_op jit(solution)/shard_map/ppermute | solution.py:20
  8.6 0.4 collective-permute-start.10
  9.0 0.2 fusion.35
  9.2 0.3 copy.27
  9.5 1.4 %collective-permute-start = (f32[25,48,2]{1,0,2:T(8,128)S(1)}, f32[25,48,2]{1,0,2:T(8,128)S(1)}, u32[]{:S(2)}, u32[]{:S(2)}) collective-permute-start(f32[25,48,2]{1,0,2:T(8,128)S(1)} %copy.27), channel_id=1, source_target_pairs={{0,4},{4,8},{8,12},{12,16},{16,20},{20,24},{24,28},{28,0},{1,5},{5... | collective-permute-start | bytes 28808 | tf_op jit(solution)/shard_map/ppermute | solution.py:20
  10.9 0.3 copy.29
  11.2 1.0 %fusion.40 = (f32[16,48,2]{2,1,0:T(8,128)}, f32[16,48,2]{2,1,0:T(8,128)}) fusion(f32[16,48,128]{2,1,0:T(8,128)S(1)} %bitcast.35), kind=kLoop, calls=%fused_computation.127 | loop fusion | bytes 24576 | tf_op jit(solution)/shard_map/slice | solution.py:18
  12.3 1.9 %collective-permute-start.1 = (f32[16,48,2]{2,1,0:T(8,128)}, f32[16,48,2]{2,1,0:T(8,128)}, u32[]{:S(2)}, u32[]{:S(2)}) collective-permute-start(f32[16,48,2]{2,1,0:T(8,128)} %get-tuple-element.21), channel_id=1, source_target_pairs={{0,4},{4,8},{8,12},{12,16},{16,20},{20,24},{24,28},{28,0},{1,5},{5... | collective-permute-start | bytes 18440 | tf_op jit(solution)/shard_map/ppermute | solution.py:20
  14.2 0.3 copy.28
  14.5 0.2 broadcast_compare_fusion
  14.8 0.3 copy.30
  15.1 0.1 fusion.31
  15.2 0.7 copy-done.4
  16.0 0.3 slice_multiply_fusion
  16.3 2.2 %collective-permute-start.11 = (f32[16,2,128]{2,1,0:T(2,128)}, f32[16,2,128]{2,1,0:T(2,128)S(1)}, u32[]{:S(2)}, u32[]{:S(2)}) collective-permute-start(f32[16,2,128]{2,1,0:T(2,128)} %collective-permute-done.10), channel_id=1, source_target_pairs={{0,8},{4,12},{8,0},{12,4},{16,24},{20,28},{24,16},{28,20},{1,9},{5... | collective-permute-start | bytes 49160 | tf_op jit(solution)/shard_map/ppermute | solution.py:10
  18.5 0.2 fusion.25
  18.7 1.5 %collective-permute-done.1 = f32[16,48,2]{2,1,0:T(8,128)} collective-permute-done((f32[16,48,2]{2,1,0:T(8,128)}, f32[16,48,2]{2,1,0:T(8,128)}, u32[]{:S(2)}, u32[]{:S(2)}) %collective-permute-start.1) | collective-permute-done | bytes 6176 | tf_op jit(solution)/shard_map/ppermute | solution.py:20
  20.3 1.3 %collective-permute-start.8 = (f32[25,2,128]{2,1,0:T(2,128)S(1)}, f32[25,2,128]{2,1,0:T(2,128)S(1)}, u32[]{:S(2)}, u32[]{:S(2)}) collective-permute-start(f32[25,2,128]{2,1,0:T(2,128)S(1)} %get-tuple-element.12), channel_id=1, source_target_pairs={{1,0},{2,1},{3,2},{5,4},{6,5},{7,6},{9,8},{10,9},{11,10},{13,12},{... | collective-permute-start | bytes 76808 | tf_op jit(solution)/shard_map/ppermute | solution.py:21
  21.5 4.6 %collective-permute-done.2 = f32[16,48,2]{2,1,0:T(8,128)} collective-permute-done((f32[16,48,2]{2,1,0:T(8,128)}, f32[16,48,2]{2,1,0:T(8,128)}, u32[]{:S(2)}, u32[]{:S(2)}) %collective-permute-start.2) | collective-permute-done | bytes 6176 | tf_op jit(solution)/shard_map/ppermute | solution.py:21
  26.2 1.3 %collective-permute-start.13 = (f32[16,2,128]{2,1,0:T(2,128)S(1)}, f32[16,2,128]{2,1,0:T(2,128)S(1)}, u32[]{:S(2)}, u32[]{:S(2)}) collective-permute-start(f32[16,2,128]{2,1,0:T(2,128)S(1)} %copy-done.13), channel_id=1, source_target_pairs={{1,0},{2,1},{3,2},{5,4},{6,5},{7,6},{9,8},{10,9},{11,10},{13,12},{... | collective-permute-start | bytes 49160 | tf_op jit(solution)/shard_map/ppermute | solution.py:21
  27.5 0.4 collective-permute-start.6
  27.9 0.3 collective-permute-start.12
  28.2 3.3 %subtract_multiply_fusion.2 = f32[2,8,48,129]{3,2,1,0:T(8,128)} fusion(f32[2,8,48,2]{3,2,1,0:T(8,128)} %bitcast.3, f32[2,8,48,128]{3,2,1,0:T(8,128)S(1)} %copy-done.3, f32[2,8,48,2]{3,2,1,0:T(8,128)} %bitcast.2, f32[8,48,129]{2,1,0:T(8,128)S(1)} %slice_multiply_fusion, f32[8,48,129]{2,1,0:T(8,128)S(1)} %fusion.25, ...), kind=kLoop, calls=%fused_computation.23 | loop fusion | flops 2278656 | bytes 1643904 | tf_op jit(solution)/shard_map/mul | solution.py:37
  31.5 4.2 %collective-permute-start.4 = (f32[25,2,128]{2,1,0:T(2,128)S(1)}, f32[25,2,128]{2,1,0:T(2,128)S(1)}, u32[]{:S(2)}, u32[]{:S(2)}) collective-permute-start(f32[25,2,128]{2,1,0:T(2,128)S(1)} %get-tuple-element.11), channel_id=1, source_target_pairs={{0,1},{1,2},{2,3},{4,5},{5,6},{6,7},{8,9},{9,10},{10,11},{12,13},{... | collective-permute-start | bytes 76808 | tf_op jit(solution)/shard_map/ppermute | solution.py:20
  35.7 1.5 %collective-permute-start.7 = (f32[17,2,128]{2,1,0:T(2,128)S(1)}, f32[17,2,128]{2,1,0:T(2,128)S(1)}, u32[]{:S(2)}, u32[]{:S(2)}) collective-permute-start(f32[17,2,128]{2,1,0:T(2,128)S(1)} %collective-permute-done.6), channel_id=1, source_target_pairs={{0,16},{4,20},{8,24},{12,28},{16,0},{20,4},{24,8},{28,12},{1,17},{... | collective-permute-start | bytes 52232 | tf_op jit(solution)/shard_map/ppermute | solution.py:10
  37.2 0.1 rev.17
  37.4 1.0 %collective-permute-done.7 = f32[17,2,128]{2,1,0:T(2,128)S(1)} collective-permute-done((f32[17,2,128]{2,1,0:T(2,128)S(1)}, f32[17,2,128]{2,1,0:T(2,128)S(1)}, u32[]{:S(2)}, u32[]{:S(2)}) %collective-permute-start.7) | collective-permute-done | bytes 17440 | tf_op jit(solution)/shard_map/ppermute | solution.py:10
  38.4 0.1 rev.16
  38.8 0.6 copy-done.6
  39.4 1.4 %subtract_multiply_fusion.5 = f32[2,8,49,128]{3,2,1,0:T(8,128)S(1)} fusion(f32[2,8,2,128]{3,2,1,0:T(2,128)S(1)} %bitcast.40, f32[2,8,48,128]{3,2,1,0:T(8,128)S(1)} %copy-done.3, f32[2,8,2,128]{3,2,1,0:T(2,128)} %bitcast.5, f32[8,49,128]{2,1,0:T(8,128)S(1)} %get-tuple-element.25, f32[8,49,128]{2,1,0:T(8,128)S(1)} %get-tuple-element.26, ...), kind=kLoop, calls=%fused_computation.48 | loop fusion | flops 2308096 | bytes 1680384 | tf_op jit(solution)/shard_map/mul | solution.py:37
  40.8 0.2 fusion.22
  41.0 4.4 %collective-permute-start.17 = (f32[16,2,128]{2,1,0:T(2,128)S(1)}, f32[16,2,128]{2,1,0:T(2,128)S(1)}, u32[]{:S(2)}, u32[]{:S(2)}) collective-permute-start(f32[16,2,128]{2,1,0:T(2,128)S(1)} %slice.309), channel_id=1, source_target_pairs={{0,4},{4,0},{8,12},{12,8},{16,20},{20,16},{24,28},{28,24},{1,5},{5... | collective-permute-start | bytes 49160 | tf_op jit(solution)/shard_map/ppermute | solution.py:10
  45.5 0.8 %collective-permute-done.17 = f32[16,2,128]{2,1,0:T(2,128)S(1)} collective-permute-done((f32[16,2,128]{2,1,0:T(2,128)S(1)}, f32[16,2,128]{2,1,0:T(2,128)S(1)}, u32[]{:S(2)}, u32[]{:S(2)}) %collective-permute-start.17) | collective-permute-done | bytes 16416 | tf_op jit(solution)/shard_map/ppermute | solution.py:10
  46.3 1.7 %collective-permute-start.18 = (f32[16,2,128]{2,1,0:T(2,128)S(1)}, f32[16,2,128]{2,1,0:T(2,128)S(1)}, u32[]{:S(2)}, u32[]{:S(2)}) collective-permute-start(f32[16,2,128]{2,1,0:T(2,128)S(1)} %collective-permute-done.17), channel_id=1, source_target_pairs={{0,8},{4,12},{8,0},{12,4},{16,24},{20,28},{24,16},{28,20},{1,9},{5... | collective-permute-start | bytes 49160 | tf_op jit(solution)/shard_map/ppermute | solution.py:10
  48.0 0.2 fusion.38
  48.2 0.7 collective-permute-start.15
  48.8 1.1 %collective-permute-start.14 = (f32[16,48,2]{2,1,0:T(8,128)S(1)}, f32[16,48,2]{2,1,0:T(8,128)S(1)}, u32[]{:S(2)}, u32[]{:S(2)}) collective-permute-start(f32[16,48,2]{2,1,0:T(8,128)S(1)} %get-tuple-element.17), channel_id=1, source_target_pairs={{0,4},{4,8},{8,12},{12,16},{16,20},{20,24},{24,28},{28,0},{1,5},{5... | collective-permute-start | bytes 18440 | tf_op jit(solution)/shard_map/ppermute | solution.py:20
  50.0 3.6 %collective-permute-start.16 = (f32[16,2,128]{2,1,0:T(2,128)S(1)}, f32[16,2,128]{2,1,0:T(2,128)S(1)}, u32[]{:S(2)}, u32[]{:S(2)}) collective-permute-start(f32[16,2,128]{2,1,0:T(2,128)S(1)} %get-tuple-element.20), channel_id=1, source_target_pairs={{0,1},{1,2},{2,3},{4,5},{5,6},{6,7},{8,9},{9,10},{10,11},{12,13},{... | collective-permute-start | bytes 49160 | tf_op jit(solution)/shard_map/ppermute | solution.py:20
  53.6 1.3 %collective-permute-start.20 = (f32[16,2,128]{2,1,0:T(2,128)S(1)}, f32[16,2,128]{2,1,0:T(2,128)S(1)}, u32[]{:S(2)}, u32[]{:S(2)}) collective-permute-start(f32[16,2,128]{2,1,0:T(2,128)S(1)} %get-tuple-element.19), channel_id=1, source_target_pairs={{1,0},{2,1},{3,2},{5,4},{6,5},{7,6},{9,8},{10,9},{11,10},{13,12},{... | collective-permute-start | bytes 49160 | tf_op jit(solution)/shard_map/ppermute | solution.py:21
  55.0 4.3 %collective-permute-done.15 = f32[16,48,2]{2,1,0:T(8,128)S(1)} collective-permute-done((f32[16,48,2]{2,1,0:T(8,128)S(1)}, f32[16,48,2]{2,1,0:T(8,128)S(1)}, u32[]{:S(2)}, u32[]{:S(2)}) %collective-permute-start.15) | collective-permute-done | bytes 6176 | tf_op jit(solution)/shard_map/ppermute | solution.py:21
  59.3 2.0 %subtract_multiply_fusion.1 = f32[2,8,48,129]{3,2,1,0:T(8,128)} fusion(f32[2,8,48,2]{3,2,1,0:T(8,128)S(1)} %bitcast.38, f32[2,8,48,128]{3,2,1,0:T(8,128)S(1)} %fusion.22, f32[2,8,48,2]{3,2,1,0:T(8,128)S(1)} %bitcast.39, f32[8,48,129]{2,1,0:T(8,128)S(1)} %slice_multiply_fusion, f32[8,48,129]{2,1,0:T(8,128)S(1)} %fusion.25, ...), kind=kLoop, calls=%fused_computation.22 | loop fusion | flops 2278656 | bytes 1643904 | tf_op jit(solution)/shard_map/mul | solution.py:37
  61.3 0.1 rev.18
  61.5 0.6 subtract_multiply_fusion.4
  62.1 0.5 copy-done.12
  62.6 0.2 fusion.20
  62.9 0.6 collective-permute-start.24
  63.5 0.8 %collective-permute-done.24 = f32[16,2,128]{2,1,0:T(2,128)S(1)} collective-permute-done((f32[16,2,128]{2,1,0:T(2,128)S(1)}, f32[16,2,128]{2,1,0:T(2,128)S(1)}, u32[]{:S(2)}, u32[]{:S(2)}) %collective-permute-start.24) | collective-permute-done | bytes 16416 | tf_op jit(solution)/shard_map/ppermute | solution.py:10
  64.3 0.7 collective-permute-start.25
  65.1 0.2 fusion.36
  65.2 1.3 %collective-permute-start.21 = (f32[16,48,2]{2,1,0:T(8,128)S(1)}, f32[16,48,2]{2,1,0:T(8,128)S(1)}, u32[]{:S(2)}, u32[]{:S(2)}) collective-permute-start(f32[16,48,2]{2,1,0:T(8,128)S(1)} %get-tuple-element.13), channel_id=1, source_target_pairs={{0,4},{4,8},{8,12},{12,16},{16,20},{20,24},{24,28},{28,0},{1,5},{5... | collective-permute-start | bytes 18440 | tf_op jit(solution)/shard_map/ppermute | solution.py:20
  66.5 3.6 %collective-permute-start.23 = (f32[16,2,128]{2,1,0:T(2,128)S(1)}, f32[16,2,128]{2,1,0:T(2,128)S(1)}, u32[]{:S(2)}, u32[]{:S(2)}) collective-permute-start(f32[16,2,128]{2,1,0:T(2,128)S(1)} %get-tuple-element.16), channel_id=1, source_target_pairs={{0,1},{1,2},{2,3},{4,5},{5,6},{6,7},{8,9},{9,10},{10,11},{12,13},{... | collective-permute-start | bytes 49160 | tf_op jit(solution)/shard_map/ppermute | solution.py:20
  70.2 1.3 %collective-permute-start.27 = (f32[16,2,128]{2,1,0:T(2,128)S(1)}, f32[16,2,128]{2,1,0:T(2,128)S(1)}, u32[]{:S(2)}, u32[]{:S(2)}) collective-permute-start(f32[16,2,128]{2,1,0:T(2,128)S(1)} %get-tuple-element.15), channel_id=1, source_target_pairs={{1,0},{2,1},{3,2},{5,4},{6,5},{7,6},{9,8},{10,9},{11,10},{13,12},{... | collective-permute-start | bytes 49160 | tf_op jit(solution)/shard_map/ppermute | solution.py:21
  71.5 1.7 %collective-permute-start.26 = (f32[16,2,128]{2,1,0:T(2,128)S(1)}, f32[16,2,128]{2,1,0:T(2,128)S(1)}, u32[]{:S(2)}, u32[]{:S(2)}) collective-permute-start(f32[16,2,128]{2,1,0:T(2,128)S(1)} %collective-permute-done.25), channel_id=1, source_target_pairs={{0,16},{4,20},{8,24},{12,28},{16,0},{20,4},{24,8},{28,12},{1,17},{... | collective-permute-start | bytes 49160 | tf_op jit(solution)/shard_map/ppermute | solution.py:10
  73.2 0.1 collective-permute-done.21
  73.3 3.9 %collective-permute-done.22 = f32[16,48,2]{2,1,0:T(8,128)S(1)} collective-permute-done((f32[16,48,2]{2,1,0:T(8,128)S(1)}, f32[16,48,2]{2,1,0:T(8,128)S(1)}, u32[]{:S(2)}, u32[]{:S(2)}) %collective-permute-start.22) | collective-permute-done | bytes 6176 | tf_op jit(solution)/shard_map/ppermute | solution.py:21
  77.2 2.0 %subtract_multiply_fusion = f32[2,8,48,129]{3,2,1,0:T(8,128)} fusion(f32[2,8,48,2]{3,2,1,0:T(8,128)S(1)} %bitcast.37, f32[2,8,48,128]{3,2,1,0:T(8,128)S(1)} %fusion.20, f32[2,8,48,2]{3,2,1,0:T(8,128)S(1)} %bitcast.36, f32[8,48,129]{2,1,0:T(8,128)S(1)} %slice_multiply_fusion, f32[8,48,129]{2,1,0:T(8,128)S(1)} %fusion.25, ...), kind=kLoop, calls=%fused_computation.21 | loop fusion | flops 2278656 | bytes 1643904 | tf_op jit(solution)/shard_map/mul | solution.py:37
  79.2 0.1 rev.19
  79.3 0.6 subtract_multiply_fusion.3
  79.9 0.5 copy-done.11
  80.5 0.9 %fusion.18 = f32[2,8,48,128]{3,2,1,0:T(8,128)} fusion(f32[2,8,49,128]{3,2,1,0:T(8,128)S(1)} %subtract_multiply_fusion.3, f32[2,8,48,128]{3,2,1,0:T(8,128)S(1)} %fusion.20, f32[2,8,48,129]{3,2,1,0:T(8,128)S(1)} %copy-done.11), kind=kLoop, calls=%fused_computation.50 | loop fusion | flops 393216 | bytes 2359296 | tf_op jit(solution)/shard_map/sub | solution.py:106
  (68 shorter events, 0.9 us)
Async XLA Ops:
  0.0 8.9 %copy-start.2 = (f32[8,48,128]{2,1,0:T(8,128)S(1)}, f32[8,48,128]{2,1,0:T(8,128)}, u32[]{:S(2)}) copy-start(f32[8,48,128]{2,1,0:T(8,128)} %param.6) | copy-start | bytes 589828
  0.8 8.1 %copy-start = (f32[8,48,128]{2,1,0:T(8,128)S(1)}, f32[8,48,128]{2,1,0:T(8,128)}, u32[]{:S(2)}) copy-start(f32[8,48,128]{2,1,0:T(8,128)} %param.7) | copy-start | bytes 589828
  0.8 8.1 %copy-start.1 = (f32[8,48,128]{2,1,0:T(8,128)S(1)}, f32[8,48,128]{2,1,0:T(8,128)}, u32[]{:S(2)}) copy-start(f32[8,48,128]{2,1,0:T(8,128)} %param.8) | copy-start | bytes 589828
  1.7 25.8 %collective-permute-start.5 = (f32[17,2,128]{2,1,0:T(2,128)S(1)}, f32[17,2,128]{2,1,0:T(2,128)}, u32[]{:S(2)}, u32[]{:S(2)}) collective-permute-start(f32[17,2,128]{2,1,0:T(2,128)S(1)} %slice.282), channel_id=1, source_target_pairs={{0,4},{4,0},{8,12},{12,8},{16,20},{20,16},{24,28},{28,24},{1,5},{5... | collective-permute-start | bytes 52232 | tf_op jit(solution)/shard_map/ppermute | solution.py:10
  3.2 35.6 %collective-permute-start.9 = (f32[16,2,128]{2,1,0:T(2,128)S(1)}, f32[16,2,128]{2,1,0:T(2,128)}, u32[]{:S(2)}, u32[]{:S(2)}) collective-permute-start(f32[16,2,128]{2,1,0:T(2,128)S(1)} %get-tuple-element.24), channel_id=1, source_target_pairs={{0,1},{1,2},{2,3},{4,5},{5,6},{6,7},{8,9},{9,10},{10,11},{12,13},{... | collective-permute-start | bytes 49160 | tf_op jit(solution)/shard_map/ppermute | solution.py:20
  8.6 7.8 %collective-permute-start.10 = (f32[16,2,128]{2,1,0:T(2,128)S(1)}, f32[16,2,128]{2,1,0:T(2,128)}, u32[]{:S(2)}, u32[]{:S(2)}) collective-permute-start(f32[16,2,128]{2,1,0:T(2,128)S(1)} %slice.287), channel_id=1, source_target_pairs={{0,4},{4,0},{8,12},{12,8},{16,20},{20,16},{24,28},{28,24},{1,5},{5... | collective-permute-start | bytes 49160 | tf_op jit(solution)/shard_map/ppermute | solution.py:10
  9.5 1.7 %copy-start.3 = (f32[2,8,48,128]{3,2,1,0:T(8,128)S(1)}, f32[2,8,48,128]{3,2,1,0:T(8,128)}, u32[]{:S(2)}) copy-start(f32[2,8,48,128]{3,2,1,0:T(8,128)} %param.5) | copy-start | bytes 1179652
  9.5 2.8 %collective-permute-start = (f32[25,48,2]{1,0,2:T(8,128)S(1)}, f32[25,48,2]{1,0,2:T(8,128)S(1)}, u32[]{:S(2)}, u32[]{:S(2)}) collective-permute-start(f32[25,48,2]{1,0,2:T(8,128)S(1)} %copy.27), channel_id=1, source_target_pairs={{0,4},{4,8},{8,12},{12,16},{16,20},{20,24},{24,28},{28,0},{1,5},{5... | collective-permute-start | bytes 28808 | tf_op jit(solution)/shard_map/ppermute | solution.py:20
  11.2 3.6 %collective-permute-start.3 = (f32[25,48,2]{1,0,2:T(8,128)S(1)}, f32[25,48,2]{1,0,2:T(8,128)S(1)}, u32[]{:S(2)}, u32[]{:S(2)}) collective-permute-start(f32[25,48,2]{1,0,2:T(8,128)S(1)} %copy.29), channel_id=1, source_target_pairs={{4,0},{8,4},{12,8},{16,12},{20,16},{24,20},{28,24},{0,28},{5,1},{9... | collective-permute-start | bytes 28808 | tf_op jit(solution)/shard_map/ppermute | solution.py:21
  12.3 8.0 %collective-permute-start.1 = (f32[16,48,2]{2,1,0:T(8,128)}, f32[16,48,2]{2,1,0:T(8,128)}, u32[]{:S(2)}, u32[]{:S(2)}) collective-permute-start(f32[16,48,2]{2,1,0:T(8,128)} %get-tuple-element.21), channel_id=1, source_target_pairs={{0,4},{4,8},{8,12},{12,16},{16,20},{20,24},{24,28},{28,0},{1,5},{5... | collective-permute-start | bytes 18440 | tf_op jit(solution)/shard_map/ppermute | solution.py:20
  14.7 11.5 %collective-permute-start.2 = (f32[16,48,2]{2,1,0:T(8,128)}, f32[16,48,2]{2,1,0:T(8,128)}, u32[]{:S(2)}, u32[]{:S(2)}) collective-permute-start(f32[16,48,2]{2,1,0:T(8,128)} %get-tuple-element.22), channel_id=1, source_target_pairs={{4,0},{8,4},{12,8},{16,12},{20,16},{24,20},{28,24},{0,28},{5,1},{9... | collective-permute-start | bytes 18440 | tf_op jit(solution)/shard_map/ppermute | solution.py:21
  15.1 0.8 %copy-start.4 = (f32[25,48,2]{2,1,0:T(8,128)}, f32[25,48,2]{2,1,0:T(8,128)S(1)}, u32[]{:S(2)}) copy-start(f32[25,48,2]{2,1,0:T(8,128)S(1)} %copy.30) | copy-start | bytes 28804
  16.2 2.3 %copy-start.5 = (f32[25,48,2]{2,1,0:T(8,128)S(1)}, f32[25,48,2]{2,1,0:T(8,128)}, u32[]{:S(2)}) copy-start(f32[25,48,2]{2,1,0:T(8,128)} %copy-done.4) | copy-start | bytes 28804
  16.3 9.9 %copy-start.13 = (f32[16,2,128]{2,1,0:T(2,128)S(1)}, f32[16,2,128]{2,1,0:T(2,128)}, u32[]{:S(2)}) copy-start(f32[16,2,128]{2,1,0:T(2,128)} %get-tuple-element.23) | copy-start | bytes 49156
  16.3 11.6 %collective-permute-start.11 = (f32[16,2,128]{2,1,0:T(2,128)}, f32[16,2,128]{2,1,0:T(2,128)S(1)}, u32[]{:S(2)}, u32[]{:S(2)}) collective-permute-start(f32[16,2,128]{2,1,0:T(2,128)} %collective-permute-done.10), channel_id=1, source_target_pairs={{0,8},{4,12},{8,0},{12,4},{16,24},{20,28},{24,16},{28,20},{1,9},{5... | collective-permute-start | bytes 49160 | tf_op jit(solution)/shard_map/ppermute | solution.py:10
  20.3 18.2 %collective-permute-start.8 = (f32[25,2,128]{2,1,0:T(2,128)S(1)}, f32[25,2,128]{2,1,0:T(2,128)S(1)}, u32[]{:S(2)}, u32[]{:S(2)}) collective-permute-start(f32[25,2,128]{2,1,0:T(2,128)S(1)} %get-tuple-element.12), channel_id=1, source_target_pairs={{1,0},{2,1},{3,2},{5,4},{6,5},{7,6},{9,8},{10,9},{11,10},{13,12},{... | collective-permute-start | bytes 76808 | tf_op jit(solution)/shard_map/ppermute | solution.py:21
  26.2 11.1 %collective-permute-start.13 = (f32[16,2,128]{2,1,0:T(2,128)S(1)}, f32[16,2,128]{2,1,0:T(2,128)S(1)}, u32[]{:S(2)}, u32[]{:S(2)}) collective-permute-start(f32[16,2,128]{2,1,0:T(2,128)S(1)} %copy-done.13), channel_id=1, source_target_pairs={{1,0},{2,1},{3,2},{5,4},{6,5},{7,6},{9,8},{10,9},{11,10},{13,12},{... | collective-permute-start | bytes 49160 | tf_op jit(solution)/shard_map/ppermute | solution.py:21
  27.5 4.0 %collective-permute-start.6 = (f32[17,2,128]{2,1,0:T(2,128)}, f32[17,2,128]{2,1,0:T(2,128)S(1)}, u32[]{:S(2)}, u32[]{:S(2)}) collective-permute-start(f32[17,2,128]{2,1,0:T(2,128)} %collective-permute-done.5), channel_id=1, source_target_pairs={{0,8},{4,12},{8,0},{12,4},{16,24},{20,28},{24,16},{28,20},{1,9},{5... | collective-permute-start | bytes 52232 | tf_op jit(solution)/shard_map/ppermute | solution.py:10
  27.9 7.8 %collective-permute-start.12 = (f32[16,2,128]{2,1,0:T(2,128)S(1)}, f32[16,2,128]{2,1,0:T(2,128)S(1)}, u32[]{:S(2)}, u32[]{:S(2)}) collective-permute-start(f32[16,2,128]{2,1,0:T(2,128)S(1)} %collective-permute-done.11), channel_id=1, source_target_pairs={{0,16},{4,20},{8,24},{12,28},{16,0},{20,4},{24,8},{28,12},{1,17},{... | collective-permute-start | bytes 49160 | tf_op jit(solution)/shard_map/ppermute | solution.py:10
  31.5 7.1 %collective-permute-start.4 = (f32[25,2,128]{2,1,0:T(2,128)S(1)}, f32[25,2,128]{2,1,0:T(2,128)S(1)}, u32[]{:S(2)}, u32[]{:S(2)}) collective-permute-start(f32[25,2,128]{2,1,0:T(2,128)S(1)} %get-tuple-element.11), channel_id=1, source_target_pairs={{0,1},{1,2},{2,3},{4,5},{5,6},{6,7},{8,9},{9,10},{10,11},{12,13},{... | collective-permute-start | bytes 76808 | tf_op jit(solution)/shard_map/ppermute | solution.py:20
  35.7 2.7 %collective-permute-start.7 = (f32[17,2,128]{2,1,0:T(2,128)S(1)}, f32[17,2,128]{2,1,0:T(2,128)S(1)}, u32[]{:S(2)}, u32[]{:S(2)}) collective-permute-start(f32[17,2,128]{2,1,0:T(2,128)S(1)} %collective-permute-done.6), channel_id=1, source_target_pairs={{0,16},{4,20},{8,24},{12,28},{16,0},{20,4},{24,8},{28,12},{1,17},{... | collective-permute-start | bytes 52232 | tf_op jit(solution)/shard_map/ppermute | solution.py:10
  38.7 0.7 copy-start.6
  38.8 22.7 %copy-start.8 = (f32[8,49,128]{2,1,0:T(8,128)}, f32[8,49,128]{2,1,0:T(8,128)S(1)}, u32[]{:S(2)}) copy-start(f32[8,49,128]{2,1,0:T(8,128)S(1)} %subtract_multiply_fusion.7) | copy-start | bytes 602116
  39.4 1.4 %copy-start.10 = (f32[2,8,48,129]{3,2,1,0:T(8,128)S(1)}, f32[2,8,48,129]{3,2,1,0:T(8,128)}, u32[]{:S(2)}) copy-start(f32[2,8,48,129]{3,2,1,0:T(8,128)} %subtract_multiply_fusion.2) | copy-start | bytes 1188868
  41.0 5.3 %collective-permute-start.17 = (f32[16,2,128]{2,1,0:T(2,128)S(1)}, f32[16,2,128]{2,1,0:T(2,128)S(1)}, u32[]{:S(2)}, u32[]{:S(2)}) collective-permute-start(f32[16,2,128]{2,1,0:T(2,128)S(1)} %slice.309), channel_id=1, source_target_pairs={{0,4},{4,0},{8,12},{12,8},{16,20},{20,16},{24,28},{28,24},{1,5},{5... | collective-permute-start | bytes 49160 | tf_op jit(solution)/shard_map/ppermute | solution.py:10
  46.3 8.6 %collective-permute-start.18 = (f32[16,2,128]{2,1,0:T(2,128)S(1)}, f32[16,2,128]{2,1,0:T(2,128)S(1)}, u32[]{:S(2)}, u32[]{:S(2)}) collective-permute-start(f32[16,2,128]{2,1,0:T(2,128)S(1)} %collective-permute-done.17), channel_id=1, source_target_pairs={{0,8},{4,12},{8,0},{12,4},{16,24},{20,28},{24,16},{28,20},{1,9},{5... | collective-permute-start | bytes 49160 | tf_op jit(solution)/shard_map/ppermute | solution.py:10
  48.2 11.2 %collective-permute-start.15 = (f32[16,48,2]{2,1,0:T(8,128)S(1)}, f32[16,48,2]{2,1,0:T(8,128)S(1)}, u32[]{:S(2)}, u32[]{:S(2)}) collective-permute-start(f32[16,48,2]{2,1,0:T(8,128)S(1)} %get-tuple-element.18), channel_id=1, source_target_pairs={{4,0},{8,4},{12,8},{16,12},{20,16},{24,20},{28,24},{0,28},{5,1},{9... | collective-permute-start | bytes 18440 | tf_op jit(solution)/shard_map/ppermute | solution.py:21
  48.8 10.5 %collective-permute-start.14 = (f32[16,48,2]{2,1,0:T(8,128)S(1)}, f32[16,48,2]{2,1,0:T(8,128)S(1)}, u32[]{:S(2)}, u32[]{:S(2)}) collective-permute-start(f32[16,48,2]{2,1,0:T(8,128)S(1)} %get-tuple-element.17), channel_id=1, source_target_pairs={{0,4},{4,8},{8,12},{12,16},{16,20},{20,24},{24,28},{28,0},{1,5},{5... | collective-permute-start | bytes 18440 | tf_op jit(solution)/shard_map/ppermute | solution.py:20
  50.0 11.5 %collective-permute-start.16 = (f32[16,2,128]{2,1,0:T(2,128)S(1)}, f32[16,2,128]{2,1,0:T(2,128)S(1)}, u32[]{:S(2)}, u32[]{:S(2)}) collective-permute-start(f32[16,2,128]{2,1,0:T(2,128)S(1)} %get-tuple-element.20), channel_id=1, source_target_pairs={{0,1},{1,2},{2,3},{4,5},{5,6},{6,7},{8,9},{9,10},{10,11},{12,13},{... | collective-permute-start | bytes 49160 | tf_op jit(solution)/shard_map/ppermute | solution.py:20
  53.6 7.8 %collective-permute-start.20 = (f32[16,2,128]{2,1,0:T(2,128)S(1)}, f32[16,2,128]{2,1,0:T(2,128)S(1)}, u32[]{:S(2)}, u32[]{:S(2)}) collective-permute-start(f32[16,2,128]{2,1,0:T(2,128)S(1)} %get-tuple-element.19), channel_id=1, source_target_pairs={{1,0},{2,1},{3,2},{5,4},{6,5},{7,6},{9,8},{10,9},{11,10},{13,12},{... | collective-permute-start | bytes 49160 | tf_op jit(solution)/shard_map/ppermute | solution.py:21
  54.9 6.4 %collective-permute-start.19 = (f32[16,2,128]{2,1,0:T(2,128)S(1)}, f32[16,2,128]{2,1,0:T(2,128)S(1)}, u32[]{:S(2)}, u32[]{:S(2)}) collective-permute-start(f32[16,2,128]{2,1,0:T(2,128)S(1)} %collective-permute-done.18), channel_id=1, source_target_pairs={{0,16},{4,20},{8,24},{12,28},{16,0},{20,4},{24,8},{28,12},{1,17},{... | collective-permute-start | bytes 49160 | tf_op jit(solution)/shard_map/ppermute | solution.py:10
  59.3 2.2 %copy-start.7 = (f32[8,49,128]{2,1,0:T(8,128)S(1)}, f32[8,49,128]{2,1,0:T(8,128)}, u32[]{:S(2)}) copy-start(f32[8,49,128]{2,1,0:T(8,128)} %copy-done.6) | copy-start | bytes 602116
  61.5 1.1 %copy-start.12 = (f32[2,8,48,129]{3,2,1,0:T(8,128)S(1)}, f32[2,8,48,129]{3,2,1,0:T(8,128)}, u32[]{:S(2)}) copy-start(f32[2,8,48,129]{3,2,1,0:T(8,128)} %subtract_multiply_fusion.1) | copy-start | bytes 1188868
  62.9 1.4 %collective-permute-start.24 = (f32[16,2,128]{2,1,0:T(2,128)S(1)}, f32[16,2,128]{2,1,0:T(2,128)S(1)}, u32[]{:S(2)}, u32[]{:S(2)}) collective-permute-start(f32[16,2,128]{2,1,0:T(2,128)S(1)} %slice.326), channel_id=1, source_target_pairs={{0,4},{4,0},{8,12},{12,8},{16,20},{20,16},{24,28},{28,24},{1,5},{5... | collective-permute-start | bytes 49160 | tf_op jit(solution)/shard_map/ppermute | solution.py:10
  64.3 7.2 %collective-permute-start.25 = (f32[16,2,128]{2,1,0:T(2,128)S(1)}, f32[16,2,128]{2,1,0:T(2,128)S(1)}, u32[]{:S(2)}, u32[]{:S(2)}) collective-permute-start(f32[16,2,128]{2,1,0:T(2,128)S(1)} %collective-permute-done.24), channel_id=1, source_target_pairs={{0,8},{4,12},{8,0},{12,4},{16,24},{20,28},{24,16},{28,20},{1,9},{5... | collective-permute-start | bytes 49160 | tf_op jit(solution)/shard_map/ppermute | solution.py:10
  65.2 8.1 %collective-permute-start.21 = (f32[16,48,2]{2,1,0:T(8,128)S(1)}, f32[16,48,2]{2,1,0:T(8,128)S(1)}, u32[]{:S(2)}, u32[]{:S(2)}) collective-permute-start(f32[16,48,2]{2,1,0:T(8,128)S(1)} %get-tuple-element.13), channel_id=1, source_target_pairs={{0,4},{4,8},{8,12},{12,16},{16,20},{20,24},{24,28},{28,0},{1,5},{5... | collective-permute-start | bytes 18440 | tf_op jit(solution)/shard_map/ppermute | solution.py:20
  66.5 10.6 %collective-permute-start.22 = (f32[16,48,2]{2,1,0:T(8,128)S(1)}, f32[16,48,2]{2,1,0:T(8,128)S(1)}, u32[]{:S(2)}, u32[]{:S(2)}) collective-permute-start(f32[16,48,2]{2,1,0:T(8,128)S(1)} %get-tuple-element.14), channel_id=1, source_target_pairs={{4,0},{8,4},{12,8},{16,12},{20,16},{24,20},{28,24},{0,28},{5,1},{9... | collective-permute-start | bytes 18440 | tf_op jit(solution)/shard_map/ppermute | solution.py:21
  66.5 12.8 %collective-permute-start.23 = (f32[16,2,128]{2,1,0:T(2,128)S(1)}, f32[16,2,128]{2,1,0:T(2,128)S(1)}, u32[]{:S(2)}, u32[]{:S(2)}) collective-permute-start(f32[16,2,128]{2,1,0:T(2,128)S(1)} %get-tuple-element.16), channel_id=1, source_target_pairs={{0,1},{1,2},{2,3},{4,5},{5,6},{6,7},{8,9},{9,10},{10,11},{12,13},{... | collective-permute-start | bytes 49160 | tf_op jit(solution)/shard_map/ppermute | solution.py:20
  70.2 9.1 %collective-permute-start.27 = (f32[16,2,128]{2,1,0:T(2,128)S(1)}, f32[16,2,128]{2,1,0:T(2,128)S(1)}, u32[]{:S(2)}, u32[]{:S(2)}) collective-permute-start(f32[16,2,128]{2,1,0:T(2,128)S(1)} %get-tuple-element.15), channel_id=1, source_target_pairs={{1,0},{2,1},{3,2},{5,4},{6,5},{7,6},{9,8},{10,9},{11,10},{13,12},{... | collective-permute-start | bytes 49160 | tf_op jit(solution)/shard_map/ppermute | solution.py:21
  71.5 7.7 %collective-permute-start.26 = (f32[16,2,128]{2,1,0:T(2,128)S(1)}, f32[16,2,128]{2,1,0:T(2,128)S(1)}, u32[]{:S(2)}, u32[]{:S(2)}) collective-permute-start(f32[16,2,128]{2,1,0:T(2,128)S(1)} %collective-permute-done.25), channel_id=1, source_target_pairs={{0,16},{4,20},{8,24},{12,28},{16,0},{20,4},{24,8},{28,12},{1,17},{... | collective-permute-start | bytes 49160 | tf_op jit(solution)/shard_map/ppermute | solution.py:10
  77.2 2.2 %copy-start.9 = (f32[8,49,128]{2,1,0:T(8,128)S(1)}, f32[8,49,128]{2,1,0:T(8,128)}, u32[]{:S(2)}) copy-start(f32[8,49,128]{2,1,0:T(8,128)} %copy-done.8) | copy-start | bytes 602116
  79.3 1.1 %copy-start.11 = (f32[2,8,48,129]{3,2,1,0:T(8,128)S(1)}, f32[2,8,48,129]{3,2,1,0:T(8,128)}, u32[]{:S(2)}) copy-start(f32[2,8,48,129]{3,2,1,0:T(8,128)} %subtract_multiply_fusion) | copy-start | bytes 1188868
where the time goes:
time: 82 us; the launch traced here: 81.4 us
  starting transfers between devices  42.4 us (52%)
  waiting for transfers between devices  17.2 us (21%)
  other arithmetic  14 us (17%)
  local copies, waits for them, and re-layouts  7.24 us (9%)
    ppermute x8, starting transfers between devices, padded(): before = lax.ppermute(last, axis, up)  22.4 us
    ppermute x12, starting transfers between devices, from_partner(): lax.ppermute(shard, axis, [(i, i ^ 1 << stride) for i in range(lax.axis_s...  14 us
    ppermute x8, waiting for transfers between devices, padded(): after = lax.ppermute(leading, axis, down)  12.8 us
    mul x6, other arithmetic, face_flux(): (courant * upwind + 0.5 * magnitude * (1.0 - magnitude) * limited - face_...  9.9 us
    ppermute x8, starting transfers between devices, padded(): after = lax.ppermute(leading, axis, down)  5.94 us
    ppermute x12, waiting for transfers between devices, from_partner(): lax.ppermute(shard, axis, [(i, i ^ 1 << stride) for i in range(lax.axis_s...  2.7 us
    unnamed x28, local copies, waits for them, and re-layouts  2.38 us
    slice x5, local copies, waits for them, and re-layouts, padded(): last = lax.slice_in_dim(shard, length - width, length, axis=dim)  1.87 us
  transfers between devices with their start and end apart: 28, of which 8 were waited for; matrix products, arithmetic and copies ran while one was open for 16% of the time, Pallas kernels for 0%

commit v1 on v0

v1 whole, which is shorter than its diff:
```python
import jax
import jax.numpy as jnp
from jax import lax
from jax.experimental import pallas as pl
from jax.experimental.pallas import tpu as pltpu
from jax.sharding import PartitionSpec as P

STEPS = 3
HALO = 2 * STEPS
AXES = ("lon", "lat")
GROUP = 4
PLANES = 5
SLOT = HALO
STRIP = 6 * HALO
VMEM = pl.BlockSpec(memory_space=pltpu.VMEM)

AT_T, AT_E, AT_N, AT_K, AT_WET, AT_PACK, AT_PACK_WET, MESSAGE = 0, 12, 16, 21, 26, 27, 31, 32
N_E, N_N, N_K = HALO - 2, HALO - 1, HALO - 1


def lanes(shape):
    return lax.broadcasted_iota(jnp.int32, shape, len(shape) - 1)


def levels_of(shape):
    return lax.broadcasted_iota(jnp.int32, shape, 0).astype(jnp.float32)


def take(value, index):
    return jnp.take_along_axis(value, index, axis=1)


def east_of(value):
    return pltpu.roll(value, value.shape[1] - 1, 1)


def west_of(value):
    return pltpu.roll(value, 1, 1)


def coefficients(speed, kappa, other_kappa, mask):
    speed = speed * mask
    magnitude = jnp.abs(speed)
    spread = jnp.minimum(speed, 0.0) - (0.5 * mask) * (kappa + other_kappa)
    return speed, spread, 0.5 * magnitude * (1.0 - magnitude)


def flux(cell, before, here, after, face):
    speed, spread, slope = face
    upslope = jnp.where(speed > 0, before, after)
    limited = jnp.maximum(
        jnp.minimum(here, upslope), jnp.minimum(jnp.maximum(here, upslope), 0.0)
    )
    return speed * cell + spread * here + slope * limited


def advance(low, high, cell_at, east_at, north_at, put):
    cells = {r: cell_at(r) for r in range(low - 2, low + 2)}
    slope = {r: cells[r + 1] - cells[r] for r in range(low - 2, low + 1)}
    below = flux(cells[low - 1], slope[low - 2], slope[low - 1], slope[low], north_at(low - 1))
    for r in range(low, high):
        cells[r + 2] = cell_at(r + 2)
        slope[r + 1] = cells[r + 2] - cells[r + 1]
        above = flux(cells[r], slope[r - 1], slope[r], slope[r + 1], north_at(r))
        step = east_of(cells[r]) - cells[r]
        eastern = flux(cells[r], west_of(step), step, east_of(step), east_at(r))
        put(r, cells[r] - (eastern - west_of(eastern)) - (above - below))
        below = above


def parities():
    lon_even = lax.rem(lax.axis_index("lon"), 2) == 0
    lat = lax.axis_index("lat")
    return lon_even, lax.rem(lat, 2) == 0, lat == lax.axis_size("lat") - 1


def wet_row(wet_ref, row):
    return wet_ref[pl.ds(row, 1), :].astype(jnp.float32)


def pack_kernel(tr, ec, nc, kd, wet, p0, p1, xm, ym):
    rows, cols = wet.shape
    lev = ec.shape[0] // rows
    lon_even, lat_even, _ = parities()
    lane = lanes((lev, cols))

    def plane(p, r):
        if p < 2:
            return tr[pl.ds(p * lev * rows + r, lev, stride=rows), :]
        return (ec, nc, kd)[p - 2][pl.ds(r, lev, stride=rows), :]

    def place(pair, value, slot):
        if pair is None:
            pair = (jnp.zeros_like(value), jnp.zeros_like(value))
        inside = (lane >= slot * SLOT) & (lane < slot * SLOT + SLOT)
        eastern = pltpu.roll(value, slot * SLOT + SLOT, 1)
        western = pltpu.roll(value, slot * SLOT, 1) if slot else value
        return jnp.where(inside, eastern, pair[0]), jnp.where(inside, western, pair[1])

    def emit(at, pair):
        p0[at] = jnp.where(lon_even, pair[0], pair[1])
        p1[at] = jnp.where(lon_even, pair[1], pair[0])

    for g in range(rows // GROUP):
        pair = None
        for k in range(GROUP):
            for p in range(PLANES):
                pair = place(pair, plane(p, g * GROUP + k), k * PLANES + p)
        emit(g, pair)
    pair = None
    for tile in range(rows // lev):
        pair = place(pair, wet[pl.ds(tile * lev, lev), :].astype(jnp.float32), tile)
    emit(rows // GROUP, pair)

    for out, north in ((xm, lat_even), (ym, jnp.logical_not(lat_even))):
        row = [jnp.where(north, rows - 1 - m, m) for m in range(HALO)]
        for m in range(HALO):
            for p in range(2):
                out[AT_T + 2 * m + p] = plane(p, row[m])
        for m in range(N_E):
            out[AT_E + m] = plane(2, row[m])
        for m in range(N_N):
            out[AT_N + m] = plane(3, row[m])
        for m in range(N_K):
            out[AT_K + m] = plane(4, row[m])
        out[AT_WET] = jnp.zeros((lev, cols), jnp.float32)
        for m in range(N_K):
            out[AT_WET, pl.ds(m, 1), :] = wet_row(wet, row[m])


def sides(lon_even, r0, r1, at):
    a, b = r0[at], r1[at]
    return jnp.where(lon_even, a, b), jnp.where(lon_even, b, a)


def forward_kernel(xm, ym, r0, r1, x, y):
    lev, cols = xm.shape[1:]
    groups = r0.shape[0] - 1
    tiles = groups * GROUP // lev
    lon_even, lat_even, _ = parities()
    lane = lanes((lev, cols))
    span = PLANES * SLOT
    turned = lane
    for k in range(GROUP):
        here = (lane >= k * span) & (lane < k * span + span)
        turned = jnp.where(here, lane + (GROUP - 1 - 2 * k) * span, turned)
    for part, out, north in ((xm, x, lat_even), (ym, y, jnp.logical_not(lat_even))):
        for i in range(AT_PACK):
            out[i] = part[i]
        index = jnp.where(north, turned, lane)
        for h in range(2):
            pair = sides(lon_even, r0, r1, jnp.where(north, groups - 1 - h, h))
            for s in range(2):
                out[AT_PACK + 2 * s + h] = take(pair[s], index)
        pair = sides(lon_even, r0, r1, groups)
        index = jnp.where(north, lane + (tiles - 1) * SLOT, lane)
        eastern = take(pair[0], jnp.minimum(index, cols - 1))
        western = pltpu.roll(take(pair[1], jnp.minimum(index, cols - 1)), SLOT, 1)
        out[AT_PACK_WET] = jnp.where(lane < SLOT, eastern, western)


def interior_kernel(tr, ec, nc, kd, wet, t0, t1, t2, t3, raw, face):
    rows, cols = wet.shape
    lev = ec.shape[0] // rows
    level = levels_of((lev, cols))

    def mask_at(r):
        return jnp.where(level < wet_row(wet, r), 1.0, 0.0)

    mask = mask_at(0)
    for r in range(rows):
        for p in range(2):
            t0[r, p] = tr[pl.ds(p * lev * rows + r, lev, stride=rows), :]
        for p, source in enumerate((ec, nc, kd)):
            raw[r, p] = source[pl.ds(r, lev, stride=rows), :]
        kappa = raw[r, 2]
        put_face(face, r, 0, coefficients(raw[r, 0], kappa, east_of(kappa), mask * east_of(mask)))
        if r + 1 < rows:
            higher = kd[pl.ds(r + 1, lev, stride=rows), :]
            mask_above = mask_at(r + 1)
            put_face(face, r, 3, coefficients(raw[r, 1], kappa, higher, mask * mask_above))
            mask = mask_above
    sources, results = (t0, t1, t2), (t1, t2, t3)
    for s in range(STEPS):
        for p in range(2):
            advance(
                2 * s + 2,
                rows - 2 * s - 2,
                lambda r: sources[s][r, p],
                lambda r: get_face(face, r, 0),
                lambda r: get_face(face, r, 3),
                lambda r, v: results[s].__setitem__((r, p), v),
            )


def put_face(face, r, at, values):
    for i in range(3):
        face[r, at + i] = values[i]


def get_face(face, r, at):
    return tuple(face[r, at + i] for i in range(3))


class Strip:
    def __init__(self, lev, cols):
        lane = lanes((lev, cols))
        self.half = cols // 2
        self.second = lane >= self.half
        q = jnp.where(self.second, lane - self.half, lane)
        self.base = lane - q
        self.q = q
        self.own = jnp.clip(
            jnp.where(q < 2 * HALO, q + cols - 2 * HALO, q - 4 * HALO), 0, cols - 1
        )
        self.is_east = (q >= 2 * HALO) & (q < 3 * HALO)
        self.is_west = (q >= 3 * HALO) & (q < 4 * HALO)
        self.offset = jnp.clip(jnp.where(q < 3 * HALO, q - 2 * HALO, q - 3 * HALO), 0, HALO - 1)
        self.lane = lane
        self.cols = cols

    def join(self, own, eastern, western):
        return jnp.where(self.is_east, eastern, jnp.where(self.is_west, western, own))

    def one(self, main, eastern, western, slot, west_shift=0):
        index = self.offset + slot * SLOT
        west_index = index + west_shift if west_shift else index
        return self.join(take(main, self.own), take(eastern, index), take(western, west_index))

    def both(self, first, second, eastern, western, slot):
        index = self.offset + jnp.where(self.second, slot * SLOT + SLOT, slot * SLOT)
        own = jnp.where(self.second, take(second, self.own), take(first, self.own))
        return self.join(own, take(eastern, index), take(western, index))

    def back(self, main, strip, p):
        index = jnp.where(self.lane < HALO, self.lane + 4 * HALO, self.lane - self.cols + 2 * HALO)
        index = jnp.clip(index, 0, STRIP - 1) + p * self.half
        edge = (self.lane < HALO) | (self.lane >= self.cols - HALO)
        return jnp.where(edge, take(strip, index), main)


def strip_kernel(t0, t3, raw, wet, r0, r1, out, s0, s1, s2, s3, face, ends):
    rows, cols = wet.shape
    lev = t0.shape[2]
    lon_even, _, _ = parities()
    strip = Strip(lev, cols)
    level = levels_of((lev, cols))
    groups = rows // GROUP
    wet_east, wet_west = r0, r1

    def mask_at(r):
        at = pl.ds(r % lev, 1)
        a = jnp.broadcast_to(r0[groups, at, :], (lev, cols))
        b = jnp.broadcast_to(r1[groups, at, :], (lev, cols))
        own = jnp.broadcast_to(wet_row(wet, r), (lev, cols))
        eastern, western = jnp.where(lon_even, a, b), jnp.where(lon_even, b, a)
        return jnp.where(level < strip.one(own, eastern, western, r // lev), 1.0, 0.0)

    def planes_at(r):
        pair = sides(lon_even, r0, r1, r // GROUP)
        slot = (r % GROUP) * PLANES
        s0[r] = strip.both(t0[r, 0], t0[r, 1], *pair, slot)
        return [strip.one(raw[r, i], *pair, slot + 2 + i) for i in range(3)] + [mask_at(r)]

    speed_e, speed_n, kappa, mask = planes_at(0)
    for r in range(rows):
        if r == 0 or r == rows - 1:
            for i, value in enumerate((speed_n, kappa, mask)):
                ends[r // (rows - 1), i] = value
        put_face(face, r, 0, coefficients(speed_e, kappa, east_of(kappa), mask * east_of(mask)))
        if r + 1 < rows:
            higher = planes_at(r + 1)
            put_face(face, r, 3, coefficients(speed_n, kappa, higher[2], mask * higher[3]))
            speed_e, speed_n, kappa, mask = higher
    sources, results = (s0, s1, s2), (s1, s2, s3)
    for s in range(STEPS):
        advance(
            2 * s + 2,
            rows - 2 * s - 2,
            lambda r: sources[s][r],
            lambda r: get_face(face, r, 0),
            lambda r: get_face(face, r, 3),
            lambda r, v: results[s].__setitem__(r, v),
        )
    for r in range(HALO, rows - HALO):
        for p in range(2):
            out[pl.ds(p * lev * rows + r, lev, stride=rows), :] = strip.back(t3[r, p], s3[r], p)


def frame_kernel(mid, t0, t1, t2, raw, face, wet, s0, s1, s2, sface, ends, x, y, out):
    rows, cols = wet.shape
    lev = t0.shape[2]
    _, lat_even, top = parities()
    strip = Strip(lev, cols)
    level = levels_of((lev, cols))
    turn = jnp.where(top, -1.0, 1.0)
    lane = strip.lane

    out[...] = mid[...]

    def halo(north):
        def piece(at):
            a, b = x[at], y[at]
            return jnp.where(lat_even, a, b) if north else jnp.where(lat_even, b, a)

        def wet_piece(at, sub):
            a = jnp.broadcast_to(x[at, pl.ds(sub, 1), :], (lev, cols))
            b = jnp.broadcast_to(y[at, pl.ds(sub, 1), :], (lev, cols))
            return jnp.where(lat_even, a, b) if north else jnp.where(lat_even, b, a)

        def pair(m):
            return piece(AT_PACK + m // GROUP), piece(AT_PACK + 2 + m // GROUP)

        main = dict(
            t=[[piece(AT_T + 2 * m + p) for p in range(2)] for m in range(HALO)],
            e=[piece(AT_E + m) for m in range(N_E)],
            n=[piece(AT_N + m) for m in range(N_N)],
            k=[piece(AT_K + m) for m in range(N_K)],
            w=[wet_piece(AT_WET, m) for m in range(N_K)],
        )
        slot = [(m % GROUP) * PLANES for m in range(HALO)]
        side = dict(
            t=[[strip.both(*main["t"][m], *pair(m), slot[m])] for m in range(HALO)],
            e=[strip.one(main["e"][m], *pair(m), slot[m] + 2) for m in range(N_E)],
            n=[strip.one(main["n"][m], *pair(m), slot[m] + 3) for m in range(N_N)],
            k=[strip.one(main["k"][m], *pair(m), slot[m] + 4) for m in range(N_K)],
            w=[],
        )
        for m in range(N_K):
            sub = jnp.where(top, lev - 1 - m, m) if north else lev - 1 - m
            corner = wet_piece(AT_PACK_WET, sub)
            side["w"].append(strip.one(main["w"][m], corner, corner, 0, SLOT))
        if north:
            cells = jnp.where(top, cols - 1 - lane, lane)
            faces = jnp.where(top, jnp.where(lane == cols - 1, cols - 1, cols - 2 - lane), lane)
            main = turned(main, cells, faces)
            last = STRIP - 1
            q = strip.q
            cells = jnp.where(top & (q <= last), strip.base + last - q, lane)
            faces = jnp.where(top & (q < last), strip.base + last - 1 - q, lane)
            side = turned(side, cells, faces)
        return main, side

    def turned(planes, cells, faces):
        return dict(
            t=[[take(v, cells) for v in values] for values in planes["t"]],
            e=[turn * take(v, faces) for v in planes["e"]],
            n=[turn * take(v, cells) for v in planes["n"]],
            k=[take(v, cells) for v in planes["k"]],
            w=[take(v, cells) for v in planes["w"]],
        )

    south, north = halo(False), halo(True)

    def run(kind, own, saved, own_face, end_planes):
        lower, upper = south[kind], north[kind]
        for planes in (lower, upper):
            planes["m"] = [jnp.where(level < w, 1.0, 0.0) for w in planes["w"]]
        (_, low_kappa, low_mask), (high_speed, high_kappa, high_mask) = end_planes
        east, northern = {}, {}
        for m in range(N_E):
            for r, planes in ((-1 - m, lower), (rows + m, upper)):
                kappa, mask = planes["k"][m], planes["m"][m]
                east[r] = coefficients(
                    planes["e"][m], kappa, east_of(kappa), mask * east_of(mask)
                )
        for m in range(N_N):
            kappa, mask = (low_kappa, low_mask) if m == 0 else (lower["k"][m - 1], lower["m"][m - 1])
            northern[-1 - m] = coefficients(
                lower["n"][m], lower["k"][m], kappa, lower["m"][m] * mask
            )
        for m in range(N_E + 1):
            if m == 0:
                kappa, mask = high_kappa, high_mask
                speed = jnp.where(top, 0.5 * (high_speed + upper["n"][0]), high_speed)
            else:
                kappa, mask = upper["k"][m - 1], upper["m"][m - 1]
                speed = jnp.where(top, upper["n"][m], upper["n"][m - 1]) if m < N_N else None
            northern[rows - 1 + m] = coefficients(speed, kappa, upper["k"][m], mask * upper["m"][m])
        east_at = lambda r: east[r] if r in east else get_face(own_face, r, 0)
        north_at = lambda r: northern[r] if r in northern else get_face(own_face, r, 3)
        finals = []
        for p in range(len(lower["t"][0])):
            now = {}
            for m in range(HALO):
                now[-1 - m], now[rows + m] = lower["t"][m][p], upper["t"][m][p]
            for s in range(STEPS):
                later = {}
                for low in (2 * s + 2 - HALO, rows - 2 * s - 2):
                    advance(
                        low,
                        low + HALO,
                        lambda r: now[r] if r in now else saved(s, r, p),
                        east_at,
                        north_at,
                        later.__setitem__,
                    )
                now = later
            finals.append(now)
        return finals

    def mask_at(r):
        return jnp.where(level < wet_row(wet, r), 1.0, 0.0)

    main_ends = [(raw[r, 1], raw[r, 2], mask_at(r)) for r in (0, rows - 1)]
    strip_ends = [tuple(ends[e, i] for i in range(3)) for e in range(2)]
    (columns,) = run(1, None, lambda s, r, p: (s0, s1, s2)[s][r], sface, strip_ends)
    finals = run(0, None, lambda s, r, p: (t0, t1, t2)[s][r, p], face, main_ends)
    for p in range(2):
        for r, value in finals[p].items():
            out[pl.ds(p * lev * rows + r, lev, stride=rows), :] = strip.back(value, columns[r], p)


def call(kernel, shapes, *operands, **options):
    return pl.pallas_call(
        kernel,
        out_shape=[jax.ShapeDtypeStruct(s, jnp.float32) for s in shapes],
        in_specs=[VMEM] * len(operands),
        out_specs=[VMEM] * len(shapes),
        **options,
    )(*operands)


def lon_swap(sizes, parity):
    lon, lat = sizes
    pairs = []
    for i in range(lon):
        other = (i + 1 if i % 2 == parity else i - 1) % lon
        pairs += [(i * lat + j, other * lat + j) for j in range(lat)]
    return pairs


def lat_swap(sizes, parity):
    lon, lat = sizes
    pairs = []
    for i in range(lon):
        for j in range(lat):
            if j % 2 != parity:
                if j > 0:
                    pairs.append((i * lat + j, i * lat + j - 1))
            elif j + 1 < lat:
                pairs.append((i * lat + j, i * lat + j + 1))
            else:
                pairs.append((i * lat + j, (lon - 1 - i) * lat + j))
    return pairs


def per_device(tracers, east_courant, north_courant, diffusivity, wet_levels):
    count, lev, rows, cols = tracers.shape
    sizes = (lax.axis_size("lon"), lax.axis_size("lat"))
    tr = tracers.reshape(count * lev * rows, cols)
    ec, nc, kd = (v.reshape(lev * rows, cols) for v in (east_courant, north_courant, diffusivity))
    block = (lev, cols)
    packed = (rows // GROUP + 1,) + block
    p0, p1, xm, ym = call(
        pack_kernel, [packed, packed, (AT_PACK,) + block, (AT_PACK,) + block],
        tr, ec, nc, kd, wet_levels,
    )
    r1 = lax.ppermute(p1, AXES, lon_swap(sizes, 1))
    r0 = lax.ppermute(p0, AXES, lon_swap(sizes, 0))
    state = (rows, count) + block
    t0, t1, t2, t3, raw, face = call(
        interior_kernel, [state] * 4 + [(rows, 3) + block, (rows, 6) + block],
        tr, ec, nc, kd, wet_levels,
    )
    x, y = call(forward_kernel, [(MESSAGE,) + block] * 2, xm, ym, r0, r1)
    y = lax.ppermute(y, AXES, lat_swap(sizes, 1))
    x = lax.ppermute(x, AXES, lat_swap(sizes, 0))
    mid, s0, s1, s2, s3, sface, ends = call(
        strip_kernel, [tr.shape] + [(rows,) + block] * 4 + [(rows, 6) + block, (2, 3) + block],
        t0, t3, raw, wet_levels, r0, r1,
    )
    (out,) = call(
        frame_kernel, [tr.shape],
        mid, t0, t1, t2, raw, face, wet_levels, s0, s1, s2, sface, ends, x, y,
    )
    return out.reshape(tracers.shape)


def solution(mesh):
    placed = (
        P(None, None, "lat", "lon"),
        P(None, "lat", "lon"),
        P(None, "lat", "lon"),
        P(None, "lat", "lon"),
        P("lat", "lon"),
    )
    return jax.shard_map(
        per_device,
        mesh=mesh,
        in_specs=placed,
        out_specs=P(None, None, "lat", "lon"),
        check_vma=False,
    )
```

time: 82 us -> 60.8 us (0.74)
  the two profiles are of different devices: /device:TPU:1 before, /device:TPU:24 now
where the time goes in v1:
time: 60.8 us; the launch traced here: 59.9 us
  Pallas kernels  49.3 us (81%)
  starting transfers between devices  7.15 us (12%)
  waiting for transfers between devices  2.15 us (4%)
  local copies, waits for them, and re-layouts  1.28 us (2%)
    pallas_call x5, Pallas kernels, call(): pl.pallas_call(kernel, out_shape=[jax.ShapeDtypeStruct(s, jnp.float32) fo...  49.3 us
    ppermute x1, starting transfers between devices, per_device(): y = lax.ppermute(y, AXES, lat_swap(sizes, 1))  4.13 us
    ppermute x1, starting transfers between devices, per_device(): r1 = lax.ppermute(p1, AXES, lon_swap(sizes, 1))  2.56 us
    ppermute x1, waiting for transfers between devices, per_device(): r1 = lax.ppermute(p1, AXES, lon_swap(sizes, 1))  2.15 us
    unnamed x8, local copies, waits for them, and re-layouts  1.28 us
  transfers between devices with their start and end apart: 4, of which 1 were waited for; matrix products, arithmetic and copies ran while one was open for 0% of the time, Pallas kernels for 59%

profile of v1, /device:TPU:24, one launch (start us, length us, event | category | flops | bytes accessed | tf_op | source)
XLA Modules:
  0.0 59.9 jit_solution(2253100285370316644)
XLA Ops:
  0.0 2.5 %shard_map.56 = (f32[13,8,128]{2,1,0:T(8,128)}, f32[13,8,128]{2,1,0:T(8,128)}, f32[27,8,128]{2,1,0:T(8,128)}, f32[27,8,128]{2,1,0:T(8,128)}) custom-call(f32[768,128]{1,0:T(8,128)} %bitcast.5, f32[384,128]{1,0:T(8,128)} %bitcast.7, f32[384,128]{1,0:T(8,128)} %bitcast.9, f32[384,128]{1,0:T(8,128)} %bitcast.11, s32[48,128]{1,0:T(8,128)} %wet.7), custom_call_target="tpu_custom_call" | custom-call | tf_op jit(solution)/shard_map/pallas_call | solution.py:415
  2.5 0.0 collective-permute-start
  2.6 2.6 %collective-permute-start.1 = (f32[13,8,128]{2,1,0:T(8,128)}, f32[13,8,128]{2,1,0:T(8,128)S(1)}, u32[]{:S(2)}, u32[]{:S(2)}) collective-permute-start(f32[13,8,128]{2,1,0:T(8,128)} %get-tuple-element.27), channel_id=1, source_target_pairs={{0,28},{1,29},{2,30},{3,31},{4,8},{5,9},{6,10},{7,11},{8,4},{9,5},... | collective-permute-start | bytes 159752 | tf_op jit(solution)/shard_map/ppermute | solution.py:459
  5.1 0.0 collective-permute-done.r0
  5.1 0.0 copy-start
  5.1 2.1 %collective-permute-done.1.r1 = f32[13,8,128]{2,1,0:T(8,128)S(1)} collective-permute-done((f32[13,8,128]{2,1,0:T(8,128)}, f32[13,8,128]{2,1,0:T(8,128)S(1)}, u32[]{:S(2)}, u32[]{:S(2)}) %collective-permute-start.1) | collective-permute-done | bytes 53280 | tf_op jit(solution)/shard_map/ppermute | solution.py:459
  7.3 0.0 copy-start.1
  7.3 0.0 copy-done
  7.3 0.6 %copy-done.1 = f32[13,8,128]{2,1,0:T(8,128)} copy-done((f32[13,8,128]{2,1,0:T(8,128)}, f32[13,8,128]{2,1,0:T(8,128)S(1)}, u32[]{:S(2)}) %copy-start.1) | copy-done | bytes 53272
  7.9 1.8 %shard_map.58 = (f32[32,8,128]{2,1,0:T(8,128)}, f32[32,8,128]{2,1,0:T(8,128)}) custom-call(f32[27,8,128]{2,1,0:T(8,128)} %get-tuple-element.37.xm, f32[27,8,128]{2,1,0:T(8,128)} %get-tuple-element.38.ym, f32[13,8,128]{2,1,0:T(8,128)} %copy-done, f32[13,8,128]{2,1,0:T(8,128)} %copy-done.1), custom_call_target="tpu_custom_call" | custom-call | tf_op jit(solution)/shard_map/pallas_call | solution.py:415
  9.7 0.5 collective-permute-start.2
  10.2 4.1 %collective-permute-start.3 = (f32[32,8,128]{2,1,0:T(8,128)}, f32[32,8,128]{2,1,0:T(8,128)S(1)}, u32[]{:S(2)}, u32[]{:S(2)}) collective-permute-start(f32[32,8,128]{2,1,0:T(8,128)} %get-tuple-element.40), channel_id=1, source_target_pairs={{1,2},{2,1},{3,31},{5,6},{6,5},{7,27},{9,10},{10,9},{11,23},{13,14... | collective-permute-start | bytes 393224 | tf_op jit(solution)/shard_map/ppermute | solution.py:467
  14.3 18.8 %shard_map.55 = (f32[48,2,8,128]{3,2,1,0:T(8,128)}, f32[48,2,8,128]{3,2,1,0:T(8,128)}, f32[48,2,8,128]{3,2,1,0:T(8,128)}, f32[48,2,8,128]{3,2,1,0:T(8,128)}, f32...) custom-call(f32[768,128]{1,0:T(8,128)} %bitcast.6, f32[384,128]{1,0:T(8,128)} %bitcast.8, f32[384,128]{1,0:T(8,128)} %bitcast.10, ...), custom_call_target="tpu_custom_call" | custom-call | tf_op jit(solution)/shard_map/pallas_call | solution.py:415
  33.0 16.4 %shard_map.57 = (f32[768,128]{1,0:T(8,128)}, f32[48,8,128]{2,1,0:T(8,128)}, f32[48,8,128]{2,1,0:T(8,128)}, f32[48,8,128]{2,1,0:T(8,128)}, f32[48,8,128]{2,1,0:T(...) custom-call(f32[48,2,8,128]{3,2,1,0:T(8,128)} %get-tuple-element.23.t0, ...), custom_call_target="tpu_custom_call" | custom-call | tf_op jit(solution)/shard_map/pallas_call | solution.py:415
  49.4 0.0 collective-permute-done.2.x
  49.4 0.0 copy-start.2
  49.4 0.0 collective-permute-done.3.y
  49.5 0.0 copy-start.3
  49.5 0.6 %copy-done.2 = f32[32,8,128]{2,1,0:T(8,128)} copy-done((f32[32,8,128]{2,1,0:T(8,128)}, f32[32,8,128]{2,1,0:T(8,128)S(1)}, u32[]{:S(2)}) %copy-start.2) | copy-done | bytes 131096
  50.1 0.1 copy-done.3
  50.1 9.8 %shard_map.59 = f32[768,128]{1,0:T(8,128)} custom-call(f32[768,128]{1,0:T(8,128)} %get-tuple-element.28.mid, f32[48,2,8,128]{3,2,1,0:T(8,128)} %get-tuple-element.23.t0, f32[48,2,8,128]{3,2,1,0:T(8,128)} %get-tuple-element.29.t1, f32[48,2,8,128]{3,2,1,0:T(8,128)} %get-tuple-element.30.t2, f32[48,3,8,128]{3,2,1,0:T(8,128)} %get-tuple-element.25.raw, ...), custom_call_target="tpu_custom_call" | custom-call | tf_op jit(solution)/shard_map/pallas_call | solution.py:415
Async XLA Ops:
  2.5 2.6 %collective-permute-start = (f32[13,8,128]{2,1,0:T(8,128)}, f32[13,8,128]{2,1,0:T(8,128)S(1)}, u32[]{:S(2)}, u32[]{:S(2)}) collective-permute-start(f32[13,8,128]{2,1,0:T(8,128)} %get-tuple-element.26), channel_id=1, source_target_pairs={{0,4},{1,5},{2,6},{3,7},{4,0},{5,1},{6,2},{7,3},{8,12},{9,13},{10,... | collective-permute-start | bytes 159752 | tf_op jit(solution)/shard_map/ppermute | solution.py:460
  2.6 4.7 %collective-permute-start.1 = (f32[13,8,128]{2,1,0:T(8,128)}, f32[13,8,128]{2,1,0:T(8,128)S(1)}, u32[]{:S(2)}, u32[]{:S(2)}) collective-permute-start(f32[13,8,128]{2,1,0:T(8,128)} %get-tuple-element.27), channel_id=1, source_target_pairs={{0,28},{1,29},{2,30},{3,31},{4,8},{5,9},{6,10},{7,11},{8,4},{9,5},... | collective-permute-start | bytes 159752 | tf_op jit(solution)/shard_map/ppermute | solution.py:459
  5.1 2.2 %copy-start = (f32[13,8,128]{2,1,0:T(8,128)}, f32[13,8,128]{2,1,0:T(8,128)S(1)}, u32[]{:S(2)}) copy-start(f32[13,8,128]{2,1,0:T(8,128)S(1)} %collective-permute-done.r0) | copy-start | bytes 159748
  7.3 0.6 %copy-start.1 = (f32[13,8,128]{2,1,0:T(8,128)}, f32[13,8,128]{2,1,0:T(8,128)S(1)}, u32[]{:S(2)}) copy-start(f32[13,8,128]{2,1,0:T(8,128)S(1)} %collective-permute-done.1.r1) | copy-start | bytes 159748
  9.7 39.7 %collective-permute-start.2 = (f32[32,8,128]{2,1,0:T(8,128)}, f32[32,8,128]{2,1,0:T(8,128)S(1)}, u32[]{:S(2)}, u32[]{:S(2)}) collective-permute-start(f32[32,8,128]{2,1,0:T(8,128)} %get-tuple-element.39), channel_id=1, source_target_pairs={{0,1},{1,0},{2,3},{3,2},{4,5},{5,4},{6,7},{7,6},{8,9},{9,8},{10,11... | collective-permute-start | bytes 393224 | tf_op jit(solution)/shard_map/ppermute | solution.py:468
  10.2 39.3 %collective-permute-start.3 = (f32[32,8,128]{2,1,0:T(8,128)}, f32[32,8,128]{2,1,0:T(8,128)S(1)}, u32[]{:S(2)}, u32[]{:S(2)}) collective-permute-start(f32[32,8,128]{2,1,0:T(8,128)} %get-tuple-element.40), channel_id=1, source_target_pairs={{1,2},{2,1},{3,31},{5,6},{6,5},{7,27},{9,10},{10,9},{11,23},{13,14... | collective-permute-start | bytes 393224 | tf_op jit(solution)/shard_map/ppermute | solution.py:467
  49.4 0.6 %copy-start.2 = (f32[32,8,128]{2,1,0:T(8,128)}, f32[32,8,128]{2,1,0:T(8,128)S(1)}, u32[]{:S(2)}) copy-start(f32[32,8,128]{2,1,0:T(8,128)S(1)} %collective-permute-done.2.x) | copy-start | bytes 393220
  49.5 0.7 %copy-start.3 = (f32[32,8,128]{2,1,0:T(8,128)}, f32[32,8,128]{2,1,0:T(8,128)S(1)}, u32[]{:S(2)}) copy-start(f32[32,8,128]{2,1,0:T(8,128)S(1)} %collective-permute-done.3.y) | copy-start | bytes 393220

commit v2 on v0

v2 whole, which is shorter than its diff:
```python
import jax
import jax.numpy as jnp
from jax import lax
from jax.experimental import pallas as pl
from jax.experimental.pallas import tpu as pltpu
from jax.sharding import PartitionSpec as P

STEPS = 3
HALO = 2 * STEPS
AXES = ("lon", "lat")
SUB = 8
PLANES = 5
KINDS = 3
PAIR = 2
SMALL = 16 << 20
VMEM = pl.BlockSpec(memory_space=pltpu.VMEM)
ANY = pl.BlockSpec(memory_space=pl.ANY)

AT_T, AT_E, AT_N, AT_K, AT_WET, MESSAGE = 0, 12, 16, 21, 26, 27
N_E, N_N, N_K = HALO - 2, HALO - 1, HALO - 1


def lanes(shape):
    return lax.broadcasted_iota(jnp.int32, shape, len(shape) - 1)


def take(value, index):
    return jnp.take_along_axis(value, index, axis=1)


def later_block(value):
    return pltpu.roll(value, value.shape[1] - 1, 1)


def earlier_block(value):
    return pltpu.roll(value, 1, 1)


def loop(count, body):
    def step(i, _):
        body(i)
        return 0

    lax.fori_loop(0, count, step, 0)


def parities():
    lon_even = lax.rem(lax.axis_index("lon"), 2) == 0
    lat = lax.axis_index("lat")
    return lon_even, lax.rem(lat, 2) == 0, lat == lax.axis_size("lat") - 1


def stage_kernel(tr, ec, nc, kd, wet, own, x, y, counts, done):
    lev = ec.shape[0]
    copies = [(tr, own.at[pl.ds(0, 2 * lev)]), (wet, counts)]
    copies += [(a, own.at[pl.ds(i * lev, lev)]) for i, a in ((2, ec), (3, nc), (4, kd))]
    copies = [pltpu.make_async_copy(a, b, done.at[i]) for i, (a, b) in enumerate(copies)]
    for copy in copies:
        copy.start()
    for copy in copies:
        copy.wait()
    own[own.shape[0] - 1] = counts[...].astype(jnp.float32)
    count, rows, cols = own.shape
    lev = count // PLANES
    _, lat_even, _ = parities()
    flat = own.reshape(count * rows, cols)
    for out, upper in ((x, lat_even), (y, jnp.logical_not(lat_even))):
        row = [jnp.where(upper, rows - 1 - m, m) for m in range(HALO)]

        def plane(i, m):
            return flat[pl.ds(i * lev * rows + row[m], lev, stride=rows), :]

        for m in range(HALO):
            for i in range(2):
                out[AT_T + 2 * m + i] = plane(i, m)
        for at, i, n in ((AT_E, 2, N_E), (AT_N, 3, N_N), (AT_K, 4, N_K)):
            for m in range(n):
                out[at + m] = plane(i, m)
        out[AT_WET] = jnp.zeros((lev, cols), jnp.float32)
        for m in range(N_K):
            out[AT_WET, pl.ds(m, 1), :] = own[count - 1, pl.ds(row[m], 1), :]


def turn_kernel(own, x, y, t0, se, sn, kw, p0, p1, te, ee, ne, ke):
    count, rows, cols = own.shape
    lev = count // PLANES
    planes = 2 * lev
    tall = rows + 2 * SUB
    lon_even, lat_even, top = parities()
    shape = (lev, cols)
    lane = lanes(shape)
    level = lax.broadcasted_iota(jnp.int32, shape, 0).astype(jnp.float32)
    zero = jnp.zeros((SUB, cols), jnp.float32)

    def fill(p):
        for e in range(tall // SUB):
            halo = e == 0 or e == tall // SUB - 1
            at = pl.ds(0 if halo else (e - 1) * SUB, SUB)

            def put_tile(target, q, value):
                target[pl.ds(pl.multiple_of(q * tall + e * SUB, SUB), SUB), :] = zero if halo else value

            for i in range(2):
                put_tile(te, p + i * lev, own[p + i * lev, at, :])
            put_tile(ee, p, own[p + 2 * lev, at, :])
            put_tile(ne, p, own[p + 3 * lev, at, :])
            counts = own[count - 1, at, :]
            put_tile(ke, p, jnp.where(counts > p.astype(jnp.float32), own[p + 4 * lev, at, :], -1.0))

    loop(lev, fill)

    turn = jnp.where(top, -1.0, 1.0)
    cells = jnp.where(top, cols - 1 - lane, lane)
    faces = jnp.where(top, jnp.where(lane == cols - 1, cols - 1, cols - 2 - lane), lane)
    for north in (False, True):
        def piece(at):
            a, b = x[at], y[at]
            return jnp.where(lat_even, a, b) if north else jnp.where(lat_even, b, a)

        def put(target, row, value, first=0):
            target[pl.ds(first * tall + row, lev, stride=tall), :] = value

        def turned(value, index):
            return take(value, index) if north else value

        at = [tall - SUB + m if north else SUB - 1 - m for m in range(HALO)]
        for m in range(HALO):
            for i in range(2):
                put(te, at[m], turned(piece(AT_T + 2 * m + i), cells), i * lev)
        wets = piece(AT_WET)
        for m in range(N_K):
            counts = jnp.broadcast_to(wets[m : m + 1], shape)
            kappa = jnp.where(level < counts, piece(AT_K + m), -1.0)
            put(ke, at[m], turned(kappa, cells))
        for m in range(N_E):
            value = turned(piece(AT_E + m), faces)
            put(ee, at[m], turn * value if north else value)
        if north:
            speeds = [turn * take(piece(AT_N + m), cells) for m in range(N_N)]
            last = ne[pl.ds(tall - SUB - 1, lev, stride=tall), :]
            put(ne, tall - SUB - 1, jnp.where(top, 0.5 * (last + speeds[0]), last))
            for m in range(N_E):
                put(ne, at[m], jnp.where(top, speeds[m + 1], speeds[m]))
        else:
            for m in range(N_N):
                put(ne, at[m], piece(AT_N + m))

    def transpose(i):
        for j in (2 * i, 2 * i + 1):
            for source, target, n in ((te, t0, planes), (ee, se, lev), (ne, sn, lev), (ke, kw, lev)):
                parts = [source[pl.ds(p * tall + j, tall // SUB, stride=SUB), :] for p in range(n)]
                matrix = jnp.concatenate(parts * (planes // n), 0)
                target[j, pl.ds(SUB, cols), :] = matrix.T

    loop(SUB // 2, transpose)
    for j in range(SUB):
        se[j, pl.ds(SUB - 1, 1), :] = se[j, pl.ds(SUB + cols - 1, 1), :]

    left = lanes((SUB, cols)) < cols // 2

    def edges(j):
        for out, eastern in ((p0, lon_even), (p1, jnp.logical_not(lon_even))):
            start = jnp.where(eastern, SUB + cols - HALO, SUB)
            here = pl.ds(start, SUB)
            faced = pl.ds(jnp.where(eastern, start, start - 1), SUB)
            kappa = kw[j, here, :]
            values = (
                t0[j, here, :],
                jnp.where(left, se[j, faced, :], sn[j, here, :]),
                jnp.where(left, jnp.maximum(kappa, 0.0), jnp.where(kappa > 0, 1.0, 0.0)),
            )
            for i, value in enumerate(values):
                out[pl.ds((KINDS * j + i) * HALO + 2, SUB), :] = value

    for out in (p0, p1):
        out[0:SUB, :] = zero
        out[out.shape[0] - SUB : out.shape[0], :] = zero
    loop(SUB, edges)


def coefficients(speed, kappa, other_kappa):
    wet = jnp.minimum(kappa, other_kappa) > 0
    speed = jnp.where(wet, speed, 0.0)
    magnitude = jnp.abs(speed)
    spread = jnp.minimum(speed, 0.0) - jnp.where(wet, 0.5 * (kappa + other_kappa), 0.0)
    return speed, spread, 0.5 * magnitude * (1.0 - magnitude)


def all_coefficients(se, sn, kw, face, low, at, kappa_low, kappa_high, north_low):
    here = pl.ds(at, SUB)
    kappa = [kw[j, here, :] for j in range(SUB)] + [kappa_high]
    for c, value in enumerate(coefficients(north_low, kappa_low, kappa[0])):
        low[c, here, :] = value
    for j in range(SUB):
        eastern = coefficients(se[j, here, :], kappa[j], kw[j, pl.ds(at + 1, SUB), :])
        northern = coefficients(sn[j, here, :], kappa[j], kappa[j + 1])
        for c, value in enumerate(eastern + northern):
            face[c, j, here, :] = value


def flux(cell, before, here, after, face):
    speed, spread, slope = face
    upslope = jnp.where(speed > 0, before, after)
    limited = jnp.maximum(
        jnp.minimum(here, upslope), jnp.minimum(jnp.maximum(here, upslope), 0.0)
    )
    return speed * cell + spread * here + slope * limited


def east_flux(t, face, s, j, at):
    behind, cell, after, beyond = (t[s, j, pl.ds(at + i, SUB), :] for i in (-1, 0, 1, 2))
    coefs = tuple(face[c, j, pl.ds(at, SUB), :] for c in range(3))
    return flux(cell, cell - behind, after - cell, beyond - after, coefs)


def advance(t, face, low, s, at, beside, fluxes=None):
    here = pl.ds(at, SUB)
    cell = [t[s, j, here, :] for j in range(SUB)]
    if fluxes is None:
        divergence = [
            east_flux(t, face, s, j, at) - east_flux(t, face, s, j, at - 1) for j in range(SUB)
        ]
    else:
        east = [east_flux(t, face, s, j, at) for j in range(SUB)]
        for j in range(SUB):
            fluxes[j, here, :] = east[j]
        divergence = [east[j] - fluxes[j, pl.ds(at - 1, SUB), :] for j in range(SUB)]
    rows = [beside[0], beside[1], *cell, beside[2], beside[3]]
    slope = [b - a for a, b in zip(rows, rows[1:])]
    north = []
    for j in range(-1, SUB):
        coefs = tuple(low[c, here, :] if j < 0 else face[3 + c, j, here, :] for c in range(3))
        north.append(flux(rows[j + 2], slope[j + 1], slope[j + 2], slope[j + 3], coefs))
    for j in range(SUB):
        t[s + 1, j, here, :] = cell[j] - divergence[j] - (north[j + 1] - north[j])


def rows_beside(t, s, at):
    here = pl.ds(at, SUB)
    before = [earlier_block(t[s, j, here, :]) for j in (SUB - 2, SUB - 1)]
    return before + [later_block(t[s, j, here, :]) for j in (0, 1)]


def interior_kernel(t0, se, sn, kw, t, face, low, fluxes, beside):
    cols = t.shape[3]
    passes = cols // SUB // PAIR

    def start(g):
        return pl.multiple_of(SUB + g * SUB, SUB)

    def turn_coefficients(b):
        values = []
        for k in range(PAIR):
            here = pl.ds(start(b * PAIR + k), SUB)
            values.append((
                earlier_block(kw[SUB - 1, here, :]),
                later_block(kw[0, here, :]),
                earlier_block(sn[SUB - 1, here, :]),
            ))
        return values

    def turn_cells(n):
        s = lax.div(n, passes)
        return [rows_beside(t, s, start((n - s * passes) * PAIR + k)) for k in range(PAIR)]

    def keep(values):
        for k, group in enumerate(values):
            for i, value in enumerate(group):
                beside[k, i] = value

    def prepare(b):
        turned = [[beside[k, i] for i in range(3)] for k in range(PAIR)]
        later = turn_coefficients(jnp.minimum(b + 1, passes - 1))
        for k in range(PAIR):
            at = start(b * PAIR + k)
            for j in range(SUB):
                t[0, j, pl.ds(at, SUB), :] = t0[j, pl.ds(at, SUB), :]
            all_coefficients(se, sn, kw, face, low, at, *turned[k])
        keep(later)

    keep(turn_coefficients(0))
    loop(passes, prepare)
    keep(turn_cells(0))

    def step(n):
        turned = [[beside[k, i] for i in range(4)] for k in range(PAIR)]
        s = lax.div(n, passes)
        later = turn_cells(jnp.minimum(n + 1, STEPS * passes - 1))
        for k in range(PAIR):
            advance(t, face, low, s, start((n - s * passes) * PAIR + k), turned[k], fluxes)
        keep(later)

    loop(STEPS * passes, step)


def frame_kernel(t_in, face_in, se_in, sn_in, kw_in, low_in, r0, r1, out, t, face, se, sn, kw, low, tall, done):
    cols = t.shape[3]
    planes, rows = out.shape[:2]
    height = tall.shape[0] // planes
    lon_even, _, top = parities()
    shape = (SUB, cols)
    lane = lanes(shape)
    sub = lax.broadcasted_iota(jnp.int32, shape, 0)
    left = lane < cols // 2
    fold = top & ((lane & (height // SUB - 1)) == height // SUB - 1)
    end = SUB + cols

    def halves(value):
        other = pltpu.roll(value, cols // 2, 1)
        return jnp.where(left, value, other), jnp.where(left, other, value)

    def unpack(j):
        for west in (False, True):
            def piece(i):
                at = pl.ds((KINDS * j + i) * HALO + (0 if west else 2), SUB)
                a, b = r0[at, :], r1[at, :]
                return jnp.where(lon_even, b, a) if west else jnp.where(lon_even, a, b)

            here = pl.ds(0 if west else end, SUB)
            t[0, j, here, :] = piece(0)
            speed, northern = halves(piece(1))
            kappa, wet = halves(piece(2))
            sn[j, here, :] = northern
            kw[j, here, :] = jnp.where(wet > 0, kappa, -1.0)
            if west:
                kept = (sub == SUB - 1) & fold
            else:
                here = pl.ds(end - 1, SUB)
                kept = (sub == 0) & jnp.logical_not(fold)
            se[j, here, :] = jnp.where(kept, se[j, here, :], speed)

    def unpack_two(i):
        for k in range(2):
            unpack(2 * i + k)

    loop(SUB // 2, unpack_two)
    for at in (0, end - 1):
        here = pl.ds(at, SUB)
        all_coefficients(
            se, sn, kw, face, low, at,
            earlier_block(kw[SUB - 1, here, :]), later_block(kw[0, here, :]), earlier_block(sn[SUB - 1, here, :]),
        )

    def step(s):
        west = SUB - 2 * (STEPS - 1) + 2 * s
        east = end - SUB + 2 * (STEPS - 1) - 2 * s
        beside = [rows_beside(t, s, at) for at in (west, east)]
        for at, rows_turned in zip((west, east), beside):
            advance(t, face, low, s, at, rows_turned)

    loop(STEPS, step)

    def transpose(i):
        n = height // SUB
        for k in range(4):
            j = 4 * i + k
            matrix = t[STEPS, j, pl.ds(SUB, cols), :].T
            for p in range(planes):
                tall[pl.ds(p * height + j, n, stride=SUB), :] = matrix[p * n : (p + 1) * n]

    loop(SUB // 4, transpose)
    copy = pltpu.make_async_copy(
        tall.reshape(planes, height, cols).at[:, pl.ds(SUB, rows), :], out, done
    )
    copy.start()
    copy.wait()


def call(kernel, shapes, *operands, specs=None, outs=None, grant=SMALL, scratch=(), alias=None):
    return pl.pallas_call(
        kernel,
        out_shape=[jax.ShapeDtypeStruct(s, jnp.float32) for s in shapes],
        in_specs=specs or [VMEM] * len(operands),
        out_specs=outs or [VMEM] * len(shapes),
        scratch_shapes=[pltpu.VMEM(s, jnp.float32) if isinstance(s, tuple) else s for s in scratch],
        input_output_aliases=alias or {},
        compiler_params=pltpu.CompilerParams(vmem_limit_bytes=grant),
        cost_estimate=pl.CostEstimate(flops=1 << 20, bytes_accessed=1 << 20, transcendentals=0),
    )(*operands)


def lon_swap(sizes, parity):
    lon, lat = sizes
    pairs = []
    for i in range(lon):
        other = (i + 1 if i % 2 == parity else i - 1) % lon
        pairs += [(i * lat + j, other * lat + j) for j in range(lat)]
    return pairs


def lat_swap(sizes, parity):
    lon, lat = sizes
    pairs = []
    for i in range(lon):
        for j in range(lat):
            if j % 2 != parity:
                if j > 0:
                    pairs.append((i * lat + j, i * lat + j - 1))
            elif j + 1 < lat:
                pairs.append((i * lat + j, i * lat + j + 1))
            else:
                pairs.append((i * lat + j, (lon - 1 - i) * lat + j))
    return pairs


def per_device(tracers, east_courant, north_courant, diffusivity, wet_levels):
    count, lev, rows, cols = tracers.shape
    planes, tall = count * lev, rows + 2 * SUB
    assert planes * (tall // SUB) == cols and rows % SUB == 0
    sizes = (lax.axis_size("lon"), lax.axis_size("lat"))
    message = (MESSAGE, lev, cols)
    stack = (PLANES * lev + 1, rows, cols)
    own, x, y = call(
        stage_kernel, [stack, message, message],
        *(
            pltpu.with_memory_space_constraint(v, pltpu.HBM)
            for v in (tracers.reshape(planes, rows, cols), east_courant, north_courant, diffusivity, wet_levels)
        ),
        specs=[ANY] * 5,
        scratch=[pltpu.VMEM((rows, cols), jnp.int32), pltpu.SemaphoreType.DMA((5,))],
    )
    y = lax.ppermute(y, AXES, lat_swap(sizes, 1))
    x = lax.ppermute(x, AXES, lat_swap(sizes, 0))
    wide = (SUB, cols + 2 * SUB, cols)
    packed = (-(-(SUB * KINDS * HALO + SUB) // SUB) * SUB, cols)
    t0, se, sn, kw, p0, p1 = call(
        turn_kernel, [wide] * 4 + [packed] * 2, own, x, y,
        scratch=[(n * tall, cols) for n in (planes, lev, lev, lev)],
    )
    r1 = lax.ppermute(p1, AXES, lon_swap(sizes, 1))
    r0 = lax.ppermute(p0, AXES, lon_swap(sizes, 0))
    t, face, low = call(
        interior_kernel, [(STEPS + 1,) + wide, (6,) + wide, (3,) + wide[1:]], t0, se, sn, kw,
        scratch=[wide, (PAIR, 4, SUB, cols)],
    )
    out, *_ = call(
        frame_kernel, [(planes, rows, cols), t.shape, face.shape, wide, wide, wide, low.shape],
        t, face, se, sn, kw, low, r0, r1,
        outs=[ANY] + [VMEM] * 6, alias={i: i + 1 for i in range(6)},
        scratch=[(planes * tall, cols), pltpu.SemaphoreType.DMA],
    )
    return out.reshape(tracers.shape)


def solution(mesh):
    placed = (
        P(None, None, "lat", "lon"),
        P(None, "lat", "lon"),
        P(None, "lat", "lon"),
        P(None, "lat", "lon"),
        P("lat", "lon"),
    )
    return jax.shard_map(
        per_device,
        mesh=mesh,
        in_specs=placed,
        out_specs=P(None, None, "lat", "lon"),
        check_vma=False,
    )
```

time: 82 us -> 18.9 us (0.23)
  the two profiles are of different devices: /device:TPU:1 before, /device:TPU:24 now
where the time goes in v2:
time: 18.9 us; the launch traced here: 18.7 us
  Pallas kernels  7.65 us (40%)
  starting transfers between devices  6.49 us (34%)
  waiting for transfers between devices  4.52 us (24%)
    pallas_call x4, Pallas kernels, call(): pl.pallas_call(kernel, out_shape=[jax.ShapeDtypeStruct(s, jnp.float32) fo...  7.65 us
    ppermute x1, waiting for transfers between devices, per_device(): y = lax.ppermute(y, AXES, lat_swap(sizes, 1))  3.68 us
    ppermute x1, starting transfers between devices, per_device(): y = lax.ppermute(y, AXES, lat_swap(sizes, 1))  3.5 us
    ppermute x1, starting transfers between devices, per_device(): r1 = lax.ppermute(p1, AXES, lon_swap(sizes, 1))  2.29 us
    ppermute x1, waiting for transfers between devices, per_device(): x = lax.ppermute(x, AXES, lat_swap(sizes, 0))  0.84 us
    ppermute x1, starting transfers between devices, per_device(): x = lax.ppermute(x, AXES, lat_swap(sizes, 0))  0.51 us
  transfers between devices with their start and end apart: 4, of which 2 were waited for; matrix products, arithmetic and copies ran while one was open for 0% of the time, Pallas kernels for 17%

profile of v2, /device:TPU:24, one launch (start us, length us, event | category | flops | bytes accessed | tf_op | source)
XLA Modules:
  0.0 18.7 jit_solution(14513844942760226154)
XLA Ops:
  0.0 1.4 %shard_map.55 = (f32[41,48,128]{2,1,0:T(8,128)S(1)}, f32[27,8,128]{2,1,0:T(8,128)S(1)}, f32[27,8,128]{2,1,0:T(8,128)S(1)}) custom-call(f32[16,48,128]{2,1,0:T(8,128)} %bitcast.2, f32[8,48,128]{2,1,0:T(8,128)} %ec.1, f32[8,48,128]{2,1,0:T(8,128)} %nc.1, f32[8,48,128]{2,1,0:T(8,128)} %kd.1, s32[48,128]{1,0:T(8,128)} %wet.1), custom_call_target="tpu_custom_call" | custom-call | flops 1048576 | bytes 1048576 | tf_op jit(solution)/shard_map/pallas_call | solution.py:370
  1.4 0.5 %collective-permute-start = (f32[27,8,128]{2,1,0:T(8,128)S(1)}, f32[27,8,128]{2,1,0:T(8,128)S(1)}, u32[]{:S(2)}, u32[]{:S(2)}) collective-permute-start(f32[27,8,128]{2,1,0:T(8,128)S(1)} %get-tuple-element.19), channel_id=1, source_target_pairs={{0,1},{1,0},{2,3},{3,2},{4,5},{5,4},{6,7},{7,6},{8,9},{9,8},{10,11... | collective-permute-start | bytes 331784 | tf_op jit(solution)/shard_map/ppermute | solution.py:423
  1.9 3.5 %collective-permute-start.1 = (f32[27,8,128]{2,1,0:T(8,128)S(1)}, f32[27,8,128]{2,1,0:T(8,128)S(1)}, u32[]{:S(2)}, u32[]{:S(2)}) collective-permute-start(f32[27,8,128]{2,1,0:T(8,128)S(1)} %get-tuple-element.20), channel_id=1, source_target_pairs={{1,2},{2,1},{3,31},{5,6},{6,5},{7,27},{9,10},{10,9},{11,23},{13,14... | collective-permute-start | bytes 331784 | tf_op jit(solution)/shard_map/ppermute | solution.py:422
  5.4 0.8 %collective-permute-done.x = f32[27,8,128]{2,1,0:T(8,128)S(1)} collective-permute-done((f32[27,8,128]{2,1,0:T(8,128)S(1)}, f32[27,8,128]{2,1,0:T(8,128)S(1)}, u32[]{:S(2)}, u32[]{:S(2)}) %collective-permute-start) | collective-permute-done | bytes 110624 | tf_op jit(solution)/shard_map/ppermute | solution.py:423
  6.2 3.7 %collective-permute-done.1.y = f32[27,8,128]{2,1,0:T(8,128)S(1)} collective-permute-done((f32[27,8,128]{2,1,0:T(8,128)S(1)}, f32[27,8,128]{2,1,0:T(8,128)S(1)}, u32[]{:S(2)}, u32[]{:S(2)}) %collective-permute-start.1) | collective-permute-done | bytes 110624 | tf_op jit(solution)/shard_map/ppermute | solution.py:422
  9.9 1.2 %shard_map.56 = (f32[8,144,128]{2,1,0:T(8,128)S(1)}, f32[8,144,128]{2,1,0:T(8,128)S(1)}, f32[8,144,128]{2,1,0:T(8,128)S(1)}, f32[8,144,128]{2,1,0:T(8,128)S(1)},...) custom-call(f32[41,48,128]{2,1,0:T(8,128)S(1)} %get-tuple-element.18.own, f32[27,8,128]{2,1,0:T(8,128)S(1)} %collective-permute-done.x, ...), custom_call_target="tpu_custom_call" | custom-call | flops 1048576 | bytes 1048576 | tf_op jit(solution)/shard_map/pallas_call | solution.py:370
  11.1 0.2 collective-permute-start.2
  11.3 2.3 %collective-permute-start.3 = (f32[152,128]{1,0:T(8,128)S(1)}, f32[152,128]{1,0:T(8,128)S(1)}, u32[]{:S(2)}, u32[]{:S(2)}) collective-permute-start(f32[152,128]{1,0:T(8,128)S(1)} %get-tuple-element.29), channel_id=1, source_target_pairs={{0,28},{1,29},{2,30},{3,31},{4,8},{5,9},{6,10},{7,11},{8,4},{9,5},... | collective-permute-start | bytes 233480 | tf_op jit(solution)/shard_map/ppermute | solution.py:430
  13.6 3.2 %shard_map.57 = (f32[4,8,144,128]{3,2,1,0:T(8,128)S(1)}, f32[6,8,144,128]{3,2,1,0:T(8,128)S(1)}, f32[3,144,128]{2,1,0:T(8,128)S(1)}) custom-call(f32[8,144,128]{2,1,0:T(8,128)S(1)} %get-tuple-element.21.t0, f32[8,144,128]{2,1,0:T(8,128)S(1)} %get-tuple-element.22.se.se_in, f32[8,144,128]{2,1,0:T(8,128)S(1)} %get-tuple-element.23.sn.sn_in, ...), custom_call_target="tpu_custom_call" | custom-call | flops 1048576 | bytes 1048576 | tf_op jit(solution)/shard_map/pallas_call | solution.py:370
  16.8 0.0 collective-permute-done.2.r0
  16.8 0.0 collective-permute-done.3.r1
  16.8 1.9 %shard_map.58 = (f32[16,48,128]{2,1,0:T(8,128)}, f32[4,8,144,128]{3,2,1,0:T(8,128)S(1)}, f32[6,8,144,128]{3,2,1,0:T(8,128)S(1)}, f32[8,144,128]{2,1,0:T(8,128)S(...) custom-call(f32[4,8,144,128]{3,2,1,0:T(8,128)S(1)} %get-tuple-elemen, ...), custom_call_target="tpu_custom_call", output_to_operand_aliasing={{1}: (0, {}), {2}: (1, {}), {3}: (2, {}), {4}: (3, {}), {5}... | custom-call | flops 1048576 | bytes 1048576 | tf_op jit(solution)/shard_map/pallas_call | solution.py:370
Async XLA Ops:
  1.4 4.9 %collective-permute-start = (f32[27,8,128]{2,1,0:T(8,128)S(1)}, f32[27,8,128]{2,1,0:T(8,128)S(1)}, u32[]{:S(2)}, u32[]{:S(2)}) collective-permute-start(f32[27,8,128]{2,1,0:T(8,128)S(1)} %get-tuple-element.19), channel_id=1, source_target_pairs={{0,1},{1,0},{2,3},{3,2},{4,5},{5,4},{6,7},{7,6},{8,9},{9,8},{10,11... | collective-permute-start | bytes 331784 | tf_op jit(solution)/shard_map/ppermute | solution.py:423
  1.9 8.0 %collective-permute-start.1 = (f32[27,8,128]{2,1,0:T(8,128)S(1)}, f32[27,8,128]{2,1,0:T(8,128)S(1)}, u32[]{:S(2)}, u32[]{:S(2)}) collective-permute-start(f32[27,8,128]{2,1,0:T(8,128)S(1)} %get-tuple-element.20), channel_id=1, source_target_pairs={{1,2},{2,1},{3,31},{5,6},{6,5},{7,27},{9,10},{10,9},{11,23},{13,14... | collective-permute-start | bytes 331784 | tf_op jit(solution)/shard_map/ppermute | solution.py:422
  11.1 5.7 %collective-permute-start.2 = (f32[152,128]{1,0:T(8,128)S(1)}, f32[152,128]{1,0:T(8,128)S(1)}, u32[]{:S(2)}, u32[]{:S(2)}) collective-permute-start(f32[152,128]{1,0:T(8,128)S(1)} %get-tuple-element.28), channel_id=1, source_target_pairs={{0,4},{1,5},{2,6},{3,7},{4,0},{5,1},{6,2},{7,3},{8,12},{9,13},{10,... | collective-permute-start | bytes 233480 | tf_op jit(solution)/shard_map/ppermute | solution.py:431
  11.3 5.5 %collective-permute-start.3 = (f32[152,128]{1,0:T(8,128)S(1)}, f32[152,128]{1,0:T(8,128)S(1)}, u32[]{:S(2)}, u32[]{:S(2)}) collective-permute-start(f32[152,128]{1,0:T(8,128)S(1)} %get-tuple-element.29), channel_id=1, source_target_pairs={{0,28},{1,29},{2,30},{3,31},{4,8},{5,9},{6,10},{7,11},{8,4},{9,5},... | collective-permute-start | bytes 233480 | tf_op jit(solution)/shard_map/ppermute | solution.py:430

commit v3 on v2

--- a/solution.py
+++ b/solution.py
@@ -5,13 +5,17 @@
 from jax.experimental.pallas import tpu as pltpu
 from jax.sharding import PartitionSpec as P
 
+
 STEPS = 3
 HALO = 2 * STEPS
 AXES = ("lon", "lat")
 SUB = 8
-PLANES = 5
-KINDS = 3
-PAIR = 2
+FEW = HALO - 1
+AT_SPEED, AT_KAPPA = SUB * HALO, SUB * HALO + SUB * FEW
+AT_COUNT = AT_KAPPA + SUB // 2 * FEW
+SPARE = 2
+PAIR = 4
+COLUMNS = -(-(SPARE + AT_COUNT + SUB) // SUB) * SUB
 SMALL = 16 << 20
 VMEM = pl.BlockSpec(memory_space=pltpu.VMEM)
 ANY = pl.BlockSpec(memory_space=pl.ANY)
@@ -50,72 +54,94 @@
     return lon_even, lax.rem(lat, 2) == 0, lat == lax.axis_size("lat") - 1
 
 
-def stage_kernel(tr, ec, nc, kd, wet, own, x, y, counts, done):
+def edge_kernel(tr, ec, nc, kd, wet, x, y, trs, ecs, ncs, kds, wets, done):
+    rows, cols = wet.shape
     lev = ec.shape[0]
-    copies = [(tr, own.at[pl.ds(0, 2 * lev)]), (wet, counts)]
-    copies += [(a, own.at[pl.ds(i * lev, lev)]) for i, a in ((2, ec), (3, nc), (4, kd))]
+    _, lat_even, _ = parities()
+    copies = []
+    for side, start in enumerate((0, rows - SUB)):
+        for source, target in ((tr, trs), (ec, ecs), (nc, ncs), (kd, kds)):
+            n = source.shape[0]
+            copies.append((source.at[:, pl.ds(start, SUB), :], target.at[pl.ds(side * n, n)]))
+        copies.append((wet.at[pl.ds(start, SUB), :], wets.at[pl.ds(side * SUB, SUB), :]))
     copies = [pltpu.make_async_copy(a, b, done.at[i]) for i, (a, b) in enumerate(copies)]
     for copy in copies:
         copy.start()
     for copy in copies:
         copy.wait()
-    own[own.shape[0] - 1] = counts[...].astype(jnp.float32)
-    count, rows, cols = own.shape
-    lev = count // PLANES
-    _, lat_even, _ = parities()
-    flat = own.reshape(count * rows, cols)
+    flat = [ref.reshape(ref.shape[0] * SUB, cols) for ref in (trs, ecs, ncs, kds)]
     for out, upper in ((x, lat_even), (y, jnp.logical_not(lat_even))):
-        row = [jnp.where(upper, rows - 1 - m, m) for m in range(HALO)]
-
-        def plane(i, m):
-            return flat[pl.ds(i * lev * rows + row[m], lev, stride=rows), :]
+        side = jnp.where(upper, 1, 0)
+        sub = [jnp.where(upper, SUB - 1 - m, m) for m in range(HALO)]
+
+        def plane(i, p, m):
+            start = side * (flat[i].shape[0] // 2) + p * lev * SUB + sub[m]
+            return flat[i][pl.ds(start, lev, stride=SUB), :]
 
         for m in range(HALO):
-            for i in range(2):
-                out[AT_T + 2 * m + i] = plane(i, m)
-        for at, i, n in ((AT_E, 2, N_E), (AT_N, 3, N_N), (AT_K, 4, N_K)):
-            for m in range(n):
-                out[at + m] = plane(i, m)
+            for p in range(2):
+                out[AT_T + 2 * m + p] = plane(0, p, m)
+        for at, i, count in ((AT_E, 1, N_E), (AT_N, 2, N_N), (AT_K, 3, N_K)):
+            for m in range(count):
+                out[at + m] = plane(i, 0, m)
         out[AT_WET] = jnp.zeros((lev, cols), jnp.float32)
         for m in range(N_K):
-            out[AT_WET, pl.ds(m, 1), :] = own[count - 1, pl.ds(row[m], 1), :]
-
-
-def turn_kernel(own, x, y, t0, se, sn, kw, p0, p1, te, ee, ne, ke):
-    count, rows, cols = own.shape
-    lev = count // PLANES
-    planes = 2 * lev
-    tall = rows + 2 * SUB
+            out[AT_WET, pl.ds(m, 1), :] = wets[pl.ds(side * SUB + sub[m], 1), :].astype(jnp.float32)
+
+
+def fill_kernel(tr, ec, nc, kd, wet, te, ee, ne, ke, ce, wets, done):
+    rows, cols = wet.shape
+    lev = ec.shape[0]
+    copies = [(wet, wets)]
+    for source, target in ((kd, ke), (tr, te), (ec, ee), (nc, ne)):
+        copies.append((source, target.at[:, pl.ds(SUB, rows), :]))
+    copies = [pltpu.make_async_copy(a, b, done.at[i]) for i, (a, b) in enumerate(copies)]
+    for copy in copies:
+        copy.start()
+    zero = jnp.zeros((SUB, cols), jnp.float32)
+
+    def clear(p):
+        for start in (0, SUB + rows):
+            for target in (ee, ne, ke):
+                target[p, pl.ds(start, SUB), :] = zero
+            te[p, pl.ds(start, SUB), :] = zero
+            te[p + lev, pl.ds(start, SUB), :] = zero
+
+    loop(lev, clear)
+    for start in (0, SUB + rows):
+        ce[pl.ds(start, SUB), :] = zero
+    for copy in copies:
+        copy.wait()
+    ce[pl.ds(SUB, rows), :] = wets[...].astype(jnp.float32)
+
+    def dry(p):
+        for b in range(rows // SUB):
+            at = pl.ds(SUB + b * SUB, SUB)
+            wet_cells = wets[pl.ds(b * SUB, SUB), :] > p
+            ke[p, at, :] = jnp.where(wet_cells, ke[p, at, :], -1.0)
+
+    loop(lev, dry)
+
+
+def turn_kernel(te_in, ee_in, ne_in, ke_in, ce_in, x, y, te, ee, ne, ke, ce, t0, se, sn, kw, p0, p1, cw):
+    planes, tall, cols = te.shape
+    lev = ee.shape[0]
+    te, ee, ne, ke = (ref.reshape(ref.shape[0] * tall, cols) for ref in (te, ee, ne, ke))
     lon_even, lat_even, top = parities()
+    bottom = lax.axis_index("lat") == 0
     shape = (lev, cols)
     lane = lanes(shape)
     level = lax.broadcasted_iota(jnp.int32, shape, 0).astype(jnp.float32)
     zero = jnp.zeros((SUB, cols), jnp.float32)
-
-    def fill(p):
-        for e in range(tall // SUB):
-            halo = e == 0 or e == tall // SUB - 1
-            at = pl.ds(0 if halo else (e - 1) * SUB, SUB)
-
-            def put_tile(target, q, value):
-                target[pl.ds(pl.multiple_of(q * tall + e * SUB, SUB), SUB), :] = zero if halo else value
-
-            for i in range(2):
-                put_tile(te, p + i * lev, own[p + i * lev, at, :])
-            put_tile(ee, p, own[p + 2 * lev, at, :])
-            put_tile(ne, p, own[p + 3 * lev, at, :])
-            counts = own[count - 1, at, :]
-            put_tile(ke, p, jnp.where(counts > p.astype(jnp.float32), own[p + 4 * lev, at, :], -1.0))
-
-    loop(lev, fill)
-
     turn = jnp.where(top, -1.0, 1.0)
     cells = jnp.where(top, cols - 1 - lane, lane)
     faces = jnp.where(top, jnp.where(lane == cols - 1, cols - 1, cols - 2 - lane), lane)
     for north in (False, True):
         def piece(at):
             a, b = x[at], y[at]
-            return jnp.where(lat_even, a, b) if north else jnp.where(lat_even, b, a)
+            if north:
+                return jnp.where(lat_even, a, b)
+            return jnp.where(bottom, 0.0, jnp.where(lat_even, b, a))
 
         def put(target, row, value, first=0):
             target[pl.ds(first * tall + row, lev, stride=tall), :] = value
@@ -132,6 +158,9 @@
             counts = jnp.broadcast_to(wets[m : m + 1], shape)
             kappa = jnp.where(level < counts, piece(AT_K + m), -1.0)
             put(ke, at[m], turned(kappa, cells))
+        wets = turned(wets, cells)
+        for m in range(N_K):
+            ce[pl.ds(at[m], 1), :] = wets[m : m + 1]
         for m in range(N_E):
             value = turned(piece(AT_E + m), faces)
             put(ee, at[m], turn * value if north else value)
@@ -156,26 +185,23 @@
     for j in range(SUB):
         se[j, pl.ds(SUB - 1, 1), :] = se[j, pl.ds(SUB + cols - 1, 1), :]
 
+    parts = [ce[pl.ds(j, tall // SUB, stride=SUB), :] for j in range(SUB)]
+    cw[pl.ds(SUB, cols), :] = jnp.concatenate(parts * (cols // tall), 0).T
+
     left = lanes((SUB, cols)) < cols // 2
-
-    def edges(j):
-        for out, eastern in ((p0, lon_even), (p1, jnp.logical_not(lon_even))):
-            start = jnp.where(eastern, SUB + cols - HALO, SUB)
-            here = pl.ds(start, SUB)
-            faced = pl.ds(jnp.where(eastern, start, start - 1), SUB)
-            kappa = kw[j, here, :]
-            values = (
-                t0[j, here, :],
-                jnp.where(left, se[j, faced, :], sn[j, here, :]),
-                jnp.where(left, jnp.maximum(kappa, 0.0), jnp.where(kappa > 0, 1.0, 0.0)),
-            )
-            for i, value in enumerate(values):
-                out[pl.ds((KINDS * j + i) * HALO + 2, SUB), :] = value
-
-    for out in (p0, p1):
+    for out, eastern in ((p0, lon_even), (p1, jnp.logical_not(lon_even))):
         out[0:SUB, :] = zero
-        out[out.shape[0] - SUB : out.shape[0], :] = zero
-    loop(SUB, edges)
+        far = pl.ds(jnp.where(eastern, SUB + cols - HALO, SUB), SUB)
+        here = pl.ds(jnp.where(eastern, SUB + cols - FEW, SUB), SUB)
+        faced = pl.ds(jnp.where(eastern, SUB + cols - FEW, SUB - 1), SUB)
+        for j in range(SUB):
+            out[pl.ds(SPARE + j * HALO, SUB), :] = t0[j, far, :]
+        for j in range(SUB):
+            out[pl.ds(SPARE + AT_SPEED + j * FEW, SUB), :] = jnp.where(left, se[j, faced, :], sn[j, here, :])
+        for j in range(SUB // 2):
+            kappa = jnp.where(left, kw[j, here, :], kw[j + SUB // 2, here, :])
+            out[pl.ds(SPARE + AT_KAPPA + j * FEW, SUB), :] = jnp.maximum(kappa, 0.0)
+        out[pl.ds(SPARE + AT_COUNT, SUB), :] = cw[here, :]
 
 
 def coefficients(speed, kappa, other_kappa):
@@ -302,38 +328,36 @@
     lane = lanes(shape)
     sub = lax.broadcasted_iota(jnp.int32, shape, 0)
     left = lane < cols // 2
-    fold = top & ((lane & (height // SUB - 1)) == height // SUB - 1)
+    blocks = height // SUB
+    block = lane & (blocks - 1)
+    level = (lax.shift_right_logical(lane, blocks.bit_length() - 1)) & (planes // 2 - 1)
+    level = level.astype(jnp.float32)
+    fold = top & (block == blocks - 1)
     end = SUB + cols
 
     def halves(value):
         other = pltpu.roll(value, cols // 2, 1)
         return jnp.where(left, value, other), jnp.where(left, other, value)
 
-    def unpack(j):
-        for west in (False, True):
-            def piece(i):
-                at = pl.ds((KINDS * j + i) * HALO + (0 if west else 2), SUB)
-                a, b = r0[at, :], r1[at, :]
-                return jnp.where(lon_even, b, a) if west else jnp.where(lon_even, a, b)
-
-            here = pl.ds(0 if west else end, SUB)
-            t[0, j, here, :] = piece(0)
-            speed, northern = halves(piece(1))
-            kappa, wet = halves(piece(2))
+    for west in (False, True):
+        def piece(at, n):
+            rows_at = pl.ds(SPARE + at - (SUB - n if west else 0), SUB)
+            a, b = r0[rows_at, :], r1[rows_at, :]
+            return jnp.where(lon_even, b, a) if west else jnp.where(lon_even, a, b)
+
+        here = pl.ds(0 if west else end, SUB)
+        faced = here if west else pl.ds(end - 1, SUB)
+        kept = (sub == SUB - 1) & fold if west else (sub == 0) & jnp.logical_not(fold)
+        counts = piece(AT_COUNT, FEW)
+        for j in range(SUB):
+            t[0, j, here, :] = piece(j * HALO, HALO)
+            speed, northern = halves(piece(AT_SPEED + j * FEW, FEW))
             sn[j, here, :] = northern
-            kw[j, here, :] = jnp.where(wet > 0, kappa, -1.0)
-            if west:
-                kept = (sub == SUB - 1) & fold
-            else:
-                here = pl.ds(end - 1, SUB)
-                kept = (sub == 0) & jnp.logical_not(fold)
-            se[j, here, :] = jnp.where(kept, se[j, here, :], speed)
-
-    def unpack_two(i):
-        for k in range(2):
-            unpack(2 * i + k)
-
-    loop(SUB // 2, unpack_two)
+            se[j, faced, :] = jnp.where(kept, se[j, faced, :], speed)
+        for j in range(SUB // 2):
+            for row, kappa in zip((j, j + SUB // 2), halves(piece(AT_KAPPA + j * FEW, FEW))):
+                wet = level < take(counts, block + row * blocks)
+                kw[row, here, :] = jnp.where(wet, kappa, -1.0)
     for at in (0, end - 1):
         here = pl.ds(at, SUB)
         all_coefficients(
@@ -394,38 +418,42 @@
     for i in range(lon):
         for j in range(lat):
             if j % 2 != parity:
-                if j > 0:
-                    pairs.append((i * lat + j, i * lat + j - 1))
-            elif j + 1 < lat:
-                pairs.append((i * lat + j, i * lat + j + 1))
+                other = (i, j - 1) if j > 0 else (i ^ 1, j)
             else:
-                pairs.append((i * lat + j, (lon - 1 - i) * lat + j))
+                other = (i, j + 1) if j + 1 < lat else (lon - 1 - i, j)
+            pairs.append((i * lat + j, other[0] * lat + other[1]))
     return pairs
 
 
 def per_device(tracers, east_courant, north_courant, diffusivity, wet_levels):
     count, lev, rows, cols = tracers.shape
     planes, tall = count * lev, rows + 2 * SUB
-    assert planes * (tall // SUB) == cols and rows % SUB == 0
+    blocks = tall // SUB
+    assert planes * blocks == cols and rows % SUB == 0
+    assert blocks & (blocks - 1) == 0 and lev & (lev - 1) == 0 and blocks == lev == SUB
     sizes = (lax.axis_size("lon"), lax.axis_size("lat"))
     message = (MESSAGE, lev, cols)
-    stack = (PLANES * lev + 1, rows, cols)
-    own, x, y = call(
-        stage_kernel, [stack, message, message],
-        *(
-            pltpu.with_memory_space_constraint(v, pltpu.HBM)
-            for v in (tracers.reshape(planes, rows, cols), east_courant, north_courant, diffusivity, wet_levels)
-        ),
-        specs=[ANY] * 5,
-        scratch=[pltpu.VMEM((rows, cols), jnp.int32), pltpu.SemaphoreType.DMA((5,))],
+    given = [
+        pltpu.with_memory_space_constraint(v, pltpu.HBM)
+        for v in (tracers.reshape(planes, rows, cols), east_courant, north_courant, diffusivity, wet_levels)
+    ]
+    x, y = call(
+        edge_kernel, [message] * 2, *given, specs=[ANY] * 5,
+        scratch=[(2 * n, SUB, cols) for n in (planes, lev, lev, lev)]
+        + [pltpu.VMEM((2 * SUB, cols), jnp.int32), pltpu.SemaphoreType.DMA((10,))],
     )
     y = lax.ppermute(y, AXES, lat_swap(sizes, 1))
     x = lax.ppermute(x, AXES, lat_swap(sizes, 0))
+    extended = [(n, tall, cols) for n in (planes, lev, lev, lev)] + [(tall, cols)]
+    filled = call(
+        fill_kernel, extended, *given, specs=[ANY] * 5,
+        scratch=[pltpu.VMEM((rows, cols), jnp.int32), pltpu.SemaphoreType.DMA((5,))],
+    )
     wide = (SUB, cols + 2 * SUB, cols)
-    packed = (-(-(SUB * KINDS * HALO + SUB) // SUB) * SUB, cols)
-    t0, se, sn, kw, p0, p1 = call(
-        turn_kernel, [wide] * 4 + [packed] * 2, own, x, y,
-        scratch=[(n * tall, cols) for n in (planes, lev, lev, lev)],
+    packed = (COLUMNS, cols)
+    *_, t0, se, sn, kw, p0, p1 = call(
+        turn_kernel, extended + [wide] * 4 + [packed] * 2, *filled, x, y, alias={i: i for i in range(5)},
+        scratch=[wide[1:]],
     )
     r1 = lax.ppermute(p1, AXES, lon_swap(sizes, 1))
     r0 = lax.ppermute(p0, AXES, lon_swap(sizes, 0))

time: 18.9 us -> 16.1 us (0.85)
  starting transfers between devices: 6.49 us -> 4.58 us
  waiting for transfers between devices: 4.52 us -> 3.23 us
  Pallas kernels: 7.65 us -> 8.12 us
    ppermute x1, starting transfers between devices: 3.5 us -> 1.61 us  [per_device(): y = lax.ppermute(y, AXES, lat_swap(sizes, 1))]
    ppermute x1, waiting for transfers between devices: 3.68 us -> 1.8 us  [per_device(): y = lax.ppermute(y, AXES, lat_swap(sizes, 1))]
    ppermute x1, waiting for transfers between devices: 0.84 us -> 1.42 us  [per_device(): x = lax.ppermute(x, AXES, lat_swap(sizes, 0))]
    pallas_call x4 -> x5, Pallas kernels: 7.65 us -> 8.12 us  [call(): pl.pallas_call(kernel, out_shape=[jax.ShapeDtypeStruct(s, jnp.float32) fo...]
  transfers between devices with their start and end apart: 4 -> 4, of which waited for: 2 -> 2; matrix products, arithmetic and copies ran while one was open for 0% -> 0% of each run, Pallas kernels for 17% -> 27%
where the time goes in v3:
time: 16.1 us; the launch traced here: 16 us
  Pallas kernels  8.12 us (50%)
  starting transfers between devices  4.58 us (28%)
  waiting for transfers between devices  3.23 us (20%)
    pallas_call x5, Pallas kernels, call(): pl.pallas_call(kernel, out_shape=[jax.ShapeDtypeStruct(s, jnp.float32) fo...  8.12 us
    ppermute x1, starting transfers between devices, per_device(): r1 = lax.ppermute(p1, AXES, lon_swap(sizes, 1))  2.28 us
    ppermute x1, waiting for transfers between devices, per_device(): y = lax.ppermute(y, AXES, lat_swap(sizes, 1))  1.8 us
    ppermute x1, starting transfers between devices, per_device(): y = lax.ppermute(y, AXES, lat_swap(sizes, 1))  1.61 us
    ppermute x1, waiting for transfers between devices, per_device(): x = lax.ppermute(x, AXES, lat_swap(sizes, 0))  1.42 us
    ppermute x1, starting transfers between devices, per_device(): x = lax.ppermute(x, AXES, lat_swap(sizes, 0))  0.51 us
  transfers between devices with their start and end apart: 4, of which 2 were waited for; matrix products, arithmetic and copies ran while one was open for 0% of the time, Pallas kernels for 27%

profile of v3, /device:TPU:24, one launch (start us, length us, event | category | flops | bytes accessed | tf_op | source)
XLA Modules:
  0.0 16.0 jit_solution(9455760050351048685)
XLA Ops:
  0.0 1.1 %shard_map.56 = (f32[27,8,128]{2,1,0:T(8,128)S(1)}, f32[27,8,128]{2,1,0:T(8,128)S(1)}) custom-call(f32[16,48,128]{2,1,0:T(8,128)} %bitcast.2, f32[8,48,128]{2,1,0:T(8,128)} %ec.3, f32[8,48,128]{2,1,0:T(8,128)} %nc.3, f32[8,48,128]{2,1,0:T(8,128)} %kd.3, s32[48,128]{1,0:T(8,128)} %wet.3), custom_call_target="tpu_custom_call" | custom-call | flops 1048576 | bytes 1048576 | tf_op jit(solution)/shard_map/pallas_call | solution.py:394
  1.1 0.5 %collective-permute-start = (f32[27,8,128]{2,1,0:T(8,128)S(1)}, f32[27,8,128]{2,1,0:T(8,128)S(1)}, u32[]{:S(2)}, u32[]{:S(2)}) collective-permute-start(f32[27,8,128]{2,1,0:T(8,128)S(1)} %get-tuple-element.27), channel_id=1, source_target_pairs={{0,1},{1,0},{2,3},{3,2},{4,5},{5,4},{6,7},{7,6},{8,9},{9,8},{10,11... | collective-permute-start | bytes 331784 | tf_op jit(solution)/shard_map/ppermute | solution.py:446
  1.6 1.6 %collective-permute-start.1 = (f32[27,8,128]{2,1,0:T(8,128)S(1)}, f32[27,8,128]{2,1,0:T(8,128)S(1)}, u32[]{:S(2)}, u32[]{:S(2)}) collective-permute-start(f32[27,8,128]{2,1,0:T(8,128)S(1)} %get-tuple-element.28), channel_id=1, source_target_pairs={{0,4},{1,2},{2,1},{3,31},{4,0},{5,6},{6,5},{7,27},{8,12},{9,10},{1... | collective-permute-start | bytes 331784 | tf_op jit(solution)/shard_map/ppermute | solution.py:445
  3.2 1.3 %shard_map.55 = (f32[16,64,128]{2,1,0:T(8,128)S(1)}, f32[8,64,128]{2,1,0:T(8,128)S(1)}, f32[8,64,128]{2,1,0:T(8,128)S(1)}, f32[8,64,128]{2,1,0:T(8,128)S(1)}, f32[64,128]{1,0:T(8,128)S(1)}) custom-call(f32[16,48,128]{2,1,0:T(8,128)} %bitcast.3, f32[8,48,128]{2,1,0:T(8,128)} %ec.3, f32[8,48,128]{2,1,0:T(8,128)} %nc.3, f32[8,48,128]{2,1,0:T(8,128)} %kd.3, ...), custom_call_target="tpu_custom_call" | custom-call | flops 1048576 | bytes 1048576 | tf_op jit(solution)/shard_map/pallas_call | solution.py:394
  4.6 1.4 %collective-permute-done.x = f32[27,8,128]{2,1,0:T(8,128)S(1)} collective-permute-done((f32[27,8,128]{2,1,0:T(8,128)S(1)}, f32[27,8,128]{2,1,0:T(8,128)S(1)}, u32[]{:S(2)}, u32[]{:S(2)}) %collective-permute-start) | collective-permute-done | bytes 110624 | tf_op jit(solution)/shard_map/ppermute | solution.py:446
  6.0 1.8 %collective-permute-done.1.y = f32[27,8,128]{2,1,0:T(8,128)S(1)} collective-permute-done((f32[27,8,128]{2,1,0:T(8,128)S(1)}, f32[27,8,128]{2,1,0:T(8,128)S(1)}, u32[]{:S(2)}, u32[]{:S(2)}) %collective-permute-start.1) | collective-permute-done | bytes 110624 | tf_op jit(solution)/shard_map/ppermute | solution.py:445
  7.8 1.1 %shard_map.57 = (f32[16,64,128]{2,1,0:T(8,128)S(1)}, f32[8,64,128]{2,1,0:T(8,128)S(1)}, f32[8,64,128]{2,1,0:T(8,128)S(1)}, f32[8,64,128]{2,1,0:T(8,128)S(1)}, f3...) custom-call(f32[16,64,128]{2,1,0:T(8,128)S(1)} %get-tuple-element.22, ...), custom_call_target="tpu_custom_call", output_to_operand_aliasing={{0}: (0, {}), {1}: (1, {}), {2}: (2, {}), {3}: (3, {}), {4}... | custom-call | flops 1048576 | bytes 1048576 | tf_op jit(solution)/shard_map/pallas_call | solution.py:394
  8.9 0.2 %collective-permute-start.2 = (f32[120,128]{1,0:T(8,128)S(1)}, f32[120,128]{1,0:T(8,128)S(1)}, u32[]{:S(2)}, u32[]{:S(2)}) collective-permute-start(f32[120,128]{1,0:T(8,128)S(1)} %get-tuple-element.36), channel_id=1, source_target_pairs={{0,4},{1,5},{2,6},{3,7},{4,0},{5,1},{6,2},{7,3},{8,12},{9,13},{10,... | collective-permute-start | bytes 184328 | tf_op jit(solution)/shard_map/ppermute | solution.py:459
  9.0 2.3 %collective-permute-start.3 = (f32[120,128]{1,0:T(8,128)S(1)}, f32[120,128]{1,0:T(8,128)S(1)}, u32[]{:S(2)}, u32[]{:S(2)}) collective-permute-start(f32[120,128]{1,0:T(8,128)S(1)} %get-tuple-element.37), channel_id=1, source_target_pairs={{0,28},{1,29},{2,30},{3,31},{4,8},{5,9},{6,10},{7,11},{8,4},{9,5},... | collective-permute-start | bytes 184328 | tf_op jit(solution)/shard_map/ppermute | solution.py:458
  11.3 3.0 %shard_map.58 = (f32[4,8,144,128]{3,2,1,0:T(8,128)S(1)}, f32[6,8,144,128]{3,2,1,0:T(8,128)S(1)}, f32[3,144,128]{2,1,0:T(8,128)S(1)}) custom-call(f32[8,144,128]{2,1,0:T(8,128)S(1)} %get-tuple-element.29.t0, f32[8,144,128]{2,1,0:T(8,128)S(1)} %get-tuple-element.30.se.se_in, f32[8,144,128]{2,1,0:T(8,128)S(1)} %get-tuple-element.31.sn.sn_in, ...), custom_call_target="tpu_custom_call" | custom-call | flops 1048576 | bytes 1048576 | tf_op jit(solution)/shard_map/pallas_call | solution.py:394
  14.3 0.0 collective-permute-done.2.r0
  14.3 0.0 collective-permute-done.3.r1
  14.3 1.6 %shard_map.59 = (f32[16,48,128]{2,1,0:T(8,128)}, f32[4,8,144,128]{3,2,1,0:T(8,128)S(1)}, f32[6,8,144,128]{3,2,1,0:T(8,128)S(1)}, f32[8,144,128]{2,1,0:T(8,128)S(...) custom-call(f32[4,8,144,128]{3,2,1,0:T(8,128)S(1)} %get-tuple-elemen, ...), custom_call_target="tpu_custom_call", output_to_operand_aliasing={{1}: (0, {}), {2}: (1, {}), {3}: (2, {}), {4}: (3, {}), {5}... | custom-call | flops 1048576 | bytes 1048576 | tf_op jit(solution)/shard_map/pallas_call | solution.py:394
Async XLA Ops:
  1.1 4.9 %collective-permute-start = (f32[27,8,128]{2,1,0:T(8,128)S(1)}, f32[27,8,128]{2,1,0:T(8,128)S(1)}, u32[]{:S(2)}, u32[]{:S(2)}) collective-permute-start(f32[27,8,128]{2,1,0:T(8,128)S(1)} %get-tuple-element.27), channel_id=1, source_target_pairs={{0,1},{1,0},{2,3},{3,2},{4,5},{5,4},{6,7},{7,6},{8,9},{9,8},{10,11... | collective-permute-start | bytes 331784 | tf_op jit(solution)/shard_map/ppermute | solution.py:446
  1.6 6.2 %collective-permute-start.1 = (f32[27,8,128]{2,1,0:T(8,128)S(1)}, f32[27,8,128]{2,1,0:T(8,128)S(1)}, u32[]{:S(2)}, u32[]{:S(2)}) collective-permute-start(f32[27,8,128]{2,1,0:T(8,128)S(1)} %get-tuple-element.28), channel_id=1, source_target_pairs={{0,4},{1,2},{2,1},{3,31},{4,0},{5,6},{6,5},{7,27},{8,12},{9,10},{1... | collective-permute-start | bytes 331784 | tf_op jit(solution)/shard_map/ppermute | solution.py:445
  8.9 5.5 %collective-permute-start.2 = (f32[120,128]{1,0:T(8,128)S(1)}, f32[120,128]{1,0:T(8,128)S(1)}, u32[]{:S(2)}, u32[]{:S(2)}) collective-permute-start(f32[120,128]{1,0:T(8,128)S(1)} %get-tuple-element.36), channel_id=1, source_target_pairs={{0,4},{1,5},{2,6},{3,7},{4,0},{5,1},{6,2},{7,3},{8,12},{9,13},{10,... | collective-permute-start | bytes 184328 | tf_op jit(solution)/shard_map/ppermute | solution.py:459
  9.0 5.3 %collective-permute-start.3 = (f32[120,128]{1,0:T(8,128)S(1)}, f32[120,128]{1,0:T(8,128)S(1)}, u32[]{:S(2)}, u32[]{:S(2)}) collective-permute-start(f32[120,128]{1,0:T(8,128)S(1)} %get-tuple-element.37), channel_id=1, source_target_pairs={{0,28},{1,29},{2,30},{3,31},{4,8},{5,9},{6,10},{7,11},{8,4},{9,5},... | collective-permute-start | bytes 184328 | tf_op jit(solution)/shard_map/ppermute | solution.py:458

commit v4 on v3

--- a/solution.py
+++ b/solution.py
@@ -123,7 +123,7 @@
     loop(lev, dry)
 
 
-def turn_kernel(te_in, ee_in, ne_in, ke_in, ce_in, x, y, te, ee, ne, ke, ce, t0, se, sn, kw, p0, p1, cw):
+def turn_kernel(te_in, ee_in, ne_in, ke_in, ce_in, x, y, te, ee, ne, ke, ce, t0, sp, kh, p0, p1, cw):
     planes, tall, cols = te.shape
     lev = ee.shape[0]
     te, ee, ne, ke = (ref.reshape(ref.shape[0] * tall, cols) for ref in (te, ee, ne, ke))
@@ -174,16 +174,22 @@
             for m in range(N_N):
                 put(ne, at[m], piece(AT_N + m))
 
+    def rows_of(source, j, n):
+        return [source[pl.ds(p * tall + j, tall // SUB, stride=SUB), :] for p in range(n)]
+
     def transpose(i):
-        for j in (2 * i, 2 * i + 1):
-            for source, target, n in ((te, t0, planes), (ee, se, lev), (ne, sn, lev), (ke, kw, lev)):
-                parts = [source[pl.ds(p * tall + j, tall // SUB, stride=SUB), :] for p in range(n)]
-                matrix = jnp.concatenate(parts * (planes // n), 0)
-                target[j, pl.ds(SUB, cols), :] = matrix.T
-
-    loop(SUB // 2, transpose)
+        for k in range(SUB // 4):
+            j = i * (SUB // 4) + k
+            for row in (2 * j, 2 * j + 1):
+                t0[row, pl.ds(SUB, cols), :] = jnp.concatenate(rows_of(te, row, planes), 0).T
+                both = rows_of(ee, row, lev) + rows_of(ne, row, lev)
+                sp[row, pl.ds(SUB, cols), :] = jnp.concatenate(both, 0).T
+            both = rows_of(ke, j, lev) + rows_of(ke, j + SUB // 2, lev)
+            kh[j, pl.ds(SUB, cols), :] = jnp.concatenate(both, 0).T
+
+    loop(2, transpose)
     for j in range(SUB):
-        se[j, pl.ds(SUB - 1, 1), :] = se[j, pl.ds(SUB + cols - 1, 1), :]
+        sp[j, pl.ds(SUB - 1, 1), :] = sp[j, pl.ds(SUB + cols - 1, 1), :]
 
     parts = [ce[pl.ds(j, tall // SUB, stride=SUB), :] for j in range(SUB)]
     cw[pl.ds(SUB, cols), :] = jnp.concatenate(parts * (cols // tall), 0).T
@@ -197,10 +203,9 @@
         for j in range(SUB):
             out[pl.ds(SPARE + j * HALO, SUB), :] = t0[j, far, :]
         for j in range(SUB):
-            out[pl.ds(SPARE + AT_SPEED + j * FEW, SUB), :] = jnp.where(left, se[j, faced, :], sn[j, here, :])
+            out[pl.ds(SPARE + AT_SPEED + j * FEW, SUB), :] = jnp.where(left, sp[j, faced, :], sp[j, here, :])
         for j in range(SUB // 2):
-            kappa = jnp.where(left, kw[j, here, :], kw[j + SUB // 2, here, :])
-            out[pl.ds(SPARE + AT_KAPPA + j * FEW, SUB), :] = jnp.maximum(kappa, 0.0)
+            out[pl.ds(SPARE + AT_KAPPA + j * FEW, SUB), :] = jnp.maximum(kh[j, here, :], 0.0)
         out[pl.ds(SPARE + AT_COUNT, SUB), :] = cw[here, :]
 
 
@@ -267,23 +272,47 @@
     return before + [later_block(t[s, j, here, :]) for j in (0, 1)]
 
 
-def interior_kernel(t0, se, sn, kw, t, face, low, fluxes, beside):
+def interior_kernel(t0, sp, kh, t, face, low, se, sn, kw, fluxes, beside):
     cols = t.shape[3]
     passes = cols // SUB // PAIR
 
     def start(g):
         return pl.multiple_of(SUB + g * SUB, SUB)
+
+    lane = lanes((SUB, cols))
+    half = cols // 2
+    left = lane < half
+    within = lane & (half - 1)
+    before = half + ((within - 1) & (half - 1))
+    after = (within + 1) & (half - 1)
+
+    def halves(value):
+        other = pltpu.roll(value, half, 1)
+        return jnp.where(left, value, other), jnp.where(left, other, value)
 
     def turn_coefficients(b):
         values = []
         for k in range(PAIR):
             here = pl.ds(start(b * PAIR + k), SUB)
             values.append((
-                earlier_block(kw[SUB - 1, here, :]),
-                later_block(kw[0, here, :]),
-                earlier_block(sn[SUB - 1, here, :]),
+                take(kh[SUB // 2 - 1, here, :], before), take(kh[0, here, :], after), take(sp[SUB - 1, here, :], before)
             ))
         return values
+
+    def spread(b):
+        values = []
+        for k in range(PAIR):
+            here = pl.ds(start(b * PAIR + k), SUB)
+            speeds = [halves(sp[j, here, :]) for j in range(SUB)]
+            values.append((here, speeds, [halves(kh[j, here, :]) for j in range(SUB // 2)]))
+        return values
+
+    def put_spread(values):
+        for here, speeds, kappas in values:
+            for j, (eastern, northern) in enumerate(speeds):
+                se[j, here, :], sn[j, here, :] = eastern, northern
+            for j, (lower, upper) in enumerate(kappas):
+                kw[j, here, :], kw[j + SUB // 2, here, :] = lower, upper
 
     def turn_cells(n):
         s = lax.div(n, passes)
@@ -294,18 +323,25 @@
             for i, value in enumerate(group):
                 beside[k, i] = value
 
-    def prepare(b):
+    def prepare(n):
+        b = jnp.maximum(n - 1, 0)
         turned = [[beside[k, i] for i in range(3)] for k in range(PAIR)]
-        later = turn_coefficients(jnp.minimum(b + 1, passes - 1))
+        following = jnp.minimum(n, passes - 1)
+        later = turn_coefficients(following)
+        values = spread(following)
         for k in range(PAIR):
+            if k == PAIR - 1:
+                put_spread(values)
             at = start(b * PAIR + k)
             for j in range(SUB):
                 t[0, j, pl.ds(at, SUB), :] = t0[j, pl.ds(at, SUB), :]
             all_coefficients(se, sn, kw, face, low, at, *turned[k])
         keep(later)
 
-    keep(turn_coefficients(0))
-    loop(passes, prepare)
+    wrapped = [halves(sp[j, 0:SUB, :])[0] for j in range(SUB)]
+    loop(passes + 1, prepare)
+    for j in range(SUB):
+        se[j, 0:SUB, :] = wrapped[j]
     keep(turn_cells(0))
 
     def step(n):
@@ -451,14 +487,14 @@
     )
     wide = (SUB, cols + 2 * SUB, cols)
     packed = (COLUMNS, cols)
-    *_, t0, se, sn, kw, p0, p1 = call(
-        turn_kernel, extended + [wide] * 4 + [packed] * 2, *filled, x, y, alias={i: i for i in range(5)},
+    *_, t0, sp, kh, p0, p1 = call(
+        turn_kernel, extended + [wide] * 2 + [(SUB // 2,) + wide[1:]] + [packed] * 2, *filled, x, y, alias={i: i for i in range(5)},
         scratch=[wide[1:]],
     )
     r1 = lax.ppermute(p1, AXES, lon_swap(sizes, 1))
     r0 = lax.ppermute(p0, AXES, lon_swap(sizes, 0))
-    t, face, low = call(
-        interior_kernel, [(STEPS + 1,) + wide, (6,) + wide, (3,) + wide[1:]], t0, se, sn, kw,
+    t, face, low, se, sn, kw = call(
+        interior_kernel, [(STEPS + 1,) + wide, (6,) + wide, (3,) + wide[1:]] + [wide] * 3, t0, sp, kh,
         scratch=[wide, (PAIR, 4, SUB, cols)],
     )
     out, *_ = call(

time: 16.1 us -> 16.2 us (level)
  transfers between devices with their start and end apart: 4 -> 4, of which waited for: 2 -> 2; matrix products, arithmetic and copies ran while one was open for 0% -> 0% of each run, Pallas kernels for 27% -> 29%
where the time goes in v4:
time: 16.2 us; the launch traced here: 16 us
  Pallas kernels  8.18 us (50%)
  starting transfers between devices  4.58 us (28%)
  waiting for transfers between devices  3.23 us (20%)
    pallas_call x5, Pallas kernels, call(): pl.pallas_call(kernel, out_shape=[jax.ShapeDtypeStruct(s, jnp.float32) fo...  8.18 us
    ppermute x1, starting transfers between devices, per_device(): r1 = lax.ppermute(p1, AXES, lon_swap(sizes, 1))  2.28 us
    ppermute x1, waiting for transfers between devices, per_device(): y = lax.ppermute(y, AXES, lat_swap(sizes, 1))  1.8 us
    ppermute x1, starting transfers between devices, per_device(): y = lax.ppermute(y, AXES, lat_swap(sizes, 1))  1.61 us
    ppermute x1, waiting for transfers between devices, per_device(): x = lax.ppermute(x, AXES, lat_swap(sizes, 0))  1.42 us
    ppermute x1, starting transfers between devices, per_device(): x = lax.ppermute(x, AXES, lat_swap(sizes, 0))  0.51 us
  transfers between devices with their start and end apart: 4, of which 2 were waited for; matrix products, arithmetic and copies ran while one was open for 0% of the time, Pallas kernels for 29%

profile of v4, /device:TPU:24, one launch (start us, length us, event | category | flops | bytes accessed | tf_op | source)
XLA Modules:
  0.0 16.0 jit_solution(15736968927616727267)
XLA Ops:
  0.0 1.1 %shard_map.56 = (f32[27,8,128]{2,1,0:T(8,128)S(1)}, f32[27,8,128]{2,1,0:T(8,128)S(1)}) custom-call(f32[16,48,128]{2,1,0:T(8,128)} %bitcast.2, f32[8,48,128]{2,1,0:T(8,128)} %ec.3, f32[8,48,128]{2,1,0:T(8,128)} %nc.3, f32[8,48,128]{2,1,0:T(8,128)} %kd.3, s32[48,128]{1,0:T(8,128)} %wet.3), custom_call_target="tpu_custom_call" | custom-call | flops 1048576 | bytes 1048576 | tf_op jit(solution)/shard_map/pallas_call | solution.py:430
  1.1 0.5 %collective-permute-start = (f32[27,8,128]{2,1,0:T(8,128)S(1)}, f32[27,8,128]{2,1,0:T(8,128)S(1)}, u32[]{:S(2)}, u32[]{:S(2)}) collective-permute-start(f32[27,8,128]{2,1,0:T(8,128)S(1)} %get-tuple-element.29), channel_id=1, source_target_pairs={{0,1},{1,0},{2,3},{3,2},{4,5},{5,4},{6,7},{7,6},{8,9},{9,8},{10,11... | collective-permute-start | bytes 331784 | tf_op jit(solution)/shard_map/ppermute | solution.py:482
  1.6 1.6 %collective-permute-start.1 = (f32[27,8,128]{2,1,0:T(8,128)S(1)}, f32[27,8,128]{2,1,0:T(8,128)S(1)}, u32[]{:S(2)}, u32[]{:S(2)}) collective-permute-start(f32[27,8,128]{2,1,0:T(8,128)S(1)} %get-tuple-element.30), channel_id=1, source_target_pairs={{0,4},{1,2},{2,1},{3,31},{4,0},{5,6},{6,5},{7,27},{8,12},{9,10},{1... | collective-permute-start | bytes 331784 | tf_op jit(solution)/shard_map/ppermute | solution.py:481
  3.2 1.3 %shard_map.55 = (f32[16,64,128]{2,1,0:T(8,128)S(1)}, f32[8,64,128]{2,1,0:T(8,128)S(1)}, f32[8,64,128]{2,1,0:T(8,128)S(1)}, f32[8,64,128]{2,1,0:T(8,128)S(1)}, f32[64,128]{1,0:T(8,128)S(1)}) custom-call(f32[16,48,128]{2,1,0:T(8,128)} %bitcast.3, f32[8,48,128]{2,1,0:T(8,128)} %ec.3, f32[8,48,128]{2,1,0:T(8,128)} %nc.3, f32[8,48,128]{2,1,0:T(8,128)} %kd.3, ...), custom_call_target="tpu_custom_call" | custom-call | flops 1048576 | bytes 1048576 | tf_op jit(solution)/shard_map/pallas_call | solution.py:430
  4.6 1.4 %collective-permute-done.x = f32[27,8,128]{2,1,0:T(8,128)S(1)} collective-permute-done((f32[27,8,128]{2,1,0:T(8,128)S(1)}, f32[27,8,128]{2,1,0:T(8,128)S(1)}, u32[]{:S(2)}, u32[]{:S(2)}) %collective-permute-start) | collective-permute-done | bytes 110624 | tf_op jit(solution)/shard_map/ppermute | solution.py:482
  6.0 1.8 %collective-permute-done.1.y = f32[27,8,128]{2,1,0:T(8,128)S(1)} collective-permute-done((f32[27,8,128]{2,1,0:T(8,128)S(1)}, f32[27,8,128]{2,1,0:T(8,128)S(1)}, u32[]{:S(2)}, u32[]{:S(2)}) %collective-permute-start.1) | collective-permute-done | bytes 110624 | tf_op jit(solution)/shard_map/ppermute | solution.py:481
  7.8 0.7 %shard_map.57 = (f32[16,64,128]{2,1,0:T(8,128)S(1)}, f32[8,64,128]{2,1,0:T(8,128)S(1)}, f32[8,64,128]{2,1,0:T(8,128)S(1)}, f32[8,64,128]{2,1,0:T(8,128)S(1)}, f3...) custom-call(f32[16,64,128]{2,1,0:T(8,128)S(1)} %get-tuple-element.24, ...), custom_call_target="tpu_custom_call", output_to_operand_aliasing={{0}: (0, {}), {1}: (1, {}), {2}: (2, {}), {3}: (3, {}), {4}... | custom-call | flops 1048576 | bytes 1048576 | tf_op jit(solution)/shard_map/pallas_call | solution.py:430
  8.5 0.2 %collective-permute-start.2 = (f32[120,128]{1,0:T(8,128)S(1)}, f32[120,128]{1,0:T(8,128)S(1)}, u32[]{:S(2)}, u32[]{:S(2)}) collective-permute-start(f32[120,128]{1,0:T(8,128)S(1)} %get-tuple-element.40), channel_id=1, source_target_pairs={{0,4},{1,5},{2,6},{3,7},{4,0},{5,1},{6,2},{7,3},{8,12},{9,13},{10,... | collective-permute-start | bytes 184328 | tf_op jit(solution)/shard_map/ppermute | solution.py:495
  8.7 2.3 %collective-permute-start.3 = (f32[120,128]{1,0:T(8,128)S(1)}, f32[120,128]{1,0:T(8,128)S(1)}, u32[]{:S(2)}, u32[]{:S(2)}) collective-permute-start(f32[120,128]{1,0:T(8,128)S(1)} %get-tuple-element.41), channel_id=1, source_target_pairs={{0,28},{1,29},{2,30},{3,31},{4,8},{5,9},{6,10},{7,11},{8,4},{9,5},... | collective-permute-start | bytes 184328 | tf_op jit(solution)/shard_map/ppermute | solution.py:494
  11.0 3.4 %shard_map.58 = (f32[4,8,144,128]{3,2,1,0:T(8,128)S(1)}, f32[6,8,144,128]{3,2,1,0:T(8,128)S(1)}, f32[3,144,128]{2,1,0:T(8,128)S(1)}, f32[8,144,128]{2,1,0:T(8,12...) custom-call(f32[8,144,128]{2,1,0:T(8,128)S(1)} %get-tuple-element.31.t0, ...), custom_call_target="tpu_custom_call" | custom-call | flops 1048576 | bytes 1048576 | tf_op jit(solution)/shard_map/pallas_call | solution.py:430
  14.4 0.0 collective-permute-done.2.r0
  14.4 0.0 collective-permute-done.3.r1
  14.4 1.6 %shard_map.59 = (f32[16,48,128]{2,1,0:T(8,128)}, f32[4,8,144,128]{3,2,1,0:T(8,128)S(1)}, f32[6,8,144,128]{3,2,1,0:T(8,128)S(1)}, f32[8,144,128]{2,1,0:T(8,128)S(...) custom-call(f32[4,8,144,128]{3,2,1,0:T(8,128)S(1)} %get-tuple-elemen, ...), custom_call_target="tpu_custom_call", output_to_operand_aliasing={{1}: (0, {}), {2}: (1, {}), {3}: (2, {}), {4}: (3, {}), {5}... | custom-call | flops 1048576 | bytes 1048576 | tf_op jit(solution)/shard_map/pallas_call | solution.py:430
Async XLA Ops:
  1.1 4.9 %collective-permute-start = (f32[27,8,128]{2,1,0:T(8,128)S(1)}, f32[27,8,128]{2,1,0:T(8,128)S(1)}, u32[]{:S(2)}, u32[]{:S(2)}) collective-permute-start(f32[27,8,128]{2,1,0:T(8,128)S(1)} %get-tuple-element.29), channel_id=1, source_target_pairs={{0,1},{1,0},{2,3},{3,2},{4,5},{5,4},{6,7},{7,6},{8,9},{9,8},{10,11... | collective-permute-start | bytes 331784 | tf_op jit(solution)/shard_map/ppermute | solution.py:482
  1.6 6.2 %collective-permute-start.1 = (f32[27,8,128]{2,1,0:T(8,128)S(1)}, f32[27,8,128]{2,1,0:T(8,128)S(1)}, u32[]{:S(2)}, u32[]{:S(2)}) collective-permute-start(f32[27,8,128]{2,1,0:T(8,128)S(1)} %get-tuple-element.30), channel_id=1, source_target_pairs={{0,4},{1,2},{2,1},{3,31},{4,0},{5,6},{6,5},{7,27},{8,12},{9,10},{1... | collective-permute-start | bytes 331784 | tf_op jit(solution)/shard_map/ppermute | solution.py:481
  8.5 5.8 %collective-permute-start.2 = (f32[120,128]{1,0:T(8,128)S(1)}, f32[120,128]{1,0:T(8,128)S(1)}, u32[]{:S(2)}, u32[]{:S(2)}) collective-permute-start(f32[120,128]{1,0:T(8,128)S(1)} %get-tuple-element.40), channel_id=1, source_target_pairs={{0,4},{1,5},{2,6},{3,7},{4,0},{5,1},{6,2},{7,3},{8,12},{9,13},{10,... | collective-permute-start | bytes 184328 | tf_op jit(solution)/shard_map/ppermute | solution.py:495
  8.7 5.7 %collective-permute-start.3 = (f32[120,128]{1,0:T(8,128)S(1)}, f32[120,128]{1,0:T(8,128)S(1)}, u32[]{:S(2)}, u32[]{:S(2)}) collective-permute-start(f32[120,128]{1,0:T(8,128)S(1)} %get-tuple-element.41), channel_id=1, source_target_pairs={{0,28},{1,29},{2,30},{3,31},{4,8},{5,9},{6,10},{7,11},{8,4},{9,5},... | collective-permute-start | bytes 184328 | tf_op jit(solution)/shard_map/ppermute | solution.py:494

commit v5 on v4

--- a/solution.py
+++ b/solution.py
@@ -408,17 +408,18 @@
         for at, rows_turned in zip((west, east), beside):
             advance(t, face, low, s, at, rows_turned)
 
-    loop(STEPS, step)
+    for s in range(STEPS):
+        step(s)
 
     def transpose(i):
         n = height // SUB
-        for k in range(4):
-            j = 4 * i + k
+        for k in range(SUB):
+            j = SUB * i + k
             matrix = t[STEPS, j, pl.ds(SUB, cols), :].T
             for p in range(planes):
                 tall[pl.ds(p * height + j, n, stride=SUB), :] = matrix[p * n : (p + 1) * n]
 
-    loop(SUB // 4, transpose)
+    transpose(0)
     copy = pltpu.make_async_copy(
         tall.reshape(planes, height, cols).at[:, pl.ds(SUB, rows), :], out, done
     )

time: 16.2 us -> 16 us (0.988)
  Pallas kernels: 8.18 us -> 7.99 us
    pallas_call x5, Pallas kernels: 8.18 us -> 7.99 us  [call(): pl.pallas_call(kernel, out_shape=[jax.ShapeDtypeStruct(s, jnp.float32) fo...]
  transfers between devices with their start and end apart: 4 -> 4, of which waited for: 2 -> 2; matrix products, arithmetic and copies ran while one was open for 0% -> 0% of each run, Pallas kernels for 29% -> 30%
where the time goes in v5:
time: 16 us; the launch traced here: 15.8 us
  Pallas kernels  7.99 us (50%)
  starting transfers between devices  4.58 us (29%)
  waiting for transfers between devices  3.23 us (20%)
    pallas_call x5, Pallas kernels, call(): pl.pallas_call(kernel, out_shape=[jax.ShapeDtypeStruct(s, jnp.float32) fo...  7.99 us
    ppermute x1, starting transfers between devices, per_device(): r1 = lax.ppermute(p1, AXES, lon_swap(sizes, 1))  2.28 us
    ppermute x1, waiting for transfers between devices, per_device(): y = lax.ppermute(y, AXES, lat_swap(sizes, 1))  1.8 us
    ppermute x1, starting transfers between devices, per_device(): y = lax.ppermute(y, AXES, lat_swap(sizes, 1))  1.61 us
    ppermute x1, waiting for transfers between devices, per_device(): x = lax.ppermute(x, AXES, lat_swap(sizes, 0))  1.42 us
    ppermute x1, starting transfers between devices, per_device(): x = lax.ppermute(x, AXES, lat_swap(sizes, 0))  0.51 us
  transfers between devices with their start and end apart: 4, of which 2 were waited for; matrix products, arithmetic and copies ran while one was open for 0% of the time, Pallas kernels for 30%

profile of v5, /device:TPU:24, one launch (start us, length us, event | category | flops | bytes accessed | tf_op | source)
XLA Modules:
  0.0 15.8 jit_solution(9703623147272760380)
XLA Ops:
  0.0 1.1 %shard_map.56 = (f32[27,8,128]{2,1,0:T(8,128)S(1)}, f32[27,8,128]{2,1,0:T(8,128)S(1)}) custom-call(f32[16,48,128]{2,1,0:T(8,128)} %bitcast.2, f32[8,48,128]{2,1,0:T(8,128)} %ec.3, f32[8,48,128]{2,1,0:T(8,128)} %nc.3, f32[8,48,128]{2,1,0:T(8,128)} %kd.3, s32[48,128]{1,0:T(8,128)} %wet.3), custom_call_target="tpu_custom_call" | custom-call | flops 1048576 | bytes 1048576 | tf_op jit(solution)/shard_map/pallas_call | solution.py:431
  1.1 0.5 %collective-permute-start = (f32[27,8,128]{2,1,0:T(8,128)S(1)}, f32[27,8,128]{2,1,0:T(8,128)S(1)}, u32[]{:S(2)}, u32[]{:S(2)}) collective-permute-start(f32[27,8,128]{2,1,0:T(8,128)S(1)} %get-tuple-element.29), channel_id=1, source_target_pairs={{0,1},{1,0},{2,3},{3,2},{4,5},{5,4},{6,7},{7,6},{8,9},{9,8},{10,11... | collective-permute-start | bytes 331784 | tf_op jit(solution)/shard_map/ppermute | solution.py:483
  1.6 1.6 %collective-permute-start.1 = (f32[27,8,128]{2,1,0:T(8,128)S(1)}, f32[27,8,128]{2,1,0:T(8,128)S(1)}, u32[]{:S(2)}, u32[]{:S(2)}) collective-permute-start(f32[27,8,128]{2,1,0:T(8,128)S(1)} %get-tuple-element.30), channel_id=1, source_target_pairs={{0,4},{1,2},{2,1},{3,31},{4,0},{5,6},{6,5},{7,27},{8,12},{9,10},{1... | collective-permute-start | bytes 331784 | tf_op jit(solution)/shard_map/ppermute | solution.py:482
  3.2 1.3 %shard_map.55 = (f32[16,64,128]{2,1,0:T(8,128)S(1)}, f32[8,64,128]{2,1,0:T(8,128)S(1)}, f32[8,64,128]{2,1,0:T(8,128)S(1)}, f32[8,64,128]{2,1,0:T(8,128)S(1)}, f32[64,128]{1,0:T(8,128)S(1)}) custom-call(f32[16,48,128]{2,1,0:T(8,128)} %bitcast.3, f32[8,48,128]{2,1,0:T(8,128)} %ec.3, f32[8,48,128]{2,1,0:T(8,128)} %nc.3, f32[8,48,128]{2,1,0:T(8,128)} %kd.3, ...), custom_call_target="tpu_custom_call" | custom-call | flops 1048576 | bytes 1048576 | tf_op jit(solution)/shard_map/pallas_call | solution.py:431
  4.6 1.4 %collective-permute-done.x = f32[27,8,128]{2,1,0:T(8,128)S(1)} collective-permute-done((f32[27,8,128]{2,1,0:T(8,128)S(1)}, f32[27,8,128]{2,1,0:T(8,128)S(1)}, u32[]{:S(2)}, u32[]{:S(2)}) %collective-permute-start) | collective-permute-done | bytes 110624 | tf_op jit(solution)/shard_map/ppermute | solution.py:483
  6.0 1.8 %collective-permute-done.1.y = f32[27,8,128]{2,1,0:T(8,128)S(1)} collective-permute-done((f32[27,8,128]{2,1,0:T(8,128)S(1)}, f32[27,8,128]{2,1,0:T(8,128)S(1)}, u32[]{:S(2)}, u32[]{:S(2)}) %collective-permute-start.1) | collective-permute-done | bytes 110624 | tf_op jit(solution)/shard_map/ppermute | solution.py:482
  7.8 0.7 %shard_map.57 = (f32[16,64,128]{2,1,0:T(8,128)S(1)}, f32[8,64,128]{2,1,0:T(8,128)S(1)}, f32[8,64,128]{2,1,0:T(8,128)S(1)}, f32[8,64,128]{2,1,0:T(8,128)S(1)}, f3...) custom-call(f32[16,64,128]{2,1,0:T(8,128)S(1)} %get-tuple-element.24, ...), custom_call_target="tpu_custom_call", output_to_operand_aliasing={{0}: (0, {}), {1}: (1, {}), {2}: (2, {}), {3}: (3, {}), {4}... | custom-call | flops 1048576 | bytes 1048576 | tf_op jit(solution)/shard_map/pallas_call | solution.py:431
  8.5 0.2 %collective-permute-start.2 = (f32[120,128]{1,0:T(8,128)S(1)}, f32[120,128]{1,0:T(8,128)S(1)}, u32[]{:S(2)}, u32[]{:S(2)}) collective-permute-start(f32[120,128]{1,0:T(8,128)S(1)} %get-tuple-element.40), channel_id=1, source_target_pairs={{0,4},{1,5},{2,6},{3,7},{4,0},{5,1},{6,2},{7,3},{8,12},{9,13},{10,... | collective-permute-start | bytes 184328 | tf_op jit(solution)/shard_map/ppermute | solution.py:496
  8.7 2.3 %collective-permute-start.3 = (f32[120,128]{1,0:T(8,128)S(1)}, f32[120,128]{1,0:T(8,128)S(1)}, u32[]{:S(2)}, u32[]{:S(2)}) collective-permute-start(f32[120,128]{1,0:T(8,128)S(1)} %get-tuple-element.41), channel_id=1, source_target_pairs={{0,28},{1,29},{2,30},{3,31},{4,8},{5,9},{6,10},{7,11},{8,4},{9,5},... | collective-permute-start | bytes 184328 | tf_op jit(solution)/shard_map/ppermute | solution.py:495
  11.0 3.4 %shard_map.58 = (f32[4,8,144,128]{3,2,1,0:T(8,128)S(1)}, f32[6,8,144,128]{3,2,1,0:T(8,128)S(1)}, f32[3,144,128]{2,1,0:T(8,128)S(1)}, f32[8,144,128]{2,1,0:T(8,12...) custom-call(f32[8,144,128]{2,1,0:T(8,128)S(1)} %get-tuple-element.31.t0, ...), custom_call_target="tpu_custom_call" | custom-call | flops 1048576 | bytes 1048576 | tf_op jit(solution)/shard_map/pallas_call | solution.py:431
  14.4 0.0 collective-permute-done.2.r0
  14.4 0.0 collective-permute-done.3.r1
  14.4 1.4 %shard_map.59 = (f32[16,48,128]{2,1,0:T(8,128)}, f32[4,8,144,128]{3,2,1,0:T(8,128)S(1)}, f32[6,8,144,128]{3,2,1,0:T(8,128)S(1)}, f32[8,144,128]{2,1,0:T(8,128)S(...) custom-call(f32[4,8,144,128]{3,2,1,0:T(8,128)S(1)} %get-tuple-elemen, ...), custom_call_target="tpu_custom_call", output_to_operand_aliasing={{1}: (0, {}), {2}: (1, {}), {3}: (2, {}), {4}: (3, {}), {5}... | custom-call | flops 1048576 | bytes 1048576 | tf_op jit(solution)/shard_map/pallas_call | solution.py:431
Async XLA Ops:
  1.1 4.9 %collective-permute-start = (f32[27,8,128]{2,1,0:T(8,128)S(1)}, f32[27,8,128]{2,1,0:T(8,128)S(1)}, u32[]{:S(2)}, u32[]{:S(2)}) collective-permute-start(f32[27,8,128]{2,1,0:T(8,128)S(1)} %get-tuple-element.29), channel_id=1, source_target_pairs={{0,1},{1,0},{2,3},{3,2},{4,5},{5,4},{6,7},{7,6},{8,9},{9,8},{10,11... | collective-permute-start | bytes 331784 | tf_op jit(solution)/shard_map/ppermute | solution.py:483
  1.6 6.2 %collective-permute-start.1 = (f32[27,8,128]{2,1,0:T(8,128)S(1)}, f32[27,8,128]{2,1,0:T(8,128)S(1)}, u32[]{:S(2)}, u32[]{:S(2)}) collective-permute-start(f32[27,8,128]{2,1,0:T(8,128)S(1)} %get-tuple-element.30), channel_id=1, source_target_pairs={{0,4},{1,2},{2,1},{3,31},{4,0},{5,6},{6,5},{7,27},{8,12},{9,10},{1... | collective-permute-start | bytes 331784 | tf_op jit(solution)/shard_map/ppermute | solution.py:482
  8.5 5.8 %collective-permute-start.2 = (f32[120,128]{1,0:T(8,128)S(1)}, f32[120,128]{1,0:T(8,128)S(1)}, u32[]{:S(2)}, u32[]{:S(2)}) collective-permute-start(f32[120,128]{1,0:T(8,128)S(1)} %get-tuple-element.40), channel_id=1, source_target_pairs={{0,4},{1,5},{2,6},{3,7},{4,0},{5,1},{6,2},{7,3},{8,12},{9,13},{10,... | collective-permute-start | bytes 184328 | tf_op jit(solution)/shard_map/ppermute | solution.py:496
  8.7 5.7 %collective-permute-start.3 = (f32[120,128]{1,0:T(8,128)S(1)}, f32[120,128]{1,0:T(8,128)S(1)}, u32[]{:S(2)}, u32[]{:S(2)}) collective-permute-start(f32[120,128]{1,0:T(8,128)S(1)} %get-tuple-element.41), channel_id=1, source_target_pairs={{0,28},{1,29},{2,30},{3,31},{4,8},{5,9},{6,10},{7,11},{8,4},{9,5},... | collective-permute-start | bytes 184328 | tf_op jit(solution)/shard_map/ppermute | solution.py:495

commit v6 on v5

--- a/solution.py
+++ b/solution.py
@@ -14,7 +14,7 @@
 AT_SPEED, AT_KAPPA = SUB * HALO, SUB * HALO + SUB * FEW
 AT_COUNT = AT_KAPPA + SUB // 2 * FEW
 SPARE = 2
-PAIR = 4
+PAIR = 8
 COLUMNS = -(-(SPARE + AT_COUNT + SUB) // SUB) * SUB
 SMALL = 16 << 20
 VMEM = pl.BlockSpec(memory_space=pltpu.VMEM)
@@ -244,18 +244,13 @@
     return flux(cell, cell - behind, after - cell, beyond - after, coefs)
 
 
-def advance(t, face, low, s, at, beside, fluxes=None):
+def advance(t, face, low, s, at, beside, fluxes, kept=None):
     here = pl.ds(at, SUB)
     cell = [t[s, j, here, :] for j in range(SUB)]
-    if fluxes is None:
-        divergence = [
-            east_flux(t, face, s, j, at) - east_flux(t, face, s, j, at - 1) for j in range(SUB)
-        ]
-    else:
-        east = [east_flux(t, face, s, j, at) for j in range(SUB)]
-        for j in range(SUB):
-            fluxes[j, here, :] = east[j]
-        divergence = [east[j] - fluxes[j, pl.ds(at - 1, SUB), :] for j in range(SUB)]
+    east = [east_flux(t, face, s, j, at) for j in range(SUB)]
+    for j in range(SUB):
+        fluxes[j, here, :] = east[j]
+    divergence = [east[j] - fluxes[j, pl.ds(at - 1, SUB), :] for j in range(SUB)]
     rows = [beside[0], beside[1], *cell, beside[2], beside[3]]
     slope = [b - a for a, b in zip(rows, rows[1:])]
     north = []
@@ -263,7 +258,8 @@
         coefs = tuple(low[c, here, :] if j < 0 else face[3 + c, j, here, :] for c in range(3))
         north.append(flux(rows[j + 2], slope[j + 1], slope[j + 2], slope[j + 3], coefs))
     for j in range(SUB):
-        t[s + 1, j, here, :] = cell[j] - divergence[j] - (north[j + 1] - north[j])
+        value = cell[j] - divergence[j] - (north[j + 1] - north[j])
+        t[s + 1, j, here, :] = value if kept is None else jnp.where(kept, t[s + 1, j, here, :], value)
 
 
 def rows_beside(t, s, at):
@@ -355,7 +351,7 @@
     loop(STEPS * passes, step)
 
 
-def frame_kernel(t_in, face_in, se_in, sn_in, kw_in, low_in, r0, r1, out, t, face, se, sn, kw, low, tall, done):
+def frame_kernel(t_in, face_in, se_in, sn_in, kw_in, low_in, r0, r1, out, t, face, se, sn, kw, low, tall, fluxes, done):
     cols = t.shape[3]
     planes, rows = out.shape[:2]
     height = tall.shape[0] // planes
@@ -402,11 +398,11 @@
         )
 
     def step(s):
-        west = SUB - 2 * (STEPS - 1) + 2 * s
+        west = SUB - 2 * (STEPS - 1) + 2 * s - 1
         east = end - SUB + 2 * (STEPS - 1) - 2 * s
         beside = [rows_beside(t, s, at) for at in (west, east)]
-        for at, rows_turned in zip((west, east), beside):
-            advance(t, face, low, s, at, rows_turned)
+        advance(t, face, low, s, west, beside[0], fluxes)
+        advance(t, face, low, s, east, beside[1], fluxes, sub == 0)
 
     for s in range(STEPS):
         step(s)
@@ -502,7 +498,7 @@
         frame_kernel, [(planes, rows, cols), t.shape, face.shape, wide, wide, wide, low.shape],
         t, face, se, sn, kw, low, r0, r1,
         outs=[ANY] + [VMEM] * 6, alias={i: i + 1 for i in range(6)},
-        scratch=[(planes * tall, cols), pltpu.SemaphoreType.DMA],
+        scratch=[(planes * tall, cols), wide, pltpu.SemaphoreType.DMA],
     )
     return out.reshape(tracers.shape)
 

time: 16 us -> 16 us (level)
  no operation moved by 1% of the time
where the time goes in v6:
time: 16 us; the launch traced here: 15.8 us
  Pallas kernels  7.95 us (50%)
  starting transfers between devices  4.58 us (29%)
  waiting for transfers between devices  3.23 us (20%)
    pallas_call x5, Pallas kernels, call(): pl.pallas_call(kernel, out_shape=[jax.ShapeDtypeStruct(s, jnp.float32) fo...  7.95 us
    ppermute x1, starting transfers between devices, per_device(): r1 = lax.ppermute(p1, AXES, lon_swap(sizes, 1))  2.28 us
    ppermute x1, waiting for transfers between devices, per_device(): y = lax.ppermute(y, AXES, lat_swap(sizes, 1))  1.8 us
    ppermute x1, starting transfers between devices, per_device(): y = lax.ppermute(y, AXES, lat_swap(sizes, 1))  1.61 us
    ppermute x1, waiting for transfers between devices, per_device(): x = lax.ppermute(x, AXES, lat_swap(sizes, 0))  1.42 us
    ppermute x1, starting transfers between devices, per_device(): x = lax.ppermute(x, AXES, lat_swap(sizes, 0))  0.51 us
  transfers between devices with their start and end apart: 4, of which 2 were waited for; matrix products, arithmetic and copies ran while one was open for 0% of the time, Pallas kernels for 30%

profile of v6, /device:TPU:24, one launch (start us, length us, event | category | flops | bytes accessed | tf_op | source)
XLA Modules:
  0.0 15.8 jit_solution(3583454219262661385)
XLA Ops:
  0.0 1.1 %shard_map.56 = (f32[27,8,128]{2,1,0:T(8,128)S(1)}, f32[27,8,128]{2,1,0:T(8,128)S(1)}) custom-call(f32[16,48,128]{2,1,0:T(8,128)} %bitcast.2, f32[8,48,128]{2,1,0:T(8,128)} %ec.3, f32[8,48,128]{2,1,0:T(8,128)} %nc.3, f32[8,48,128]{2,1,0:T(8,128)} %kd.3, s32[48,128]{1,0:T(8,128)} %wet.3), custom_call_target="tpu_custom_call" | custom-call | flops 1048576 | bytes 1048576 | tf_op jit(solution)/shard_map/pallas_call | solution.py:427
  1.1 0.5 %collective-permute-start = (f32[27,8,128]{2,1,0:T(8,128)S(1)}, f32[27,8,128]{2,1,0:T(8,128)S(1)}, u32[]{:S(2)}, u32[]{:S(2)}) collective-permute-start(f32[27,8,128]{2,1,0:T(8,128)S(1)} %get-tuple-element.29), channel_id=1, source_target_pairs={{0,1},{1,0},{2,3},{3,2},{4,5},{5,4},{6,7},{7,6},{8,9},{9,8},{10,11... | collective-permute-start | bytes 331784 | tf_op jit(solution)/shard_map/ppermute | solution.py:479
  1.6 1.6 %collective-permute-start.1 = (f32[27,8,128]{2,1,0:T(8,128)S(1)}, f32[27,8,128]{2,1,0:T(8,128)S(1)}, u32[]{:S(2)}, u32[]{:S(2)}) collective-permute-start(f32[27,8,128]{2,1,0:T(8,128)S(1)} %get-tuple-element.30), channel_id=1, source_target_pairs={{0,4},{1,2},{2,1},{3,31},{4,0},{5,6},{6,5},{7,27},{8,12},{9,10},{1... | collective-permute-start | bytes 331784 | tf_op jit(solution)/shard_map/ppermute | solution.py:478
  3.2 1.3 %shard_map.55 = (f32[16,64,128]{2,1,0:T(8,128)S(1)}, f32[8,64,128]{2,1,0:T(8,128)S(1)}, f32[8,64,128]{2,1,0:T(8,128)S(1)}, f32[8,64,128]{2,1,0:T(8,128)S(1)}, f32[64,128]{1,0:T(8,128)S(1)}) custom-call(f32[16,48,128]{2,1,0:T(8,128)} %bitcast.3, f32[8,48,128]{2,1,0:T(8,128)} %ec.3, f32[8,48,128]{2,1,0:T(8,128)} %nc.3, f32[8,48,128]{2,1,0:T(8,128)} %kd.3, ...), custom_call_target="tpu_custom_call" | custom-call | flops 1048576 | bytes 1048576 | tf_op jit(solution)/shard_map/pallas_call | solution.py:427
  4.6 1.4 %collective-permute-done.x = f32[27,8,128]{2,1,0:T(8,128)S(1)} collective-permute-done((f32[27,8,128]{2,1,0:T(8,128)S(1)}, f32[27,8,128]{2,1,0:T(8,128)S(1)}, u32[]{:S(2)}, u32[]{:S(2)}) %collective-permute-start) | collective-permute-done | bytes 110624 | tf_op jit(solution)/shard_map/ppermute | solution.py:479
  6.0 1.8 %collective-permute-done.1.y = f32[27,8,128]{2,1,0:T(8,128)S(1)} collective-permute-done((f32[27,8,128]{2,1,0:T(8,128)S(1)}, f32[27,8,128]{2,1,0:T(8,128)S(1)}, u32[]{:S(2)}, u32[]{:S(2)}) %collective-permute-start.1) | collective-permute-done | bytes 110624 | tf_op jit(solution)/shard_map/ppermute | solution.py:478
  7.8 0.7 %shard_map.57 = (f32[16,64,128]{2,1,0:T(8,128)S(1)}, f32[8,64,128]{2,1,0:T(8,128)S(1)}, f32[8,64,128]{2,1,0:T(8,128)S(1)}, f32[8,64,128]{2,1,0:T(8,128)S(1)}, f3...) custom-call(f32[16,64,128]{2,1,0:T(8,128)S(1)} %get-tuple-element.24, ...), custom_call_target="tpu_custom_call", output_to_operand_aliasing={{0}: (0, {}), {1}: (1, {}), {2}: (2, {}), {3}: (3, {}), {4}... | custom-call | flops 1048576 | bytes 1048576 | tf_op jit(solution)/shard_map/pallas_call | solution.py:427
  8.5 0.2 %collective-permute-start.2 = (f32[120,128]{1,0:T(8,128)S(1)}, f32[120,128]{1,0:T(8,128)S(1)}, u32[]{:S(2)}, u32[]{:S(2)}) collective-permute-start(f32[120,128]{1,0:T(8,128)S(1)} %get-tuple-element.40), channel_id=1, source_target_pairs={{0,4},{1,5},{2,6},{3,7},{4,0},{5,1},{6,2},{7,3},{8,12},{9,13},{10,... | collective-permute-start | bytes 184328 | tf_op jit(solution)/shard_map/ppermute | solution.py:492
  8.7 2.3 %collective-permute-start.3 = (f32[120,128]{1,0:T(8,128)S(1)}, f32[120,128]{1,0:T(8,128)S(1)}, u32[]{:S(2)}, u32[]{:S(2)}) collective-permute-start(f32[120,128]{1,0:T(8,128)S(1)} %get-tuple-element.41), channel_id=1, source_target_pairs={{0,28},{1,29},{2,30},{3,31},{4,8},{5,9},{6,10},{7,11},{8,4},{9,5},... | collective-permute-start | bytes 184328 | tf_op jit(solution)/shard_map/ppermute | solution.py:491
  11.0 3.4 %shard_map.58 = (f32[4,8,144,128]{3,2,1,0:T(8,128)S(1)}, f32[6,8,144,128]{3,2,1,0:T(8,128)S(1)}, f32[3,144,128]{2,1,0:T(8,128)S(1)}, f32[8,144,128]{2,1,0:T(8,12...) custom-call(f32[8,144,128]{2,1,0:T(8,128)S(1)} %get-tuple-element.31.t0, ...), custom_call_target="tpu_custom_call" | custom-call | flops 1048576 | bytes 1048576 | tf_op jit(solution)/shard_map/pallas_call | solution.py:427
  14.4 0.0 collective-permute-done.2.r0
  14.4 0.0 collective-permute-done.3.r1
  14.4 1.4 %shard_map.59 = (f32[16,48,128]{2,1,0:T(8,128)}, f32[4,8,144,128]{3,2,1,0:T(8,128)S(1)}, f32[6,8,144,128]{3,2,1,0:T(8,128)S(1)}, f32[8,144,128]{2,1,0:T(8,128)S(...) custom-call(f32[4,8,144,128]{3,2,1,0:T(8,128)S(1)} %get-tuple-elemen, ...), custom_call_target="tpu_custom_call", output_to_operand_aliasing={{1}: (0, {}), {2}: (1, {}), {3}: (2, {}), {4}: (3, {}), {5}... | custom-call | flops 1048576 | bytes 1048576 | tf_op jit(solution)/shard_map/pallas_call | solution.py:427
Async XLA Ops:
  1.1 4.9 %collective-permute-start = (f32[27,8,128]{2,1,0:T(8,128)S(1)}, f32[27,8,128]{2,1,0:T(8,128)S(1)}, u32[]{:S(2)}, u32[]{:S(2)}) collective-permute-start(f32[27,8,128]{2,1,0:T(8,128)S(1)} %get-tuple-element.29), channel_id=1, source_target_pairs={{0,1},{1,0},{2,3},{3,2},{4,5},{5,4},{6,7},{7,6},{8,9},{9,8},{10,11... | collective-permute-start | bytes 331784 | tf_op jit(solution)/shard_map/ppermute | solution.py:479
  1.6 6.2 %collective-permute-start.1 = (f32[27,8,128]{2,1,0:T(8,128)S(1)}, f32[27,8,128]{2,1,0:T(8,128)S(1)}, u32[]{:S(2)}, u32[]{:S(2)}) collective-permute-start(f32[27,8,128]{2,1,0:T(8,128)S(1)} %get-tuple-element.30), channel_id=1, source_target_pairs={{0,4},{1,2},{2,1},{3,31},{4,0},{5,6},{6,5},{7,27},{8,12},{9,10},{1... | collective-permute-start | bytes 331784 | tf_op jit(solution)/shard_map/ppermute | solution.py:478
  8.5 5.8 %collective-permute-start.2 = (f32[120,128]{1,0:T(8,128)S(1)}, f32[120,128]{1,0:T(8,128)S(1)}, u32[]{:S(2)}, u32[]{:S(2)}) collective-permute-start(f32[120,128]{1,0:T(8,128)S(1)} %get-tuple-element.40), channel_id=1, source_target_pairs={{0,4},{1,5},{2,6},{3,7},{4,0},{5,1},{6,2},{7,3},{8,12},{9,13},{10,... | collective-permute-start | bytes 184328 | tf_op jit(solution)/shard_map/ppermute | solution.py:492
  8.7 5.7 %collective-permute-start.3 = (f32[120,128]{1,0:T(8,128)S(1)}, f32[120,128]{1,0:T(8,128)S(1)}, u32[]{:S(2)}, u32[]{:S(2)}) collective-permute-start(f32[120,128]{1,0:T(8,128)S(1)} %get-tuple-element.41), channel_id=1, source_target_pairs={{0,28},{1,29},{2,30},{3,31},{4,8},{5,9},{6,10},{7,11},{8,4},{9,5},... | collective-permute-start | bytes 184328 | tf_op jit(solution)/shard_map/ppermute | solution.py:491

commit v7 on v6

--- a/solution.py
+++ b/solution.py
@@ -319,23 +319,25 @@
             for i, value in enumerate(group):
                 beside[k, i] = value
 
-    def prepare(n):
+    def prepare(n, more=True):
         b = jnp.maximum(n - 1, 0)
         turned = [[beside[k, i] for i in range(3)] for k in range(PAIR)]
-        following = jnp.minimum(n, passes - 1)
-        later = turn_coefficients(following)
-        values = spread(following)
+        if more:
+            later = turn_coefficients(n)
+            values = spread(n)
         for k in range(PAIR):
-            if k == PAIR - 1:
+            if more and k == PAIR - 1:
                 put_spread(values)
             at = start(b * PAIR + k)
             for j in range(SUB):
                 t[0, j, pl.ds(at, SUB), :] = t0[j, pl.ds(at, SUB), :]
             all_coefficients(se, sn, kw, face, low, at, *turned[k])
-        keep(later)
+        if more:
+            keep(later)
 
     wrapped = [halves(sp[j, 0:SUB, :])[0] for j in range(SUB)]
-    loop(passes + 1, prepare)
+    loop(passes, prepare)
+    prepare(passes, False)
     for j in range(SUB):
         se[j, 0:SUB, :] = wrapped[j]
     keep(turn_cells(0))

time: 16 us -> 15.8 us (0.988)
  Pallas kernels: 7.95 us -> 7.78 us
    pallas_call x5, Pallas kernels: 7.95 us -> 7.78 us  [call(): pl.pallas_call(kernel, out_shape=[jax.ShapeDtypeStruct(s, jnp.float32) fo...]
  transfers between devices with their start and end apart: 4 -> 4, of which waited for: 2 -> 2; matrix products, arithmetic and copies ran while one was open for 0% -> 0% of each run, Pallas kernels for 30% -> 29%
where the time goes in v7:
time: 15.8 us; the launch traced here: 15.6 us
  Pallas kernels  7.78 us (49%)
  starting transfers between devices  4.58 us (29%)
  waiting for transfers between devices  3.23 us (20%)
    pallas_call x5, Pallas kernels, call(): pl.pallas_call(kernel, out_shape=[jax.ShapeDtypeStruct(s, jnp.float32) fo...  7.78 us
    ppermute x1, starting transfers between devices, per_device(): r1 = lax.ppermute(p1, AXES, lon_swap(sizes, 1))  2.28 us
    ppermute x1, waiting for transfers between devices, per_device(): y = lax.ppermute(y, AXES, lat_swap(sizes, 1))  1.8 us
    ppermute x1, starting transfers between devices, per_device(): y = lax.ppermute(y, AXES, lat_swap(sizes, 1))  1.61 us
    ppermute x1, waiting for transfers between devices, per_device(): x = lax.ppermute(x, AXES, lat_swap(sizes, 0))  1.42 us
    ppermute x1, starting transfers between devices, per_device(): x = lax.ppermute(x, AXES, lat_swap(sizes, 0))  0.51 us
  transfers between devices with their start and end apart: 4, of which 2 were waited for; matrix products, arithmetic and copies ran while one was open for 0% of the time, Pallas kernels for 29%

profile of v7, /device:TPU:24, one launch (start us, length us, event | category | flops | bytes accessed | tf_op | source)
XLA Modules:
  0.0 15.6 jit_solution(3566124215973367759)
XLA Ops:
  0.0 1.1 %shard_map.56 = (f32[27,8,128]{2,1,0:T(8,128)S(1)}, f32[27,8,128]{2,1,0:T(8,128)S(1)}) custom-call(f32[16,48,128]{2,1,0:T(8,128)} %bitcast.2, f32[8,48,128]{2,1,0:T(8,128)} %ec.3, f32[8,48,128]{2,1,0:T(8,128)} %nc.3, f32[8,48,128]{2,1,0:T(8,128)} %kd.3, s32[48,128]{1,0:T(8,128)} %wet.3), custom_call_target="tpu_custom_call" | custom-call | flops 1048576 | bytes 1048576 | tf_op jit(solution)/shard_map/pallas_call | solution.py:429
  1.1 0.5 %collective-permute-start = (f32[27,8,128]{2,1,0:T(8,128)S(1)}, f32[27,8,128]{2,1,0:T(8,128)S(1)}, u32[]{:S(2)}, u32[]{:S(2)}) collective-permute-start(f32[27,8,128]{2,1,0:T(8,128)S(1)} %get-tuple-element.29), channel_id=1, source_target_pairs={{0,1},{1,0},{2,3},{3,2},{4,5},{5,4},{6,7},{7,6},{8,9},{9,8},{10,11... | collective-permute-start | bytes 331784 | tf_op jit(solution)/shard_map/ppermute | solution.py:481
  1.6 1.6 %collective-permute-start.1 = (f32[27,8,128]{2,1,0:T(8,128)S(1)}, f32[27,8,128]{2,1,0:T(8,128)S(1)}, u32[]{:S(2)}, u32[]{:S(2)}) collective-permute-start(f32[27,8,128]{2,1,0:T(8,128)S(1)} %get-tuple-element.30), channel_id=1, source_target_pairs={{0,4},{1,2},{2,1},{3,31},{4,0},{5,6},{6,5},{7,27},{8,12},{9,10},{1... | collective-permute-start | bytes 331784 | tf_op jit(solution)/shard_map/ppermute | solution.py:480
  3.2 1.3 %shard_map.55 = (f32[16,64,128]{2,1,0:T(8,128)S(1)}, f32[8,64,128]{2,1,0:T(8,128)S(1)}, f32[8,64,128]{2,1,0:T(8,128)S(1)}, f32[8,64,128]{2,1,0:T(8,128)S(1)}, f32[64,128]{1,0:T(8,128)S(1)}) custom-call(f32[16,48,128]{2,1,0:T(8,128)} %bitcast.3, f32[8,48,128]{2,1,0:T(8,128)} %ec.3, f32[8,48,128]{2,1,0:T(8,128)} %nc.3, f32[8,48,128]{2,1,0:T(8,128)} %kd.3, ...), custom_call_target="tpu_custom_call" | custom-call | flops 1048576 | bytes 1048576 | tf_op jit(solution)/shard_map/pallas_call | solution.py:429
  4.6 1.4 %collective-permute-done.x = f32[27,8,128]{2,1,0:T(8,128)S(1)} collective-permute-done((f32[27,8,128]{2,1,0:T(8,128)S(1)}, f32[27,8,128]{2,1,0:T(8,128)S(1)}, u32[]{:S(2)}, u32[]{:S(2)}) %collective-permute-start) | collective-permute-done | bytes 110624 | tf_op jit(solution)/shard_map/ppermute | solution.py:481
  6.0 1.8 %collective-permute-done.1.y = f32[27,8,128]{2,1,0:T(8,128)S(1)} collective-permute-done((f32[27,8,128]{2,1,0:T(8,128)S(1)}, f32[27,8,128]{2,1,0:T(8,128)S(1)}, u32[]{:S(2)}, u32[]{:S(2)}) %collective-permute-start.1) | collective-permute-done | bytes 110624 | tf_op jit(solution)/shard_map/ppermute | solution.py:480
  7.8 0.7 %shard_map.57 = (f32[16,64,128]{2,1,0:T(8,128)S(1)}, f32[8,64,128]{2,1,0:T(8,128)S(1)}, f32[8,64,128]{2,1,0:T(8,128)S(1)}, f32[8,64,128]{2,1,0:T(8,128)S(1)}, f3...) custom-call(f32[16,64,128]{2,1,0:T(8,128)S(1)} %get-tuple-element.24, ...), custom_call_target="tpu_custom_call", output_to_operand_aliasing={{0}: (0, {}), {1}: (1, {}), {2}: (2, {}), {3}: (3, {}), {4}... | custom-call | flops 1048576 | bytes 1048576 | tf_op jit(solution)/shard_map/pallas_call | solution.py:429
  8.5 0.2 %collective-permute-start.2 = (f32[120,128]{1,0:T(8,128)S(1)}, f32[120,128]{1,0:T(8,128)S(1)}, u32[]{:S(2)}, u32[]{:S(2)}) collective-permute-start(f32[120,128]{1,0:T(8,128)S(1)} %get-tuple-element.40), channel_id=1, source_target_pairs={{0,4},{1,5},{2,6},{3,7},{4,0},{5,1},{6,2},{7,3},{8,12},{9,13},{10,... | collective-permute-start | bytes 184328 | tf_op jit(solution)/shard_map/ppermute | solution.py:494
  8.7 2.3 %collective-permute-start.3 = (f32[120,128]{1,0:T(8,128)S(1)}, f32[120,128]{1,0:T(8,128)S(1)}, u32[]{:S(2)}, u32[]{:S(2)}) collective-permute-start(f32[120,128]{1,0:T(8,128)S(1)} %get-tuple-element.41), channel_id=1, source_target_pairs={{0,28},{1,29},{2,30},{3,31},{4,8},{5,9},{6,10},{7,11},{8,4},{9,5},... | collective-permute-start | bytes 184328 | tf_op jit(solution)/shard_map/ppermute | solution.py:493
  11.0 3.2 %shard_map.58 = (f32[4,8,144,128]{3,2,1,0:T(8,128)S(1)}, f32[6,8,144,128]{3,2,1,0:T(8,128)S(1)}, f32[3,144,128]{2,1,0:T(8,128)S(1)}, f32[8,144,128]{2,1,0:T(8,12...) custom-call(f32[8,144,128]{2,1,0:T(8,128)S(1)} %get-tuple-element.31.t0, ...), custom_call_target="tpu_custom_call" | custom-call | flops 1048576 | bytes 1048576 | tf_op jit(solution)/shard_map/pallas_call | solution.py:429
  14.2 0.0 collective-permute-done.2.r0
  14.2 0.0 collective-permute-done.3.r1
  14.2 1.4 %shard_map.59 = (f32[16,48,128]{2,1,0:T(8,128)}, f32[4,8,144,128]{3,2,1,0:T(8,128)S(1)}, f32[6,8,144,128]{3,2,1,0:T(8,128)S(1)}, f32[8,144,128]{2,1,0:T(8,128)S(...) custom-call(f32[4,8,144,128]{3,2,1,0:T(8,128)S(1)} %get-tuple-elemen, ...), custom_call_target="tpu_custom_call", output_to_operand_aliasing={{1}: (0, {}), {2}: (1, {}), {3}: (2, {}), {4}: (3, {}), {5}... | custom-call | flops 1048576 | bytes 1048576 | tf_op jit(solution)/shard_map/pallas_call | solution.py:429
Async XLA Ops:
  1.1 4.9 %collective-permute-start = (f32[27,8,128]{2,1,0:T(8,128)S(1)}, f32[27,8,128]{2,1,0:T(8,128)S(1)}, u32[]{:S(2)}, u32[]{:S(2)}) collective-permute-start(f32[27,8,128]{2,1,0:T(8,128)S(1)} %get-tuple-element.29), channel_id=1, source_target_pairs={{0,1},{1,0},{2,3},{3,2},{4,5},{5,4},{6,7},{7,6},{8,9},{9,8},{10,11... | collective-permute-start | bytes 331784 | tf_op jit(solution)/shard_map/ppermute | solution.py:481
  1.6 6.2 %collective-permute-start.1 = (f32[27,8,128]{2,1,0:T(8,128)S(1)}, f32[27,8,128]{2,1,0:T(8,128)S(1)}, u32[]{:S(2)}, u32[]{:S(2)}) collective-permute-start(f32[27,8,128]{2,1,0:T(8,128)S(1)} %get-tuple-element.30), channel_id=1, source_target_pairs={{0,4},{1,2},{2,1},{3,31},{4,0},{5,6},{6,5},{7,27},{8,12},{9,10},{1... | collective-permute-start | bytes 331784 | tf_op jit(solution)/shard_map/ppermute | solution.py:480
  8.5 5.7 %collective-permute-start.2 = (f32[120,128]{1,0:T(8,128)S(1)}, f32[120,128]{1,0:T(8,128)S(1)}, u32[]{:S(2)}, u32[]{:S(2)}) collective-permute-start(f32[120,128]{1,0:T(8,128)S(1)} %get-tuple-element.40), channel_id=1, source_target_pairs={{0,4},{1,5},{2,6},{3,7},{4,0},{5,1},{6,2},{7,3},{8,12},{9,13},{10,... | collective-permute-start | bytes 184328 | tf_op jit(solution)/shard_map/ppermute | solution.py:494
  8.7 5.5 %collective-permute-start.3 = (f32[120,128]{1,0:T(8,128)S(1)}, f32[120,128]{1,0:T(8,128)S(1)}, u32[]{:S(2)}, u32[]{:S(2)}) collective-permute-start(f32[120,128]{1,0:T(8,128)S(1)} %get-tuple-element.41), channel_id=1, source_target_pairs={{0,28},{1,29},{2,30},{3,31},{4,8},{5,9},{6,10},{7,11},{8,4},{9,5},... | collective-permute-start | bytes 184328 | tf_op jit(solution)/shard_map/ppermute | solution.py:493

commit v8 on v7

--- a/solution.py
+++ b/solution.py
@@ -14,6 +14,7 @@
 AT_SPEED, AT_KAPPA = SUB * HALO, SUB * HALO + SUB * FEW
 AT_COUNT = AT_KAPPA + SUB // 2 * FEW
 SPARE = 2
+DRY = -1e9
 PAIR = 8
 COLUMNS = -(-(SPARE + AT_COUNT + SUB) // SUB) * SUB
 SMALL = 16 << 20
@@ -118,7 +119,7 @@
         for b in range(rows // SUB):
             at = pl.ds(SUB + b * SUB, SUB)
             wet_cells = wets[pl.ds(b * SUB, SUB), :] > p
-            ke[p, at, :] = jnp.where(wet_cells, ke[p, at, :], -1.0)
+            ke[p, at, :] = jnp.where(wet_cells, 0.5 * ke[p, at, :], DRY)
 
     loop(lev, dry)
 
@@ -156,7 +157,7 @@
         wets = piece(AT_WET)
         for m in range(N_K):
             counts = jnp.broadcast_to(wets[m : m + 1], shape)
-            kappa = jnp.where(level < counts, piece(AT_K + m), -1.0)
+            kappa = jnp.where(level < counts, 0.5 * piece(AT_K + m), DRY)
             put(ke, at[m], turned(kappa, cells))
         wets = turned(wets, cells)
         for m in range(N_K):
@@ -210,11 +211,11 @@
 
 
 def coefficients(speed, kappa, other_kappa):
-    wet = jnp.minimum(kappa, other_kappa) > 0
-    speed = jnp.where(wet, speed, 0.0)
+    face_kappa = kappa + other_kappa
+    speed = jnp.where(face_kappa > 0, speed, 0.0)
     magnitude = jnp.abs(speed)
-    spread = jnp.minimum(speed, 0.0) - jnp.where(wet, 0.5 * (kappa + other_kappa), 0.0)
-    return speed, spread, 0.5 * magnitude * (1.0 - magnitude)
+    spread = jnp.minimum(speed, 0.0) - jnp.maximum(face_kappa, 0.0)
+    return speed, spread, magnitude * (0.5 - 0.5 * magnitude)
 
 
 def all_coefficients(se, sn, kw, face, low, at, kappa_low, kappa_high, north_low):
@@ -391,7 +392,7 @@
         for j in range(SUB // 2):
             for row, kappa in zip((j, j + SUB // 2), halves(piece(AT_KAPPA + j * FEW, FEW))):
                 wet = level < take(counts, block + row * blocks)
-                kw[row, here, :] = jnp.where(wet, kappa, -1.0)
+                kw[row, here, :] = jnp.where(wet, kappa, DRY)
     for at in (0, end - 1):
         here = pl.ds(at, SUB)
         all_coefficients(

time: 15.8 us -> 15.8 us (level)
  no operation moved by 1% of the time
where the time goes in v8:
time: 15.8 us; the launch traced here: 15.6 us
  Pallas kernels  7.73 us (49%)
  starting transfers between devices  4.58 us (29%)
  waiting for transfers between devices  3.24 us (21%)
    pallas_call x5, Pallas kernels, call(): pl.pallas_call(kernel, out_shape=[jax.ShapeDtypeStruct(s, jnp.float32) fo...  7.73 us
    ppermute x1, starting transfers between devices, per_device(): r1 = lax.ppermute(p1, AXES, lon_swap(sizes, 1))  2.28 us
    ppermute x1, waiting for transfers between devices, per_device(): y = lax.ppermute(y, AXES, lat_swap(sizes, 1))  1.8 us
    ppermute x1, starting transfers between devices, per_device(): y = lax.ppermute(y, AXES, lat_swap(sizes, 1))  1.61 us
    ppermute x1, waiting for transfers between devices, per_device(): x = lax.ppermute(x, AXES, lat_swap(sizes, 0))  1.43 us
    ppermute x1, starting transfers between devices, per_device(): x = lax.ppermute(x, AXES, lat_swap(sizes, 0))  0.51 us
  transfers between devices with their start and end apart: 4, of which 2 were waited for; matrix products, arithmetic and copies ran while one was open for 0% of the time, Pallas kernels for 29%

profile of v8, /device:TPU:24, one launch (start us, length us, event | category | flops | bytes accessed | tf_op | source)
XLA Modules:
  0.0 15.6 jit_solution(3848186564799982243)
XLA Ops:
  0.0 1.1 %shard_map.56 = (f32[27,8,128]{2,1,0:T(8,128)S(1)}, f32[27,8,128]{2,1,0:T(8,128)S(1)}) custom-call(f32[16,48,128]{2,1,0:T(8,128)} %bitcast.2, f32[8,48,128]{2,1,0:T(8,128)} %ec.3, f32[8,48,128]{2,1,0:T(8,128)} %nc.3, f32[8,48,128]{2,1,0:T(8,128)} %kd.3, s32[48,128]{1,0:T(8,128)} %wet.3), custom_call_target="tpu_custom_call" | custom-call | flops 1048576 | bytes 1048576 | tf_op jit(solution)/shard_map/pallas_call | solution.py:430
  1.1 0.5 %collective-permute-start = (f32[27,8,128]{2,1,0:T(8,128)S(1)}, f32[27,8,128]{2,1,0:T(8,128)S(1)}, u32[]{:S(2)}, u32[]{:S(2)}) collective-permute-start(f32[27,8,128]{2,1,0:T(8,128)S(1)} %get-tuple-element.29), channel_id=1, source_target_pairs={{0,1},{1,0},{2,3},{3,2},{4,5},{5,4},{6,7},{7,6},{8,9},{9,8},{10,11... | collective-permute-start | bytes 331784 | tf_op jit(solution)/shard_map/ppermute | solution.py:482
  1.6 1.6 %collective-permute-start.1 = (f32[27,8,128]{2,1,0:T(8,128)S(1)}, f32[27,8,128]{2,1,0:T(8,128)S(1)}, u32[]{:S(2)}, u32[]{:S(2)}) collective-permute-start(f32[27,8,128]{2,1,0:T(8,128)S(1)} %get-tuple-element.30), channel_id=1, source_target_pairs={{0,4},{1,2},{2,1},{3,31},{4,0},{5,6},{6,5},{7,27},{8,12},{9,10},{1... | collective-permute-start | bytes 331784 | tf_op jit(solution)/shard_map/ppermute | solution.py:481
  3.2 1.3 %shard_map.55 = (f32[16,64,128]{2,1,0:T(8,128)S(1)}, f32[8,64,128]{2,1,0:T(8,128)S(1)}, f32[8,64,128]{2,1,0:T(8,128)S(1)}, f32[8,64,128]{2,1,0:T(8,128)S(1)}, f32[64,128]{1,0:T(8,128)S(1)}) custom-call(f32[16,48,128]{2,1,0:T(8,128)} %bitcast.3, f32[8,48,128]{2,1,0:T(8,128)} %ec.3, f32[8,48,128]{2,1,0:T(8,128)} %nc.3, f32[8,48,128]{2,1,0:T(8,128)} %kd.3, ...), custom_call_target="tpu_custom_call" | custom-call | flops 1048576 | bytes 1048576 | tf_op jit(solution)/shard_map/pallas_call | solution.py:430
  4.5 1.4 %collective-permute-done.x = f32[27,8,128]{2,1,0:T(8,128)S(1)} collective-permute-done((f32[27,8,128]{2,1,0:T(8,128)S(1)}, f32[27,8,128]{2,1,0:T(8,128)S(1)}, u32[]{:S(2)}, u32[]{:S(2)}) %collective-permute-start) | collective-permute-done | bytes 110624 | tf_op jit(solution)/shard_map/ppermute | solution.py:482
  6.0 1.8 %collective-permute-done.1.y = f32[27,8,128]{2,1,0:T(8,128)S(1)} collective-permute-done((f32[27,8,128]{2,1,0:T(8,128)S(1)}, f32[27,8,128]{2,1,0:T(8,128)S(1)}, u32[]{:S(2)}, u32[]{:S(2)}) %collective-permute-start.1) | collective-permute-done | bytes 110624 | tf_op jit(solution)/shard_map/ppermute | solution.py:481
  7.8 0.8 %shard_map.57 = (f32[16,64,128]{2,1,0:T(8,128)S(1)}, f32[8,64,128]{2,1,0:T(8,128)S(1)}, f32[8,64,128]{2,1,0:T(8,128)S(1)}, f32[8,64,128]{2,1,0:T(8,128)S(1)}, f3...) custom-call(f32[16,64,128]{2,1,0:T(8,128)S(1)} %get-tuple-element.24, ...), custom_call_target="tpu_custom_call", output_to_operand_aliasing={{0}: (0, {}), {1}: (1, {}), {2}: (2, {}), {3}: (3, {}), {4}... | custom-call | flops 1048576 | bytes 1048576 | tf_op jit(solution)/shard_map/pallas_call | solution.py:430
  8.5 0.2 %collective-permute-start.2 = (f32[120,128]{1,0:T(8,128)S(1)}, f32[120,128]{1,0:T(8,128)S(1)}, u32[]{:S(2)}, u32[]{:S(2)}) collective-permute-start(f32[120,128]{1,0:T(8,128)S(1)} %get-tuple-element.40), channel_id=1, source_target_pairs={{0,4},{1,5},{2,6},{3,7},{4,0},{5,1},{6,2},{7,3},{8,12},{9,13},{10,... | collective-permute-start | bytes 184328 | tf_op jit(solution)/shard_map/ppermute | solution.py:495
  8.7 2.3 %collective-permute-start.3 = (f32[120,128]{1,0:T(8,128)S(1)}, f32[120,128]{1,0:T(8,128)S(1)}, u32[]{:S(2)}, u32[]{:S(2)}) collective-permute-start(f32[120,128]{1,0:T(8,128)S(1)} %get-tuple-element.41), channel_id=1, source_target_pairs={{0,28},{1,29},{2,30},{3,31},{4,8},{5,9},{6,10},{7,11},{8,4},{9,5},... | collective-permute-start | bytes 184328 | tf_op jit(solution)/shard_map/ppermute | solution.py:494
  11.0 3.2 %shard_map.58 = (f32[4,8,144,128]{3,2,1,0:T(8,128)S(1)}, f32[6,8,144,128]{3,2,1,0:T(8,128)S(1)}, f32[3,144,128]{2,1,0:T(8,128)S(1)}, f32[8,144,128]{2,1,0:T(8,12...) custom-call(f32[8,144,128]{2,1,0:T(8,128)S(1)} %get-tuple-element.31.t0, ...), custom_call_target="tpu_custom_call" | custom-call | flops 1048576 | bytes 1048576 | tf_op jit(solution)/shard_map/pallas_call | solution.py:430
  14.1 0.0 collective-permute-done.2.r0
  14.2 0.0 collective-permute-done.3.r1
  14.2 1.4 %shard_map.59 = (f32[16,48,128]{2,1,0:T(8,128)}, f32[4,8,144,128]{3,2,1,0:T(8,128)S(1)}, f32[6,8,144,128]{3,2,1,0:T(8,128)S(1)}, f32[8,144,128]{2,1,0:T(8,128)S(...) custom-call(f32[4,8,144,128]{3,2,1,0:T(8,128)S(1)} %get-tuple-elemen, ...), custom_call_target="tpu_custom_call", output_to_operand_aliasing={{1}: (0, {}), {2}: (1, {}), {3}: (2, {}), {4}: (3, {}), {5}... | custom-call | flops 1048576 | bytes 1048576 | tf_op jit(solution)/shard_map/pallas_call | solution.py:430
Async XLA Ops:
  1.1 4.9 %collective-permute-start = (f32[27,8,128]{2,1,0:T(8,128)S(1)}, f32[27,8,128]{2,1,0:T(8,128)S(1)}, u32[]{:S(2)}, u32[]{:S(2)}) collective-permute-start(f32[27,8,128]{2,1,0:T(8,128)S(1)} %get-tuple-element.29), channel_id=1, source_target_pairs={{0,1},{1,0},{2,3},{3,2},{4,5},{5,4},{6,7},{7,6},{8,9},{9,8},{10,11... | collective-permute-start | bytes 331784 | tf_op jit(solution)/shard_map/ppermute | solution.py:482
  1.6 6.2 %collective-permute-start.1 = (f32[27,8,128]{2,1,0:T(8,128)S(1)}, f32[27,8,128]{2,1,0:T(8,128)S(1)}, u32[]{:S(2)}, u32[]{:S(2)}) collective-permute-start(f32[27,8,128]{2,1,0:T(8,128)S(1)} %get-tuple-element.30), channel_id=1, source_target_pairs={{0,4},{1,2},{2,1},{3,31},{4,0},{5,6},{6,5},{7,27},{8,12},{9,10},{1... | collective-permute-start | bytes 331784 | tf_op jit(solution)/shard_map/ppermute | solution.py:481
  8.5 5.6 %collective-permute-start.2 = (f32[120,128]{1,0:T(8,128)S(1)}, f32[120,128]{1,0:T(8,128)S(1)}, u32[]{:S(2)}, u32[]{:S(2)}) collective-permute-start(f32[120,128]{1,0:T(8,128)S(1)} %get-tuple-element.40), channel_id=1, source_target_pairs={{0,4},{1,5},{2,6},{3,7},{4,0},{5,1},{6,2},{7,3},{8,12},{9,13},{10,... | collective-permute-start | bytes 184328 | tf_op jit(solution)/shard_map/ppermute | solution.py:495
  8.7 5.5 %collective-permute-start.3 = (f32[120,128]{1,0:T(8,128)S(1)}, f32[120,128]{1,0:T(8,128)S(1)}, u32[]{:S(2)}, u32[]{:S(2)}) collective-permute-start(f32[120,128]{1,0:T(8,128)S(1)} %get-tuple-element.41), channel_id=1, source_target_pairs={{0,28},{1,29},{2,30},{3,31},{4,8},{5,9},{6,10},{7,11},{8,4},{9,5},... | collective-permute-start | bytes 184328 | tf_op jit(solution)/shard_map/ppermute | solution.py:494
